TPU v7x, 256 devices: a whole 4x4x8 slice. The times are simulated.
256 devices in a mesh: chan: 32 (over x, y, z_lo), win: 8 (over z_hi, core).
Axes of the slice: x: 4, y: 4, z: 8 (z_hi: 4, z_lo: 2; z = z_hi * 2 + z_lo), core: 2. Of those that a mesh axis runs over, the one named last changes fastest.
Arguments:
- records: float32 [32, 1024, 1024], P('win', 'chan'), may hold values from -180 to 180
- sources: int32 [32], replicated, may hold values from 0 to 1023, as said below
Outputs:
- correlations: float32 [32, 256, 1024], P('win', None, 'chan')
Inputs may be any that keep to these rules, and one draw needn't show every extreme that they name: `sources`: source s is one of the channels s * 32 to (s + 1) * 32 - 1; the first source is channel 0 and the last is channel 1024 - 1.
All inputs are finite; a program needn't handle non-finite values.
Results may differ from a plain program's by a relative error of at most 0.00022.
Values sent between devices are 32-bit elements; how exact they have to be, the bound alone decides.
No kernel may reach another device: no remote copies, remote signals or barrier semaphores. Data moves between devices by JAX's collectives and lax.ppermute only.
A program may use at most 64 MiB of HBM per device.

v0:
```python
import math

import jax
import jax.numpy as jnp
from jax import lax
from jax.sharding import PartitionSpec as P

HIGHEST = lax.Precision.HIGHEST
AMPLITUDE_FLOOR = 0.25
WHITE_EPSILON = 1e-06


def fourier_table(length):
    freq_count = length // 2
    freqs = jnp.arange(freq_count, dtype=jnp.int32)[:, None]
    sample_index = jnp.arange(length, dtype=jnp.int32)[None, :]
    angles = (freqs * sample_index % length).astype(jnp.float32) * (2.0 * math.pi / length)
    return jnp.concatenate([jnp.cos(angles), -jnp.sin(angles)], axis=0)


def band_table(freq_count, reach):
    rows_index = jnp.arange(freq_count, dtype=jnp.int32)[:, None]
    cols_index = jnp.arange(freq_count, dtype=jnp.int32)[None, :]
    return (jnp.abs(rows_index - cols_index) <= reach).astype(jnp.float32)


def inverse_table(length, lag_count, first_bin, bin_count, factor):
    freqs = first_bin + jnp.arange(bin_count, dtype=jnp.int32)
    lag_index = jnp.arange(lag_count, dtype=jnp.int32) - lag_count // 2
    angles = (lag_index[:, None] * freqs[None, :] % length).astype(jnp.float32) * (
        2.0 * math.pi / length
    )
    weights = jnp.where(freqs == 0, 1.0, 2.0).astype(jnp.float32)[None, :] * factor
    return jnp.concatenate([weights * jnp.cos(angles), -weights * jnp.sin(angles)], axis=1)


def running_level(padded, time_count, window_span):
    window_total = padded.shape[0]
    chans = padded.shape[2]
    running = jnp.concatenate(
        [jnp.zeros((window_total, 1, chans), jnp.float32), jnp.cumsum(jnp.abs(padded), axis=1)],
        axis=1,
    )
    return (running[:, window_span:] - running[:, :time_count]) / window_span


def local(records, sources):
    chan_count = lax.axis_size("chan")
    local_windows, local_time, all_channels = records.shape
    length = local_time * chan_count
    freq_count = length // 2
    chan_width = all_channels // chan_count
    half_width = min(16, local_time)
    smooth_reach = length // 32
    window_span = 2 * half_width + 1
    lag_count = length // 4
    forward = fourier_table(length)
    band_matrix = band_table(freq_count, smooth_reach)
    pieces = lax.all_to_all(records, "chan", split_axis=2, concat_axis=1, tiled=True)
    padded = jnp.pad(pieces, ((0, 0), (half_width, half_width), (0, 0)))
    amplitude = running_level(padded, length, window_span)
    whiten_pieces = pieces / jnp.maximum(amplitude, AMPLITUDE_FLOOR)
    spectrum = jnp.einsum("kt,wtc->wkc", forward, whiten_pieces, precision=HIGHEST)
    real_part = spectrum[:, :freq_count]
    imag_part = spectrum[:, freq_count:]
    magnitude = jnp.sqrt(real_part * real_part + imag_part * imag_part)
    smoothed = (
        jnp.einsum("jk,wkc->wjc", band_matrix, magnitude, precision=HIGHEST)
        / (2 * smooth_reach + 1)
        + WHITE_EPSILON
    )
    whitened = jnp.stack([real_part / smoothed, imag_part / smoothed], axis=1)
    band_data = lax.all_to_all(whitened, "win", split_axis=2, concat_axis=0, tiled=True)
    total_windows = band_data.shape[0]
    band_count = band_data.shape[2]
    chan_index = lax.axis_index("chan")
    channel_ids = jnp.arange(chan_width, dtype=jnp.int32)
    selector = (sources[:, None] == chan_index * chan_width + channel_ids[None, :]).astype(
        jnp.float32
    )
    chosen = jnp.einsum("sc,wafc->wafs", selector, band_data, precision=HIGHEST)
    spectra = lax.psum(chosen, "chan")
    source_real = spectra[:, 0]
    source_imag = spectra[:, 1]
    white_real = band_data[:, 0]
    white_imag = band_data[:, 1]
    cross_real = jnp.einsum(
        "wfs,wfc->fsc", source_real, white_real, precision=HIGHEST
    ) + jnp.einsum("wfs,wfc->fsc", source_imag, white_imag, precision=HIGHEST)
    cross_imag = jnp.einsum(
        "wfs,wfc->fsc", source_real, white_imag, precision=HIGHEST
    ) - jnp.einsum("wfs,wfc->fsc", source_imag, white_real, precision=HIGHEST)
    stacked = jnp.stack([cross_real, cross_imag])
    factor = 1.0 / math.sqrt(total_windows * freq_count)
    band_start = lax.axis_index("win") * band_count
    band_table_part = inverse_table(length, lag_count, band_start, band_count, factor).reshape(
        lag_count, 2, band_count
    )
    return lax.psum_scatter(
        jnp.einsum("tak,aksc->stc", band_table_part, stacked, precision=HIGHEST),
        "win",
        scatter_dimension=0,
        tiled=True,
    )


def solution(mesh):
    placed = (P("win", "chan", None), P())
    return jax.shard_map(
        local, mesh=mesh, in_specs=placed, out_specs=P("win", None, "chan"), check_vma=False
    )
```

profile of v0, /device:TPU:1, one launch (start us, length us, event | category | flops | bytes accessed | tf_op | source)
XLA Modules:
  0.0 525.1 jit_solution(4063981459503955568)
XLA Ops:
  6.5 1.8 copy.27
  8.3 2.1 reshape.206
  10.4 9.2 %all-to-all-start = ((f32[32,1,4096]{2,1,0:T(1,128)}), f32[32,1,4096]{2,1,0:T(1,128)S(1)}, u32[]{:S(2)}, u32[]{:S(2)}) async-start(f32[32,1,4096]{2,1,0:T(1,128)} %reshape.206), calls=%async_computation | async-start | bytes 1048576 | tf_op jit(solution)/shard_map/all_to_all | solution.py:59
  19.7 9.1 %sine_negate_fusion = (f32[512,1024]{1,0:T(8,128)S(1)}, f32[512,1024]{1,0:T(8,128)}) fusion(), kind=kLoop, calls=%fused_computation.14 | loop fusion | flops 7864320 | bytes 4194304 | tf_op jit(solution)/shard_map/neg | solution.py:18
  28.7 1.9 all-to-all-done
  31.2 1.9 reduce
  33.1 2.4 reshape.207
  35.5 4.1 copy.49
  39.6 2.4 all_to_all.29
  43.9 62.7 %reduce-window.6 = f32[4,32,9,128]{3,2,1,0:T(8,128)S(1)} reduce-window(f32[4,32,9,128]{3,2,1,0:T(8,128)} %reshape.199, f32[]{:T(128)} %constant.22.clone.1), window={size=1x1x1x128 pad=0_0x0_0x0_0x127_0}, to_apply=%region_0.1 | reduce-window | flops 18726912 | bytes 1179652 | tf_op jit(solution)/shard_map/reduce-window
  108.0 1.5 copy.29
  111.0 1.3 reduce_window_sum.16
  112.3 6.1 %fusion.16 = f32[4,1024,32]{1,2,0:T(8,128)S(1)} fusion(f32[512,1024]{1,0:T(8,128)S(1)} %get-tuple-element.13, f32[512,1024]{1,0:T(8,128)} %get-tuple-element.14, f32[4,1024,32]{1,2,0:T(8,128)} %copy-done.1, f32[4,1056,32]{1,2,0:T(8,128)S(1)} %bitcast.85, f32[4,1152,32]{1,2,0:T(8,128)S(1)} %bitcast.84), kind=kOutput, calls=%fused_computation.23 | convolution fusion | flops 1612185600 | bytes 6356992 | tf_op jit(solution)/shard_map/kt,wtc->wkc/dot_general | solution.py:63
  120.5 2.1 reshape.208
  122.6 9.8 %all-to-all-start.1 = ((f32[8,1,16384]{2,1,0:T(1,128)}), f32[8,1,16384]{2,1,0:T(1,128)S(1)}, u32[]{:S(2)}, u32[]{:S(2)}) async-start(f32[8,1,16384]{2,1,0:T(1,128)} %reshape.208), calls=%async_computation.1 | async-start | bytes 1048576 | tf_op jit(solution)/shard_map/all_to_all | solution.py:73
  132.5 15.6 %all-to-all-done.1 = f32[8,1,16384]{2,1,0:T(1,128)S(1)} async-done(((f32[8,1,16384]{2,1,0:T(1,128)}), f32[8,1,16384]{2,1,0:T(1,128)S(1)}, u32[]{:S(2)}, u32[]{:S(2)}) %all-to-all-start.1) | async-done | bytes 524320 | tf_op jit(solution)/shard_map/all_to_all | solution.py:73
  148.0 1.9 reduce.1
  151.8 1.7 fusion.44
  155.9 286.2 %all-reduce.5.cloned.1.call-done = f32[32,2,64,32]{2,3,1,0:T(8,128)} async-done(((f32[32,2,64,32]{2,3,1,0:T(8,128)}), f32[32,2,64,32]{2,3,1,0:T(8,128)}) %all-reduce.5.cloned.1.call-update) | async-done | bytes 524304 | tf_op jit(solution)/shard_map/psum | solution.py:82
  442.0 2.3 slice_bitcast_fusion.1
  444.3 2.0 copy.33
  446.3 2.8 copy.35
  454.2 5.1 fusion.11
  459.3 58.9 %reduce-scatter.2.cloned.1.call-done = f32[4,256,32]{1,2,0:T(8,128)} async-done(((f32[32,256,32]{1,2,0:T(8,128)}), f32[4,256,32]{1,2,0:T(8,128)}) %reduce-scatter.2.cloned.1.call-update) | async-done | bytes 131088 | tf_op jit(solution)/shard_map/reduce_scatter | solution.py:99
  (37 shorter events, 16.4 us)
Async XLA Ops:
  10.4 20.2 %all-to-all-start = ((f32[32,1,4096]{2,1,0:T(1,128)}), f32[32,1,4096]{2,1,0:T(1,128)S(1)}, u32[]{:S(2)}, u32[]{:S(2)}) async-start(f32[32,1,4096]{2,1,0:T(1,128)} %reshape.206), calls=%async_computation | async-start | bytes 1048576 | tf_op jit(solution)/shard_map/all_to_all | solution.py:59
  42.1 0.8 copy-start.1
  122.6 25.4 %all-to-all-start.1 = ((f32[8,1,16384]{2,1,0:T(1,128)}), f32[8,1,16384]{2,1,0:T(1,128)S(1)}, u32[]{:S(2)}, u32[]{:S(2)}) async-start(f32[8,1,16384]{2,1,0:T(1,128)} %reshape.208), calls=%async_computation.1 | async-start | bytes 1048576 | tf_op jit(solution)/shard_map/all_to_all | solution.py:73
  132.4 309.6 %all-reduce.5.cloned.1.call-start = ((), (), s32[]{:S(2)}) async-start(), calls=%async_computation.3 | async-start | bytes 2097152 | tf_op jit(solution)/shard_map/psum | solution.py:82
  151.0 0.8 copy-start.2
  153.5 364.7 %reduce-scatter.2.cloned.1.call-start = ((), (), s32[]{:S(2)}) async-start(), calls=%async_computation.4 | async-start | bytes 1179648 | tf_op jit(solution)/shard_map/reduce_scatter | solution.py:99
  450.3 1.2 copy-start
Sparse Core Ops, SparseCore 0:
  153.6 288.3 all-reduce.4
  459.4 58.7 reduce-scatter.1
where the time goes:
time: 531 us; the launch traced here: 525 us
  waiting for transfers between devices  363 us (68%)
  other arithmetic  77.8 us (15%)
  local copies, waits for them, and re-layouts  33.7 us (6%)
  starting transfers between devices  19.1 us (4%)
  matrix products  18.3 us (3%)
  between operations  13.6 us (3%)
    psum x1, waiting for transfers between devices, local(): spectra = lax.psum(chosen, 'chan')  286 us
    another operation x3, other arithmetic  64.1 us
    reduce_scatter x1, waiting for transfers between devices, local(): lax.psum_scatter(jnp.einsum('tak,aksc->stc', band_table_part, stacked, pr...  58.9 us
    all_to_all x1, waiting for transfers between devices, local(): lax.all_to_all(whitened, 'win', split_axis=2, concat_axis=0, tiled=True)  15.6 us
  transfers between devices with their start and end apart: 4, of which 4 were waited for; matrix products, arithmetic and copies ran while one was open for 2% of the time, Pallas kernels for 0%

commit v1 on v0

v1 whole, which is shorter than its diff:
```python
import functools
import math

import jax
import jax.numpy as jnp
import ml_dtypes
import numpy as np
from jax import lax
from jax.experimental import pallas as pl
from jax.experimental.pallas import tpu as pltpu
from jax.sharding import PartitionSpec as P

AMPLITUDE_FLOOR = 0.25
WHITE_EPSILON = 1e-06
HALF = 16
LANES = 128
F32 = jnp.float32
BF16 = jnp.bfloat16


def split_table(table):
    high = table.astype(np.float32).astype(ml_dtypes.bfloat16)
    low = (table - high.astype(np.float64)).astype(np.float32).astype(ml_dtypes.bfloat16)
    return high, low


def bin_order(freq_count):
    return np.concatenate([np.arange(0, freq_count, 2), np.arange(1, freq_count, 2)])


def forward_tables(length):
    freq_count = length // 2
    times = np.arange(length // 2)[:, None]
    parts = []
    for parity in range(2):
        bins = np.arange(parity, freq_count, 2)[None, :]
        angles = (bins * times % length) * (2.0 * math.pi / length)
        parts.append(np.concatenate([np.cos(angles), -np.sin(angles)], axis=1))
    return split_table(np.stack(parts))


def band_table(freq_count, reach):
    bins = bin_order(freq_count)
    return (np.abs(bins[:, None] - bins[None, :]) <= reach).astype(ml_dtypes.bfloat16)


def inverse_tables(length, lag_count, factor):
    freq_count = length // 2
    bins = bin_order(freq_count)
    lags = np.arange(lag_count) - lag_count // 2
    angles = (bins[:, None] * lags[None, :] % length) * (2.0 * math.pi / length)
    weights = np.where(bins == 0, 1.0, 2.0)[:, None] * factor
    return split_table(np.concatenate([weights * np.cos(angles), -weights * np.sin(angles)], axis=0))


def split(value):
    high = value.astype(BF16)
    return high, (value - high.astype(F32)).astype(BF16)


def mm(left, right):
    return jnp.dot(left, right, preferred_element_type=F32)


def pack_kernel(sources, records, packed):
    windows, times, channels = records.shape
    dests = packed.shape[0]
    width = channels // dests
    per_tile = LANES // width
    lane = lax.broadcasted_iota(jnp.int32, (times, LANES), 1)
    for tile in range(channels // LANES):
        loaded = [records[w, :, tile * LANES : (tile + 1) * LANES] for w in range(windows)]
        for e in range(per_tile):
            block = None
            for w in range(windows):
                shift = (w - e) * width % LANES
                moved = pltpu.roll(loaded[w], shift, 1) if shift else loaded[w]
                block = moved if block is None else jnp.where(lane >= w * width, moved, block)
            packed[tile * per_tile + e, 0:times, :] = block
    chosen = jnp.zeros((times, LANES), F32)
    for s in range(dests):
        tile = s * width // LANES
        place = sources[s] - tile * LANES
        for w in range(windows):
            target = w * dests + s
            shift = lax.rem(target + LANES - place, LANES)
            moved = pltpu.roll(records[w, :, tile * LANES : (tile + 1) * LANES], shift, 1)
            chosen = jnp.where(lane == target, moved, chosen)
    for d in range(dests):
        packed[d, times : 2 * times, :] = chosen


def main_kernel(
    place, blocks, fwd_high, fwd_low, band, inv_high, inv_low, send, keep,
    turned, white_re, white_im, cross_high, cross_low,
):
    devices, double, lanes = blocks.shape
    times = double // 2
    length = devices * times
    half = length // 2
    quarter = half // 2
    rows = 2 * lanes
    width = 32
    windows = lanes // width
    for part in range(2):
        data = blocks[:, part * times : (part + 1) * times, :].reshape(length, lanes)
        level = jnp.abs(data)
        edge = jnp.zeros((HALF, lanes), F32)
        tail = jnp.concatenate([level, edge], axis=0)
        total = jnp.concatenate([edge, level, edge], axis=0)
        size = length + 2 * HALF
        for step in (1, 2, 4, 8, 16):
            total = total + pltpu.roll(total, size - step, 0)
        amplitude = (total[:length] + tail[HALF:]) / (2 * HALF + 1)
        normal = data / jnp.maximum(amplitude, AMPLITUDE_FLOOR)
        turned[part * lanes : (part + 1) * lanes, :] = normal.T
    first = turned[:, :half]
    second = turned[:, half:]
    for parity in range(2):
        folded = first + second if parity == 0 else first - second
        high, low = split(folded)
        spectrum = (
            mm(high, fwd_high[parity]) + mm(low, fwd_high[parity]) + mm(high, fwd_low[parity])
        )
        white_re[:, parity * quarter : (parity + 1) * quarter] = spectrum[:, :quarter]
        white_im[:, parity * quarter : (parity + 1) * quarter] = spectrum[:, quarter:]
    re = white_re[...]
    im = white_im[...]
    high, low = split(jnp.sqrt(re * re + im * im))
    smooth = (mm(high, band[...]) + mm(low, band[...])) / (2 * (length // 32) + 1) + WHITE_EPSILON
    gain = 1.0 / smooth
    white_re[...] = re * gain
    white_im[...] = im * gain

    z_hi = place[0]
    core = place[1]
    for slot in range(4):
        target = lax.rem(z_hi + slot, 4)
        for which in range(2):
            turn = 4 * core if which else 4 - 4 * core
            turn = lax.rem(8 - turn, 8)
            for tile in range(half // LANES):
                span = slice(tile * LANES, (tile + 1) * LANES)
                chan_re = [white_re[w * width : (w + 1) * width, span] for w in range(windows)]
                chan_im = [white_im[w * width : (w + 1) * width, span] for w in range(windows)]
                rows8 = [
                    pl.ds(pl.multiple_of(lanes + w * width + target * 8, 8), 8)
                    for w in range(windows)
                ]
                from_re = [pltpu.roll(white_re[at, span], turn, 0) for at in rows8]
                from_im = [pltpu.roll(white_im[at, span], turn, 0) for at in rows8]
                for i in range(4):
                    out_re = None
                    for w in range(windows):
                        src_re = jnp.broadcast_to(from_re[w][i : i + 1], (width, LANES))
                        src_im = jnp.broadcast_to(from_im[w][i : i + 1], (width, LANES))
                        add_re = src_re * chan_re[w] + src_im * chan_im[w]
                        add_im = src_re * chan_im[w] - src_im * chan_re[w]
                        out_re = add_re if out_re is None else out_re + add_re
                        out_im = add_im if w == 0 else out_im + add_im
                    at = slice(i * width, (i + 1) * width)
                    cross_high[at, span], cross_low[at, span] = split(out_re)
                    span2 = slice(half + tile * LANES, half + (tile + 1) * LANES)
                    cross_high[at, span2], cross_low[at, span2] = split(out_im)
            result = (
                mm(cross_high[...], inv_high[...])
                + mm(cross_low[...], inv_high[...])
                + mm(cross_high[...], inv_low[...])
            )
            (keep if which else send)[slot] = result


def local(records, sources):
    chan_count = lax.axis_size("chan")
    windows, times, channels = records.shape
    length = times * chan_count
    lag_count = length // 4
    half = length // 2
    total_windows = windows * lax.axis_size("win")
    factor = 1.0 / math.sqrt(total_windows * half)
    vmem = pl.BlockSpec(memory_space=pltpu.VMEM)
    smem = pl.BlockSpec(memory_space=pltpu.SMEM)

    packed = pl.pallas_call(
        pack_kernel,
        out_shape=jax.ShapeDtypeStruct((chan_count, 2 * times, LANES), F32),
        in_specs=[smem, vmem],
        out_specs=vmem,
        name="pack",
    )(sources, records)
    blocks = lax.all_to_all(packed, "chan", 0, 0, tiled=True)

    fwd_high, fwd_low = (jnp.asarray(t) for t in forward_tables(length))
    inv_high, inv_low = (jnp.asarray(t) for t in inverse_tables(length, lag_count, factor))
    band = jnp.asarray(band_table(half, length // 32))
    win = lax.axis_index("win")
    place = jnp.stack([win // 2, win % 2]).astype(jnp.int32)
    part = jax.ShapeDtypeStruct((4, LANES, lag_count), F32)
    send, keep = pl.pallas_call(
        main_kernel,
        out_shape=(part, part),
        in_specs=[smem] + [vmem] * 6,
        out_specs=(vmem, vmem),
        scratch_shapes=[
            pltpu.VMEM((2 * LANES, length), F32),
            pltpu.VMEM((2 * LANES, half), F32),
            pltpu.VMEM((2 * LANES, half), F32),
            pltpu.VMEM((LANES, length), BF16),
            pltpu.VMEM((LANES, length), BF16),
        ],
        compiler_params=pltpu.CompilerParams(vmem_limit_bytes=48 << 20),
        name="stack",
    )(place, blocks, fwd_high, fwd_low, band, inv_high, inv_low)

    def shifted(value, shift):
        return lax.ppermute(value, "win", [(i, (i + shift) % 8) for i in range(8)])

    other = lax.ppermute(send, "win", [(i, i ^ 1) for i in range(8)])
    mid = LANES // 2
    pair = keep + other
    from_left = shifted(pair[2, :mid], 2)
    from_right = shifted(pair[2, mid:], -2)
    right = jnp.concatenate([pair[1, :mid] + from_left, pair[1, mid:]], axis=0)
    left = jnp.concatenate([pair[3, :mid], pair[3, mid:] + from_right], axis=0)
    result = pair[0] + shifted(right, 2) + shifted(left, -2)
    return jnp.transpose(result.reshape(4, 32, lag_count), (0, 2, 1))


def solution(mesh):
    placed = (P("win", "chan", None), P())
    return jax.shard_map(
        local, mesh=mesh, in_specs=placed, out_specs=P("win", None, "chan"), check_vma=False
    )
```

time: 531 us -> 64.1 us (0.12)
  waiting for transfers between devices: 363 us -> 28.3 us
  other arithmetic: 77.8 us -> 0.86 us
  local copies, waits for them, and re-layouts: 33.7 us -> 3.15 us
  matrix products: 18.3 us -> 0 us
  between operations: 13.6 us -> 0.07 us
  Pallas kernels: 0 us -> 10.4 us
    psum x1 -> x0, waiting for transfers between devices: 286 us -> none  [local(): spectra = lax.psum(chosen, 'chan')]
    another operation x5 -> x1, other arithmetic: 64.4 us -> 0.08 us  [local(): place = jnp.stack([win // 2, win % 2]).astype(jnp.int32)]
    reduce_scatter x1 -> x0, waiting for transfers between devices: 58.9 us -> none  [local(): lax.psum_scatter(jnp.einsum('tak,aksc->stc', band_table_part, stacked, pr...]
    dot_general x8 -> x0, matrix products: 18.3 us -> none  [the longest x1 6.13 us: local(): jnp.einsum('kt,wtc->wkc', forward, whiten_pieces, precision=HIGHEST)]
    ppermute x0 -> x5, waiting for transfers between devices: none -> 11.7 us  [the longest x4 10.2 us: shifted(): return lax.ppermute(value, 'win', [(i, (i + shift) % 8) for i in range(8)])]
    ppermute x0 -> x5, starting transfers between devices: none -> 10.9 us  [the longest x4 8.65 us: shifted(): return lax.ppermute(value, 'win', [(i, (i + shift) % 8) for i in range(8)])]
    pallas_call x0 -> x2, Pallas kernels: none -> 10.4 us  [the longest x1 7.27 us: local(): pl.pallas_call(main_kernel, out_shape=(part, part), in_specs=[smem] + [vm...]
    all_to_all x2 -> x1, starting transfers between devices: 19 us -> 9.36 us  [local(): blocks = lax.all_to_all(packed, 'chan', 0, 0, tiled=True)]
  transfers between devices with their start and end apart: 4 -> 6, of which waited for: 4 -> 6; matrix products, arithmetic and copies ran while one was open for 2% -> 0% of each run, Pallas kernels for 0% -> 0%
where the time goes in v1:
time: 64.1 us; the launch traced here: 63 us
  waiting for transfers between devices  28.3 us (44%)
  starting transfers between devices  20.3 us (32%)
  Pallas kernels  10.4 us (16%)
  local copies, waits for them, and re-layouts  3.15 us (5%)
  other arithmetic  0.86 us (1%)
    all_to_all x1, waiting for transfers between devices, local(): blocks = lax.all_to_all(packed, 'chan', 0, 0, tiled=True)  16.6 us
    ppermute x4, waiting for transfers between devices, shifted(): return lax.ppermute(value, 'win', [(i, (i + shift) % 8) for i in range(8)])  10.2 us
    all_to_all x1, starting transfers between devices, local(): blocks = lax.all_to_all(packed, 'chan', 0, 0, tiled=True)  9.36 us
    ppermute x4, starting transfers between devices, shifted(): return lax.ppermute(value, 'win', [(i, (i + shift) % 8) for i in range(8)])  8.65 us
    pallas_call x1, Pallas kernels, local(): pl.pallas_call(main_kernel, out_shape=(part, part), in_specs=[smem] + [vm...  7.27 us
    unnamed x10, local copies, waits for them, and re-layouts  3.13 us
    pallas_call x1, Pallas kernels, local(): pl.pallas_call(pack_kernel, out_shape=jax.ShapeDtypeStruct((chan_count, 2...  3.11 us
    ppermute x1, starting transfers between devices, local(): other = lax.ppermute(send, 'win', [(i, i ^ 1) for i in range(8)])  2.25 us
  transfers between devices with their start and end apart: 6, of which 6 were waited for; matrix products, arithmetic and copies ran while one was open for 0% of the time, Pallas kernels for 0%

profile of v1, /device:TPU:1, one launch (start us, length us, event | category | flops | bytes accessed | tf_op | source)
XLA Modules:
  0.0 63.0 jit_solution(13914646274838155742)
XLA Ops:
  0.0 3.1 %pack.1 = f32[32,64,128]{2,1,0:T(8,128)} custom-call(s32[32]{0:T(128)} %sources.1, f32[4,32,1024]{2,1,0:T(8,128)} %records.1), custom_call_target="tpu_custom_call" | custom-call | tf_op jit(solution)/shard_map/pack/pallas_call | solution.py:184
  3.1 0.0 copy-start
  3.1 0.0 copy-start.1
  3.1 9.4 %all-to-all-start = ((f32[32,64,128]{2,1,0:T(8,128)}), f32[32,64,128]{2,1,0:T(8,128)S(1)}, u32[]{:S(2)}, u32[]{:S(2)}) async-start(f32[32,64,128]{2,1,0:T(8,128)} %pack.1), calls=%async_computation | async-start | bytes 2097152 | tf_op jit(solution)/shard_map/all_to_all | solution.py:191
  12.5 0.1 pad_add_fusion.place
  12.6 16.6 %all-to-all-done.blocks = f32[32,64,128]{2,1,0:T(8,128)S(1)} async-done(((f32[32,64,128]{2,1,0:T(8,128)}), f32[32,64,128]{2,1,0:T(8,128)S(1)}, u32[]{:S(2)}, u32[]{:S(2)}) %all-to-all-start) | async-done | bytes 1048608 | tf_op jit(solution)/shard_map/all_to_all | solution.py:191
  29.2 0.0 copy-done
  29.2 0.0 copy-done.1
  29.2 1.0 %copy-done.2 = bf16[512,512]{1,0:T(8,128)(2,1)S(1)} copy-done((bf16[512,512]{1,0:T(8,128)(2,1)S(1)}, bf16[512,512]{1,0:T(8,128)(2,1)}, u32[]{:S(2)}) %copy-start.2) | copy-done | bytes 524312
  30.2 1.0 %copy-done.3 = bf16[1024,256]{1,0:T(8,128)(2,1)S(1)} copy-done((bf16[1024,256]{1,0:T(8,128)(2,1)S(1)}, bf16[1024,256]{1,0:T(8,128)(2,1)}, u32[]{:S(2)}) %copy-start.3) | copy-done | bytes 524312
  31.2 1.0 %copy-done.4 = bf16[1024,256]{1,0:T(8,128)(2,1)S(1)} copy-done((bf16[1024,256]{1,0:T(8,128)(2,1)S(1)}, bf16[1024,256]{1,0:T(8,128)(2,1)}, u32[]{:S(2)}) %copy-start.4) | copy-done | bytes 524312
  32.3 7.3 %stack.13 = (f32[4,128,256]{2,1,0:T(8,128)S(1)}, f32[4,128,256]{2,1,0:T(8,128)S(1)}) custom-call(s32[2]{0:T(128)S(1)} %pad_add_fusion.place, f32[32,64,128]{2,1,0:T(8,128)S(1)} %all-to-all-done.blocks, bf16[2,512,512]{2,1,0:T(8,128)(2,1)S(1)} %copy-done.1, bf16[2,512,512]{2,1,0:T(8,128)(2,1)S(1)} %copy-done, bf16[512,512]{1,0:T(8,128)(2,1)S(1)} %copy-done.2, ...), custom_call_target="tpu_custom_call" | custom-call | tf_op jit(solution)/shard_map/stack/pallas_call | solution.py:199
  39.6 2.3 %collective-permute-start = (f32[4,128,256]{2,1,0:T(8,128)S(1)}, f32[4,128,256]{2,1,0:T(8,128)S(1)}, u32[]{:S(2)}, u32[]{:S(2)}) collective-permute-start(f32[4,128,256]{2,1,0:T(8,128)S(1)} %get-tuple-element.8), channel_id=1, source_target_pairs={{0,1},{1,0},{2,3},{3,2},{4,5},{5,4},{6,7},{7,6},{8,9},{9,8},{10,11... | collective-permute-start | bytes 1572872 | tf_op jit(solution)/shard_map/ppermute | solution.py:218
  41.8 1.5 %collective-permute-done = f32[4,128,256]{2,1,0:T(8,128)S(1)} collective-permute-done((f32[4,128,256]{2,1,0:T(8,128)S(1)}, f32[4,128,256]{2,1,0:T(8,128)S(1)}, u32[]{:S(2)}, u32[]{:S(2)}) %collective-permute-start) | collective-permute-done | bytes 524320 | tf_op jit(solution)/shard_map/ppermute | solution.py:218
  43.4 0.1 add.21
  43.5 3.1 %collective-permute-start.1 = (f32[64,256]{1,0:T(8,128)S(1)}, f32[64,256]{1,0:T(8,128)S(1)}, u32[]{:S(2)}, u32[]{:S(2)}) collective-permute-start(f32[64,256]{1,0:T(8,128)S(1)} %get-tuple-element.11), channel_id=1, source_target_pairs={{0,2},{1,3},{2,4},{3,5},{4,6},{5,7},{6,0},{7,1},{8,10},{9,11},{10,... | collective-permute-start | bytes 196616 | tf_op jit(solution)/shard_map/ppermute | solution.py:216
  46.5 2.2 %collective-permute-start.3 = (f32[64,256]{1,0:T(8,128)S(1)}, f32[64,256]{1,0:T(8,128)S(1)}, u32[]{:S(2)}, u32[]{:S(2)}) collective-permute-start(f32[64,256]{1,0:T(8,128)S(1)} %get-tuple-element.12), channel_id=1, source_target_pairs={{0,6},{1,7},{2,0},{3,1},{4,2},{5,3},{6,4},{7,5},{8,14},{9,15},{10,... | collective-permute-start | bytes 196616 | tf_op jit(solution)/shard_map/ppermute | solution.py:216
  48.8 2.1 %collective-permute-done.1 = f32[64,256]{1,0:T(8,128)S(1)} collective-permute-done((f32[64,256]{1,0:T(8,128)S(1)}, f32[64,256]{1,0:T(8,128)S(1)}, u32[]{:S(2)}, u32[]{:S(2)}) %collective-permute-start.1) | collective-permute-done | bytes 65568 | tf_op jit(solution)/shard_map/ppermute | solution.py:216
  50.8 2.7 %collective-permute-done.3 = f32[64,256]{1,0:T(8,128)S(1)} collective-permute-done((f32[64,256]{1,0:T(8,128)S(1)}, f32[64,256]{1,0:T(8,128)S(1)}, u32[]{:S(2)}, u32[]{:S(2)}) %collective-permute-start.3) | collective-permute-done | bytes 65568 | tf_op jit(solution)/shard_map/ppermute | solution.py:216
  53.6 2.6 %collective-permute-start.4 = (f32[128,256]{1,0:T(8,128)S(1)}, f32[128,256]{1,0:T(8,128)S(1)}, u32[]{:S(2)}, u32[]{:S(2)}) collective-permute-start(f32[128,256]{1,0:T(8,128)S(1)} %pad_maximum_fusion.1), channel_id=1, source_target_pairs={{0,6},{1,7},{2,0},{3,1},{4,2},{5,3},{6,4},{7,5},{8,14},{9,15},{10,... | collective-permute-start | bytes 393224 | tf_op jit(solution)/shard_map/ppermute | solution.py:216
  56.2 0.8 %collective-permute-start.2 = (f32[128,256]{1,0:T(8,128)S(1)}, f32[128,256]{1,0:T(8,128)S(1)}, u32[]{:S(2)}, u32[]{:S(2)}) collective-permute-start(f32[128,256]{1,0:T(8,128)S(1)} %pad_maximum_fusion), channel_id=1, source_target_pairs={{0,2},{1,3},{2,4},{3,5},{4,6},{5,7},{6,0},{7,1},{8,10},{9,11},{10,... | collective-permute-start | bytes 393224 | tf_op jit(solution)/shard_map/ppermute | solution.py:216
  57.0 4.6 %collective-permute-done.4 = f32[128,256]{1,0:T(8,128)S(1)} collective-permute-done((f32[128,256]{1,0:T(8,128)S(1)}, f32[128,256]{1,0:T(8,128)S(1)}, u32[]{:S(2)}, u32[]{:S(2)}) %collective-permute-start.4) | collective-permute-done | bytes 131104 | tf_op jit(solution)/shard_map/ppermute | solution.py:216
  61.6 0.7 %collective-permute-done.2 = f32[128,256]{1,0:T(8,128)S(1)} collective-permute-done((f32[128,256]{1,0:T(8,128)S(1)}, f32[128,256]{1,0:T(8,128)S(1)}, u32[]{:S(2)}, u32[]{:S(2)}) %collective-permute-start.2) | collective-permute-done | bytes 131104 | tf_op jit(solution)/shard_map/ppermute | solution.py:216
  62.3 0.7 %fusion.1 = f32[128,256]{1,0:T(8,128)} fusion(f32[128,256]{1,0:T(8,128)S(1)} %collective-permute-done.4, f32[128,256]{1,0:T(8,128)S(1)} %collective-permute-done.2, f32[4,128,256]{2,1,0:T(8,128)S(1)} %add.21), kind=kLoop, calls=%fused_computation.2 | loop fusion | flops 65536 | bytes 524288 | tf_op jit(solution)/shard_map/add | solution.py:225
  (7 shorter events, 0.1 us)
Async XLA Ops:
  3.1 26.0 %copy-start = (bf16[2,512,512]{2,1,0:T(8,128)(2,1)S(1)}, bf16[2,512,512]{2,1,0:T(8,128)(2,1)}, u32[]{:S(2)}) copy-start(bf16[2,512,512]{2,1,0:T(8,128)(2,1)} %constant.39.clone.fwd_low) | copy-start | bytes 3145732
  3.1 26.0 %copy-start.1 = (bf16[2,512,512]{2,1,0:T(8,128)(2,1)S(1)}, bf16[2,512,512]{2,1,0:T(8,128)(2,1)}, u32[]{:S(2)}) copy-start(bf16[2,512,512]{2,1,0:T(8,128)(2,1)} %constant.38.clone.fwd_high) | copy-start | bytes 3145732
  3.1 26.0 %all-to-all-start = ((f32[32,64,128]{2,1,0:T(8,128)}), f32[32,64,128]{2,1,0:T(8,128)S(1)}, u32[]{:S(2)}, u32[]{:S(2)}) async-start(f32[32,64,128]{2,1,0:T(8,128)} %pack.1), calls=%async_computation | async-start | bytes 2097152 | tf_op jit(solution)/shard_map/all_to_all | solution.py:191
  29.2 1.0 %copy-start.2 = (bf16[512,512]{1,0:T(8,128)(2,1)S(1)}, bf16[512,512]{1,0:T(8,128)(2,1)}, u32[]{:S(2)}) copy-start(bf16[512,512]{1,0:T(8,128)(2,1)} %constant.42.clone.band) | copy-start | bytes 1572868
  30.2 1.0 %copy-start.3 = (bf16[1024,256]{1,0:T(8,128)(2,1)S(1)}, bf16[1024,256]{1,0:T(8,128)(2,1)}, u32[]{:S(2)}) copy-start(bf16[1024,256]{1,0:T(8,128)(2,1)} %constant.41.clone.inv_low) | copy-start | bytes 1572868
  31.2 1.0 %copy-start.4 = (bf16[1024,256]{1,0:T(8,128)(2,1)S(1)}, bf16[1024,256]{1,0:T(8,128)(2,1)}, u32[]{:S(2)}) copy-start(bf16[1024,256]{1,0:T(8,128)(2,1)} %constant.40.clone.inv_high) | copy-start | bytes 1572868
  39.6 3.8 %collective-permute-start = (f32[4,128,256]{2,1,0:T(8,128)S(1)}, f32[4,128,256]{2,1,0:T(8,128)S(1)}, u32[]{:S(2)}, u32[]{:S(2)}) collective-permute-start(f32[4,128,256]{2,1,0:T(8,128)S(1)} %get-tuple-element.8), channel_id=1, source_target_pairs={{0,1},{1,0},{2,3},{3,2},{4,5},{5,4},{6,7},{7,6},{8,9},{9,8},{10,11... | collective-permute-start | bytes 1572872 | tf_op jit(solution)/shard_map/ppermute | solution.py:218
  43.5 7.4 %collective-permute-start.1 = (f32[64,256]{1,0:T(8,128)S(1)}, f32[64,256]{1,0:T(8,128)S(1)}, u32[]{:S(2)}, u32[]{:S(2)}) collective-permute-start(f32[64,256]{1,0:T(8,128)S(1)} %get-tuple-element.11), channel_id=1, source_target_pairs={{0,2},{1,3},{2,4},{3,5},{4,6},{5,7},{6,0},{7,1},{8,10},{9,11},{10,... | collective-permute-start | bytes 196616 | tf_op jit(solution)/shard_map/ppermute | solution.py:216
  46.5 7.1 %collective-permute-start.3 = (f32[64,256]{1,0:T(8,128)S(1)}, f32[64,256]{1,0:T(8,128)S(1)}, u32[]{:S(2)}, u32[]{:S(2)}) collective-permute-start(f32[64,256]{1,0:T(8,128)S(1)} %get-tuple-element.12), channel_id=1, source_target_pairs={{0,6},{1,7},{2,0},{3,1},{4,2},{5,3},{6,4},{7,5},{8,14},{9,15},{10,... | collective-permute-start | bytes 196616 | tf_op jit(solution)/shard_map/ppermute | solution.py:216
  53.6 8.0 %collective-permute-start.4 = (f32[128,256]{1,0:T(8,128)S(1)}, f32[128,256]{1,0:T(8,128)S(1)}, u32[]{:S(2)}, u32[]{:S(2)}) collective-permute-start(f32[128,256]{1,0:T(8,128)S(1)} %pad_maximum_fusion.1), channel_id=1, source_target_pairs={{0,6},{1,7},{2,0},{3,1},{4,2},{5,3},{6,4},{7,5},{8,14},{9,15},{10,... | collective-permute-start | bytes 393224 | tf_op jit(solution)/shard_map/ppermute | solution.py:216
  56.2 6.1 %collective-permute-start.2 = (f32[128,256]{1,0:T(8,128)S(1)}, f32[128,256]{1,0:T(8,128)S(1)}, u32[]{:S(2)}, u32[]{:S(2)}) collective-permute-start(f32[128,256]{1,0:T(8,128)S(1)} %pad_maximum_fusion), channel_id=1, source_target_pairs={{0,2},{1,3},{2,4},{3,5},{4,6},{5,7},{6,0},{7,1},{8,10},{9,11},{10,... | collective-permute-start | bytes 393224 | tf_op jit(solution)/shard_map/ppermute | solution.py:216

commit v2 on v1

v2 whole, which is shorter than its diff:
```python
import functools
import math

import jax
import jax.numpy as jnp
import ml_dtypes
import numpy as np
from jax import lax
from jax.experimental import pallas as pl
from jax.experimental.pallas import tpu as pltpu
from jax.sharding import PartitionSpec as P

AMPLITUDE_FLOOR = 0.25
WHITE_EPSILON = 1e-06
HALF = 16
LANES = 128
F32 = jnp.float32
BF16 = jnp.bfloat16


def split_table(table):
    high = table.astype(np.float32).astype(ml_dtypes.bfloat16)
    low = (table - high.astype(np.float64)).astype(np.float32).astype(ml_dtypes.bfloat16)
    return high, low


def bin_order(half):
    return np.concatenate([np.arange(0, half, 2), np.arange(1, half, 2)])


def forward_tables(length):
    half = length // 2
    times = np.arange(half)[:, None]
    tables = []
    for parity in range(2):
        bins = np.arange(parity, half, 2)[None, :]
        angles = (bins * times % length) * (2.0 * math.pi / length)
        tables += split_table(np.concatenate([np.cos(angles), -np.sin(angles)], axis=1))
    return np.stack(tables)


def band_tables(half, reach):
    bins = bin_order(half)
    table = (np.abs(bins[:, None] - bins[None, :]) <= reach).astype(ml_dtypes.bfloat16)
    mid = half // 2
    return np.stack([table[:mid, :mid], table[mid:, :mid], table[:mid, mid:]])


def inverse_tables(length, lag_count, factor):
    half = length // 2
    bins = bin_order(half)
    lags = np.arange(lag_count) - lag_count // 2
    angles = (bins[:, None] * lags[None, :] % length) * (2.0 * math.pi / length)
    weights = np.where(bins == 0, 1.0, 2.0)[:, None] * factor
    return np.stack(
        split_table(np.concatenate([weights * np.cos(angles), -weights * np.sin(angles)], axis=1))
    )


def split(value):
    high = value.astype(BF16)
    return high, (value - high.astype(F32)).astype(BF16)


def mm(left, right):
    return jnp.dot(left, right, preferred_element_type=F32)


def pack_kernel(sources, records, packed, taken, blocks, chosen, sems_in, sems_out):
    windows, times, channels = records.shape
    dests = packed.shape[0]
    width = channels // dests
    per_tile = LANES // width
    tiles = channels // LANES
    loads = []
    for tile in range(tiles):
        load = pltpu.make_async_copy(
            records.at[:, :, tile * LANES : (tile + 1) * LANES], taken.at[tile], sems_in.at[tile]
        )
        load.start()
        loads.append(load)
    stores = []
    lane = lax.broadcasted_iota(jnp.int32, (times, LANES), 1)
    pick = jnp.zeros((times, LANES), F32)
    for tile in range(tiles):
        loads[tile].wait()
        loaded = [taken[tile, w] for w in range(windows)]
        for e in range(per_tile):
            block = None
            for w in range(windows):
                shift = (w - e) * width % LANES
                moved = pltpu.roll(loaded[w], shift, 1) if shift else loaded[w]
                block = moved if block is None else jnp.where(lane >= w * width, moved, block)
            blocks[tile * per_tile + e] = block
        span = pl.ds(tile * per_tile, per_tile)
        store = pltpu.make_async_copy(
            blocks.at[span], packed.at[span, 0:times, :], sems_out.at[tile]
        )
        store.start()
        stores.append(store)
        for e in range(per_tile):
            s = tile * per_tile + e
            place = sources[s] - tile * LANES
            for w in range(windows):
                target = w * dests + s
                shift = lax.rem(target + LANES - place, LANES)
                pick = jnp.where(lane == target, pltpu.roll(loaded[w], shift, 1), pick)
    for d in range(dests):
        chosen[d] = pick
    store = pltpu.make_async_copy(chosen, packed.at[:, times : 2 * times, :], sems_out.at[tiles])
    store.start()
    stores.append(store)
    for store in stores:
        store.wait()


def position():
    win = lax.axis_index("win")
    return lax.div(win, 2), lax.rem(win, 2)


def correlate(white_re, white_im, cross_high, cross_low, target, which, core, width):
    rows, half = white_re.shape
    lanes = rows // 2
    windows = lanes // width
    turn = lax.rem(8 - (4 * core if which else 4 - 4 * core), 8)
    rows8 = [
        pl.ds(pl.multiple_of(lanes + w * width + target * 8, 8), 8) for w in range(windows)
    ]
    for tile in range(half // LANES):
        span = slice(tile * LANES, (tile + 1) * LANES)
        span2 = slice(half + tile * LANES, half + (tile + 1) * LANES)
        chan_re = [white_re[w * width : (w + 1) * width, span] for w in range(windows)]
        chan_im = [white_im[w * width : (w + 1) * width, span] for w in range(windows)]
        from_re = [pltpu.roll(white_re[at, span], turn, 0) for at in rows8]
        from_im = [pltpu.roll(white_im[at, span], turn, 0) for at in rows8]
        for i in range(4):
            out_re = None
            for w in range(windows):
                src_re = jnp.broadcast_to(from_re[w][i : i + 1], (width, LANES))
                src_im = jnp.broadcast_to(from_im[w][i : i + 1], (width, LANES))
                add_re = src_re * chan_re[w] + src_im * chan_im[w]
                add_im = src_re * chan_im[w] - src_im * chan_re[w]
                out_re = add_re if w == 0 else out_re + add_re
                out_im = add_im if w == 0 else out_im + add_im
            at = slice(i * width, (i + 1) * width)
            cross_high[at, span], cross_low[at, span] = split(out_re)
            cross_high[at, span2], cross_low[at, span2] = split(out_im)


def invert(cross_high, cross_low, tables):
    half = cross_high.shape[1] // 2
    lags = half // 2
    total = None
    for part in range(2):
        high = cross_high[:, part * half : (part + 1) * half]
        low = cross_low[:, part * half : (part + 1) * half]
        wave = tables[0, :, part * lags : (part + 1) * lags]
        rest = tables[1, :, part * lags : (part + 1) * lags]
        term = mm(high, wave) + mm(low, wave) + mm(high, rest)
        total = term if part == 0 else total + term
    return total


def front_kernel(
    blocks, tables, band, white_re, white_im, turned
):
    devices, double, lanes = blocks.shape
    times = double // 2
    length = devices * times
    half = length // 2
    quarter = half // 2
    for part in range(2):
        data = blocks[:, part * times : (part + 1) * times, :].reshape(length, lanes)
        level = jnp.abs(data)
        edge = jnp.zeros((HALF, lanes), F32)
        tail = jnp.concatenate([level, edge], axis=0)
        total = jnp.concatenate([edge, level, edge], axis=0)
        size = length + 2 * HALF
        for step in (1, 2, 4, 8, 16):
            total = total + pltpu.roll(total, size - step, 0)
        amplitude = (total[:length] + tail[HALF:]) / (2 * HALF + 1)
        normal = data / jnp.maximum(amplitude, AMPLITUDE_FLOOR)
        turned[part * lanes : (part + 1) * lanes, :] = normal.T
    first = turned[:, :half]
    second = turned[:, half:]
    for parity in range(2):
        folded = first + second if parity == 0 else first - second
        high, low = split(folded)
        spectrum = (
            mm(high, tables[2 * parity])
            + mm(low, tables[2 * parity])
            + mm(high, tables[2 * parity + 1])
        )
        white_re[:, parity * quarter : (parity + 1) * quarter] = spectrum[:, :quarter]
        white_im[:, parity * quarter : (parity + 1) * quarter] = spectrum[:, quarter:]
    re = white_re[...]
    im = white_im[...]
    high, low = split(jnp.sqrt(re * re + im * im))
    for parity in range(2):
        near = slice(parity * quarter, (parity + 1) * quarter)
        other = slice((1 - parity) * quarter, (2 - parity) * quarter)
        smooth = (
            mm(high[:, near], band[0])
            + mm(low[:, near], band[0])
            + mm(high[:, other], band[1 + parity])
            + mm(low[:, other], band[1 + parity])
        )
        gain = 1.0 / (smooth / (2 * (length // 32) + 1) + WHITE_EPSILON)
        white_re[:, near] = re[:, near] * gain
        white_im[:, near] = im[:, near] * gain


def stack_kernel(slots, white_re, white_im, tables, *refs):
    send, keep, cross_high, cross_low = refs[-4:]
    z_hi, core = position()
    for n, slot in enumerate(slots):
        target = lax.rem(z_hi + slot, 4)
        for which in range(2):
            correlate(white_re, white_im, cross_high, cross_low, target, which, core, 32)
            (keep if which else send)[n] = invert(cross_high, cross_low, tables)


def local(records, sources):
    chan_count = lax.axis_size("chan")
    windows, times, channels = records.shape
    length = times * chan_count
    lag_count = length // 4
    half = length // 2
    total_windows = windows * lax.axis_size("win")
    factor = 1.0 / math.sqrt(total_windows * half)
    vmem = pl.BlockSpec(memory_space=pltpu.VMEM)
    smem = pl.BlockSpec(memory_space=pltpu.SMEM)
    hbm = pl.BlockSpec(memory_space=pltpu.HBM)
    tiles = channels // LANES

    packed = pl.pallas_call(
        pack_kernel,
        out_shape=jax.ShapeDtypeStruct((chan_count, 2 * times, LANES), F32),
        in_specs=[smem, hbm],
        out_specs=hbm,
        scratch_shapes=[
            pltpu.VMEM((tiles, windows, times, LANES), F32),
            pltpu.VMEM((chan_count, times, LANES), F32),
            pltpu.VMEM((chan_count, times, LANES), F32),
            pltpu.SemaphoreType.DMA((tiles,)),
            pltpu.SemaphoreType.DMA((tiles + 1,)),
        ],
        name="pack",
    )(sources, records)
    blocks = lax.all_to_all(packed, "chan", 0, 0, tiled=True)

    forward = jnp.asarray(forward_tables(length))
    band = jnp.asarray(band_tables(half, length // 32))
    inverse = jnp.asarray(inverse_tables(length, lag_count, factor))
    rows = 2 * LANES
    shape = jax.ShapeDtypeStruct
    white_re, white_im = pl.pallas_call(
        front_kernel,
        out_shape=(shape((rows, half), F32), shape((rows, half), F32)),
        in_specs=[vmem] * 3,
        out_specs=(vmem, vmem),
        scratch_shapes=[pltpu.VMEM((rows, length), F32)],
        compiler_params=pltpu.CompilerParams(vmem_limit_bytes=24 << 20),
        cost_estimate=pl.CostEstimate(flops=2 << 30, bytes_accessed=10 << 20, transcendentals=0),
        name="front",
    )(blocks, forward, band)

    def stack(slots, after=None, handed=None):
        part = shape((len(slots), LANES, lag_count), F32)
        extra = [] if after is None else [after]
        outs = [part, part]
        aliases = {}
        if handed is not None:
            aliases = {3 + len(extra): 0}
            extra.append(handed)
            outs.insert(0, shape(handed.shape, F32))
        return pl.pallas_call(
            functools.partial(stack_kernel, slots),
            out_shape=outs,
            in_specs=[vmem] * (3 + len(extra)),
            out_specs=[vmem] * len(outs),
            scratch_shapes=[pltpu.VMEM((LANES, length), BF16), pltpu.VMEM((LANES, length), BF16)],
            input_output_aliases=aliases,
            compiler_params=pltpu.CompilerParams(vmem_limit_bytes=16 << 20),
            cost_estimate=pl.CostEstimate(
                flops=len(slots) << 30, bytes_accessed=len(slots) << 22, transcendentals=0
            ),
            name="stack",
        )(white_re, white_im, inverse, *extra)

    def shifted(value, shift):
        return lax.ppermute(value, "win", [(i, (i + shift) % 8) for i in range(8)])

    def across(value):
        return lax.ppermute(value, "win", [(i, i ^ 1) for i in range(8)])

    mid = LANES // 2
    send_far, keep_far = stack((2,))
    keep_far, send_right, keep_right = stack((1,), handed=keep_far)
    far = keep_far[0] + across(send_far)[0]
    from_left = shifted(far[:mid], 2)
    from_right = shifted(far[mid:], -2)
    keep_right, send, keep = stack((3, 0), after=far, handed=keep_right)
    pair = keep + across(send)
    right = keep_right[0] + across(send_right)[0]
    right = jnp.concatenate([right[:mid] + from_left, right[mid:]], axis=0)
    left = jnp.concatenate([pair[0, :mid], pair[0, mid:] + from_right], axis=0)
    result = pair[1] + shifted(right, 2) + shifted(left, -2)
    return jnp.transpose(result.reshape(4, 32, lag_count), (0, 2, 1))


def solution(mesh):
    placed = (P("win", "chan", None), P())
    return jax.shard_map(
        local, mesh=mesh, in_specs=placed, out_specs=P("win", None, "chan"), check_vma=False
    )
```

time: 64.1 us -> 58.4 us (0.911); the launches traced: 63 us -> 58.1 us
  blocking collectives: 0 us -> 25.9 us
  waiting for transfers between devices: 28.3 us -> 7.97 us
  starting transfers between devices: 20.3 us -> 12.2 us
  local copies, waits for them, and re-layouts: 3.15 us -> 0.03 us
  Pallas kernels: 10.4 us -> 11.1 us
    all_to_all x0 -> x1, blocking collectives: none -> 25.9 us  [local(): blocks = lax.all_to_all(packed, 'chan', 0, 0, tiled=True)]
    all_to_all x1 -> x0, waiting for transfers between devices: 16.6 us -> none  [local(): blocks = lax.all_to_all(packed, 'chan', 0, 0, tiled=True)]
    all_to_all x1 -> x0, starting transfers between devices: 9.36 us -> none  [local(): blocks = lax.all_to_all(packed, 'chan', 0, 0, tiled=True)]
    unnamed x10 -> x6, local copies, waits for them, and re-layouts: 3.13 us -> 0.01 us
    ppermute x4, waiting for transfers between devices: 10.2 us -> 7.96 us  [shifted(): return lax.ppermute(value, 'win', [(i, (i + shift) % 8) for i in range(8)])]
    ppermute x1 -> x3, waiting for transfers between devices: 1.54 us -> 0.01 us  [across(): return lax.ppermute(value, 'win', [(i, i ^ 1) for i in range(8)])]
    pallas_call x1, Pallas kernels: 3.11 us -> 4.15 us  [local(): pl.pallas_call(pack_kernel, out_shape=jax.ShapeDtypeStruct((chan_count, 2...]
    ppermute x1 -> x3, starting transfers between devices: 2.25 us -> 3.2 us  [across(): return lax.ppermute(value, 'win', [(i, i ^ 1) for i in range(8)])]
  transfers between devices with their start and end apart: 6 -> 7, of which waited for: 6 -> 3; matrix products, arithmetic and copies ran while one was open for 0% -> 0% of each run, Pallas kernels for 0% -> 6%
where the time goes in v2:
time: 58.4 us; the launch traced here: 58.1 us
  blocking collectives  25.9 us (44%)
  starting transfers between devices  12.2 us (21%)
  Pallas kernels  11.1 us (19%)
  waiting for transfers between devices  7.97 us (14%)
  other arithmetic  0.79 us (1%)
    all_to_all x1, blocking collectives, local(): blocks = lax.all_to_all(packed, 'chan', 0, 0, tiled=True)  25.9 us
    ppermute x4, starting transfers between devices, shifted(): return lax.ppermute(value, 'win', [(i, (i + shift) % 8) for i in range(8)])  9.02 us
    ppermute x4, waiting for transfers between devices, shifted(): return lax.ppermute(value, 'win', [(i, (i + shift) % 8) for i in range(8)])  7.96 us
    pallas_call x3, Pallas kernels, stack(): pl.pallas_call(functools.partial(stack_kernel, slots), out_shape=outs, in...  4.96 us
    pallas_call x1, Pallas kernels, local(): pl.pallas_call(pack_kernel, out_shape=jax.ShapeDtypeStruct((chan_count, 2...  4.15 us
    ppermute x3, starting transfers between devices, across(): return lax.ppermute(value, 'win', [(i, i ^ 1) for i in range(8)])  3.2 us
    pallas_call x1, Pallas kernels, local(): pl.pallas_call(front_kernel, out_shape=(shape((rows, half), F32), shape((...  1.99 us
  transfers between devices with their start and end apart: 7, of which 3 were waited for; matrix products, arithmetic and copies ran while one was open for 0% of the time, Pallas kernels for 6%

profile of v2, /device:TPU:1, one launch (start us, length us, event | category | flops | bytes accessed | tf_op | source)
XLA Modules:
  0.0 58.1 jit_solution(9956981017239848624)
XLA Ops:
  0.0 4.1 %pack.1 = f32[32,64,128]{2,1,0:T(8,128)} custom-call(s32[32]{0:T(128)} %sources.1, f32[4,32,1024]{2,1,0:T(8,128)} %records.1), custom_call_target="tpu_custom_call" | custom-call | tf_op jit(solution)/shard_map/pack/pallas_call | solution.py:237
  4.2 25.9 %all_to_all.5.blocks = f32[32,64,128]{2,1,0:T(8,128)S(1)} all-to-all(f32[32,64,128]{2,1,0:T(8,128)} %pack.1), channel_id=1, replica_groups=mesh['chan'=32,'win'=8] {'chan'}, dimensions={0} | all-to-all | bytes 2097152 | tf_op jit(solution)/shard_map/all_to_all | solution.py:251
  30.1 0.0 copy-done.2
  30.1 0.0 copy-done
  30.1 2.0 %front.1 = (f32[256,512]{1,0:T(8,128)S(1)}, f32[256,512]{1,0:T(8,128)S(1)}) custom-call(f32[32,64,128]{2,1,0:T(8,128)S(1)} %all_to_all.5.blocks, bf16[4,512,512]{2,1,0:T(8,128)(2,1)S(1)} %copy-done, bf16[3,256,256]{2,1,0:T(8,128)(2,1)S(1)} %copy-done.2), custom_call_target="tpu_custom_call" | custom-call | flops 2147483648 | bytes 10485760 | tf_op jit(solution)/shard_map/front/pallas_call | solution.py:258
  32.1 0.0 copy-done.1
  32.1 1.3 %stack.3 = (f32[1,128,256]{2,1,0:T(8,128)S(1)}, f32[1,128,256]{2,1,0:T(8,128)S(1)}) custom-call(f32[256,512]{1,0:T(8,128)S(1)} %get-tuple-element.15.white_re, f32[256,512]{1,0:T(8,128)S(1)} %get-tuple-element.16.white_im, bf16[2,512,512]{2,1,0:T(8,128)(2,1)S(1)} %copy-done.1), custom_call_target="tpu_custom_call" | custom-call | flops 1073741824 | bytes 4194304 | tf_op jit(solution)/shard_map/stack/pallas_call | solution.py:278
  33.4 2.2 %collective-permute-start = (f32[1,128,256]{2,1,0:T(8,128)S(1)}, f32[1,128,256]{2,1,0:T(8,128)S(1)}, u32[]{:S(2)}, u32[]{:S(2)}) collective-permute-start(f32[1,128,256]{2,1,0:T(8,128)S(1)} %get-tuple-element.19), channel_id=1, source_target_pairs={{0,1},{1,0},{2,3},{3,2},{4,5},{5,4},{6,7},{7,6},{8,9},{9,8},{10,11... | collective-permute-start | bytes 393224 | tf_op jit(solution)/shard_map/ppermute | solution.py:296
  35.6 1.3 %stack.4 = (f32[1,128,256]{2,1,0:T(8,128)S(1)}, f32[1,128,256]{2,1,0:T(8,128)S(1)}, f32[1,128,256]{2,1,0:T(8,128)S(1)}) custom-call(f32[256,512]{1,0:T(8,128)S(1)} %get-tuple-element.15.white_re, f32[256,512]{1,0:T(8,128)S(1)} %get-tuple-element.16.white_im, bf16[2,512,512]{2,1,0:T(8,128)(2,1)S(1)} %copy-done.1, ...), custom_call_target="tpu_custom_call", output_to_operand_aliasing={{0}: (3, {})} | custom-call | flops 1073741824 | bytes 4194304 | tf_op jit(solution)/shard_map/stack/pallas_call | solution.py:278
  36.9 0.1 collective-permute-start.2
  37.0 0.0 collective-permute-done
  37.1 3.1 %collective-permute-start.3 = (f32[64,256]{1,0:T(8,128)S(1)}, f32[64,256]{1,0:T(8,128)S(1)}, u32[]{:S(2)}, u32[]{:S(2)}) collective-permute-start(f32[64,256]{1,0:T(8,128)S(1)} %get-tuple-element.25), channel_id=1, source_target_pairs={{0,2},{1,3},{2,4},{3,5},{4,6},{5,7},{6,0},{7,1},{8,10},{9,11},{10,... | collective-permute-start | bytes 196616 | tf_op jit(solution)/shard_map/ppermute | solution.py:293
  40.1 2.2 %collective-permute-start.5 = (f32[64,256]{1,0:T(8,128)S(1)}, f32[64,256]{1,0:T(8,128)S(1)}, u32[]{:S(2)}, u32[]{:S(2)}) collective-permute-start(f32[64,256]{1,0:T(8,128)S(1)} %get-tuple-element.26), channel_id=1, source_target_pairs={{0,6},{1,7},{2,0},{3,1},{4,2},{5,3},{6,4},{7,5},{8,14},{9,15},{10,... | collective-permute-start | bytes 196616 | tf_op jit(solution)/shard_map/ppermute | solution.py:293
  42.4 2.4 %stack.5 = (f32[1,128,256]{2,1,0:T(8,128)S(1)}, f32[2,128,256]{2,1,0:T(8,128)S(1)}, f32[2,128,256]{2,1,0:T(8,128)S(1)}) custom-call(f32[256,512]{1,0:T(8,128)S(1)} %get-tuple-element.15.white_re, f32[256,512]{1,0:T(8,128)S(1)} %get-tuple-element.16.white_im, bf16[2,512,512]{2,1,0:T(8,128)(2,1)S(1)} %copy-done.1, ...), custom_call_target="tpu_custom_call", output_to_operand_aliasing={{0}: (4, {})} | custom-call | flops 2147483648 | bytes 8388608 | tf_op jit(solution)/shard_map/stack/pallas_call | solution.py:278
  44.8 0.0 collective-permute-done.2
  44.8 0.9 %collective-permute-start.1 = (f32[2,128,256]{2,1,0:T(8,128)S(1)}, f32[2,128,256]{2,1,0:T(8,128)S(1)}, u32[]{:S(2)}, u32[]{:S(2)}) collective-permute-start(f32[2,128,256]{2,1,0:T(8,128)S(1)} %get-tuple-element.22), channel_id=1, source_target_pairs={{0,1},{1,0},{2,3},{3,2},{4,5},{5,4},{6,7},{7,6},{8,9},{9,8},{10,11... | collective-permute-start | bytes 786440 | tf_op jit(solution)/shard_map/ppermute | solution.py:296
  45.7 0.0 collective-permute-done.3
  45.7 1.2 %collective-permute-start.4 = (f32[128,256]{1,0:T(8,128)S(1)}, f32[128,256]{1,0:T(8,128)S(1)}, u32[]{:S(2)}, u32[]{:S(2)}) collective-permute-start(f32[128,256]{1,0:T(8,128)S(1)} %pad_maximum_fusion), channel_id=1, source_target_pairs={{0,2},{1,3},{2,4},{3,5},{4,6},{5,7},{6,0},{7,1},{8,10},{9,11},{10,... | collective-permute-start | bytes 393224 | tf_op jit(solution)/shard_map/ppermute | solution.py:293
  46.9 0.0 collective-permute-done.1
  46.9 0.3 collective-permute-done.5
  47.2 2.6 %collective-permute-start.6 = (f32[128,256]{1,0:T(8,128)S(1)}, f32[128,256]{1,0:T(8,128)S(1)}, u32[]{:S(2)}, u32[]{:S(2)}) collective-permute-start(f32[128,256]{1,0:T(8,128)S(1)} %pad_maximum_fusion.1), channel_id=1, source_target_pairs={{0,6},{1,7},{2,0},{3,1},{4,2},{5,3},{6,4},{7,5},{8,14},{9,15},{10,... | collective-permute-start | bytes 393224 | tf_op jit(solution)/shard_map/ppermute | solution.py:293
  49.8 4.0 %collective-permute-done.4 = f32[128,256]{1,0:T(8,128)S(1)} collective-permute-done((f32[128,256]{1,0:T(8,128)S(1)}, f32[128,256]{1,0:T(8,128)S(1)}, u32[]{:S(2)}, u32[]{:S(2)}) %collective-permute-start.4) | collective-permute-done | bytes 131104 | tf_op jit(solution)/shard_map/ppermute | solution.py:293
  53.8 3.7 %collective-permute-done.6 = f32[128,256]{1,0:T(8,128)S(1)} collective-permute-done((f32[128,256]{1,0:T(8,128)S(1)}, f32[128,256]{1,0:T(8,128)S(1)}, u32[]{:S(2)}, u32[]{:S(2)}) %collective-permute-start.6) | collective-permute-done | bytes 131104 | tf_op jit(solution)/shard_map/ppermute | solution.py:293
  57.5 0.7 %fusion.1 = f32[128,256]{1,0:T(8,128)} fusion(f32[128,256]{1,0:T(8,128)S(1)} %collective-permute-done.6, f32[128,256]{1,0:T(8,128)S(1)} %collective-permute-done.4, f32[2,128,256]{2,1,0:T(8,128)S(1)} %add.26), kind=kLoop, calls=%fused_computation.2 | loop fusion | flops 65536 | bytes 524288 | tf_op jit(solution)/shard_map/add | solution.py:309
  (13 shorter events, 0.1 us)
Async XLA Ops:
  0.0 30.1 %copy-start.2 = (bf16[3,256,256]{2,1,0:T(8,128)(2,1)S(1)}, bf16[3,256,256]{2,1,0:T(8,128)(2,1)}, u32[]{:S(2)}) copy-start(bf16[3,256,256]{2,1,0:T(8,128)(2,1)} %constant.7.clone.band) | copy-start | bytes 1179652
  0.0 30.1 %copy-start = (bf16[4,512,512]{2,1,0:T(8,128)(2,1)S(1)}, bf16[4,512,512]{2,1,0:T(8,128)(2,1)}, u32[]{:S(2)}) copy-start(bf16[4,512,512]{2,1,0:T(8,128)(2,1)} %constant.6.clone.tables) | copy-start | bytes 6291460
  30.1 2.0 %copy-start.1 = (bf16[2,512,512]{2,1,0:T(8,128)(2,1)S(1)}, bf16[2,512,512]{2,1,0:T(8,128)(2,1)}, u32[]{:S(2)}) copy-start(bf16[2,512,512]{2,1,0:T(8,128)(2,1)} %constant.8.clone.tables) | copy-start | bytes 3145732
  33.4 3.6 %collective-permute-start = (f32[1,128,256]{2,1,0:T(8,128)S(1)}, f32[1,128,256]{2,1,0:T(8,128)S(1)}, u32[]{:S(2)}, u32[]{:S(2)}) collective-permute-start(f32[1,128,256]{2,1,0:T(8,128)S(1)} %get-tuple-element.19), channel_id=1, source_target_pairs={{0,1},{1,0},{2,3},{3,2},{4,5},{5,4},{6,7},{7,6},{8,9},{9,8},{10,11... | collective-permute-start | bytes 393224 | tf_op jit(solution)/shard_map/ppermute | solution.py:296
  36.9 7.8 %collective-permute-start.2 = (f32[1,128,256]{2,1,0:T(8,128)S(1)}, f32[1,128,256]{2,1,0:T(8,128)S(1)}, u32[]{:S(2)}, u32[]{:S(2)}) collective-permute-start(f32[1,128,256]{2,1,0:T(8,128)S(1)} %get-tuple-element.24), channel_id=1, source_target_pairs={{0,1},{1,0},{2,3},{3,2},{4,5},{5,4},{6,7},{7,6},{8,9},{9,8},{10,11... | collective-permute-start | bytes 393224 | tf_op jit(solution)/shard_map/ppermute | solution.py:296
  37.1 8.6 %collective-permute-start.3 = (f32[64,256]{1,0:T(8,128)S(1)}, f32[64,256]{1,0:T(8,128)S(1)}, u32[]{:S(2)}, u32[]{:S(2)}) collective-permute-start(f32[64,256]{1,0:T(8,128)S(1)} %get-tuple-element.25), channel_id=1, source_target_pairs={{0,2},{1,3},{2,4},{3,5},{4,6},{5,7},{6,0},{7,1},{8,10},{9,11},{10,... | collective-permute-start | bytes 196616 | tf_op jit(solution)/shard_map/ppermute | solution.py:293
  40.1 7.1 %collective-permute-start.5 = (f32[64,256]{1,0:T(8,128)S(1)}, f32[64,256]{1,0:T(8,128)S(1)}, u32[]{:S(2)}, u32[]{:S(2)}) collective-permute-start(f32[64,256]{1,0:T(8,128)S(1)} %get-tuple-element.26), channel_id=1, source_target_pairs={{0,6},{1,7},{2,0},{3,1},{4,2},{5,3},{6,4},{7,5},{8,14},{9,15},{10,... | collective-permute-start | bytes 196616 | tf_op jit(solution)/shard_map/ppermute | solution.py:293
  44.8 2.1 %collective-permute-start.1 = (f32[2,128,256]{2,1,0:T(8,128)S(1)}, f32[2,128,256]{2,1,0:T(8,128)S(1)}, u32[]{:S(2)}, u32[]{:S(2)}) collective-permute-start(f32[2,128,256]{2,1,0:T(8,128)S(1)} %get-tuple-element.22), channel_id=1, source_target_pairs={{0,1},{1,0},{2,3},{3,2},{4,5},{5,4},{6,7},{7,6},{8,9},{9,8},{10,11... | collective-permute-start | bytes 786440 | tf_op jit(solution)/shard_map/ppermute | solution.py:296
  45.7 8.1 %collective-permute-start.4 = (f32[128,256]{1,0:T(8,128)S(1)}, f32[128,256]{1,0:T(8,128)S(1)}, u32[]{:S(2)}, u32[]{:S(2)}) collective-permute-start(f32[128,256]{1,0:T(8,128)S(1)} %pad_maximum_fusion), channel_id=1, source_target_pairs={{0,2},{1,3},{2,4},{3,5},{4,6},{5,7},{6,0},{7,1},{8,10},{9,11},{10,... | collective-permute-start | bytes 393224 | tf_op jit(solution)/shard_map/ppermute | solution.py:293
  47.2 10.2 %collective-permute-start.6 = (f32[128,256]{1,0:T(8,128)S(1)}, f32[128,256]{1,0:T(8,128)S(1)}, u32[]{:S(2)}, u32[]{:S(2)}) collective-permute-start(f32[128,256]{1,0:T(8,128)S(1)} %pad_maximum_fusion.1), channel_id=1, source_target_pairs={{0,6},{1,7},{2,0},{3,1},{4,2},{5,3},{6,4},{7,5},{8,14},{9,15},{10,... | collective-permute-start | bytes 393224 | tf_op jit(solution)/shard_map/ppermute | solution.py:293

commit v3 on v2

--- a/solution.py
+++ b/solution.py
@@ -39,11 +39,13 @@
     return np.stack(tables)
 
 
-def band_tables(half, reach):
+def front_tables(length, reach):
+    half = length // 2
+    mid = half // 2
     bins = bin_order(half)
     table = (np.abs(bins[:, None] - bins[None, :]) <= reach).astype(ml_dtypes.bfloat16)
-    mid = half // 2
-    return np.stack([table[:mid, :mid], table[mid:, :mid], table[:mid, mid:]])
+    band = np.concatenate([table[:mid, :mid], table[mid:, :mid]], axis=1)
+    return np.concatenate([*forward_tables(length), band], axis=0)
 
 
 def inverse_tables(length, lag_count, factor):
@@ -64,6 +66,10 @@
 
 def mm(left, right):
     return jnp.dot(left, right, preferred_element_type=F32)
+
+
+def mm_turned(left, right):
+    return lax.dot_general(left, right, (((1,), (1,)), ((), ())), preferred_element_type=F32)
 
 
 def pack_kernel(sources, records, packed, taken, blocks, chosen, sems_in, sems_out):
@@ -82,6 +88,10 @@
     stores = []
     lane = lax.broadcasted_iota(jnp.int32, (times, LANES), 1)
     pick = jnp.zeros((times, LANES), F32)
+    column = lax.rem(lane, dests)
+    place = jnp.zeros((times, LANES), jnp.int32)
+    for s in range(dests):
+        place = jnp.where(column == s, sources[s] - s * width // LANES * LANES, place)
     for tile in range(tiles):
         loads[tile].wait()
         loaded = [taken[tile, w] for w in range(windows)]
@@ -98,13 +108,10 @@
         )
         store.start()
         stores.append(store)
-        for e in range(per_tile):
-            s = tile * per_tile + e
-            place = sources[s] - tile * LANES
-            for w in range(windows):
-                target = w * dests + s
-                shift = lax.rem(target + LANES - place, LANES)
-                pick = jnp.where(lane == target, pltpu.roll(loaded[w], shift, 1), pick)
+        for w in range(windows):
+            moved = jnp.take_along_axis(loaded[w], place, axis=1)
+            low = w * dests + tile * per_tile
+            pick = jnp.where((lane >= low) & (lane < low + per_tile), moved, pick)
     for d in range(dests):
         chosen[d] = pick
     store = pltpu.make_async_copy(chosen, packed.at[:, times : 2 * times, :], sems_out.at[tiles])
@@ -114,16 +121,10 @@
         store.wait()
 
 
-def position():
-    win = lax.axis_index("win")
-    return lax.div(win, 2), lax.rem(win, 2)
-
-
-def correlate(white_re, white_im, cross_high, cross_low, target, which, core, width):
+def correlate(white_re, white_im, cross_high, cross_low, target, width):
     rows, half = white_re.shape
     lanes = rows // 2
     windows = lanes // width
-    turn = lax.rem(8 - (4 * core if which else 4 - 4 * core), 8)
     rows8 = [
         pl.ds(pl.multiple_of(lanes + w * width + target * 8, 8), 8) for w in range(windows)
     ]
@@ -132,10 +133,9 @@
         span2 = slice(half + tile * LANES, half + (tile + 1) * LANES)
         chan_re = [white_re[w * width : (w + 1) * width, span] for w in range(windows)]
         chan_im = [white_im[w * width : (w + 1) * width, span] for w in range(windows)]
-        from_re = [pltpu.roll(white_re[at, span], turn, 0) for at in rows8]
-        from_im = [pltpu.roll(white_im[at, span], turn, 0) for at in rows8]
-        for i in range(4):
-            out_re = None
+        from_re = [white_re[at, span] for at in rows8]
+        from_im = [white_im[at, span] for at in rows8]
+        for i in range(8):
             for w in range(windows):
                 src_re = jnp.broadcast_to(from_re[w][i : i + 1], (width, LANES))
                 src_im = jnp.broadcast_to(from_im[w][i : i + 1], (width, LANES))
@@ -163,7 +163,7 @@
 
 
 def front_kernel(
-    blocks, tables, band, white_re, white_im, turned
+    blocks, tables, white_re, white_im, turned
 ):
     devices, double, lanes = blocks.shape
     times = double // 2
@@ -182,15 +182,17 @@
         amplitude = (total[:length] + tail[HALF:]) / (2 * HALF + 1)
         normal = data / jnp.maximum(amplitude, AMPLITUDE_FLOOR)
         turned[part * lanes : (part + 1) * lanes, :] = normal.T
+    waves = [tables[n * half : (n + 1) * half, :] for n in range(4)]
+    band = [tables[4 * half :, :quarter], tables[4 * half :, quarter:]]
     first = turned[:, :half]
     second = turned[:, half:]
     for parity in range(2):
         folded = first + second if parity == 0 else first - second
         high, low = split(folded)
         spectrum = (
-            mm(high, tables[2 * parity])
-            + mm(low, tables[2 * parity])
-            + mm(high, tables[2 * parity + 1])
+            mm(high, waves[2 * parity])
+            + mm(low, waves[2 * parity])
+            + mm(high, waves[2 * parity + 1])
         )
         white_re[:, parity * quarter : (parity + 1) * quarter] = spectrum[:, :quarter]
         white_im[:, parity * quarter : (parity + 1) * quarter] = spectrum[:, quarter:]
@@ -200,11 +202,12 @@
     for parity in range(2):
         near = slice(parity * quarter, (parity + 1) * quarter)
         other = slice((1 - parity) * quarter, (2 - parity) * quarter)
+        cross_mm = mm_turned if parity else mm
         smooth = (
             mm(high[:, near], band[0])
             + mm(low[:, near], band[0])
-            + mm(high[:, other], band[1 + parity])
-            + mm(low[:, other], band[1 + parity])
+            + cross_mm(high[:, other], band[1])
+            + cross_mm(low[:, other], band[1])
         )
         gain = 1.0 / (smooth / (2 * (length // 32) + 1) + WHITE_EPSILON)
         white_re[:, near] = re[:, near] * gain
@@ -212,13 +215,22 @@
 
 
 def stack_kernel(slots, white_re, white_im, tables, *refs):
-    send, keep, cross_high, cross_low = refs[-4:]
-    z_hi, core = position()
+    send, keep, cross_high, cross_low, both = refs[-5:]
+    win = lax.axis_index("win")
+    z_hi, core = lax.div(win, 2), lax.rem(win, 2)
     for n, slot in enumerate(slots):
         target = lax.rem(z_hi + slot, 4)
-        for which in range(2):
-            correlate(white_re, white_im, cross_high, cross_low, target, which, core, 32)
-            (keep if which else send)[n] = invert(cross_high, cross_low, tables)
+        correlate(white_re, white_im, cross_high.at[n], cross_low.at[n], target, 32)
+        result = invert(cross_high.at[n], cross_low.at[n], tables)
+        both[n] = result.reshape(both.shape[1:])
+    for n in range(len(slots)):
+        keep[n] = both[n, core]
+        send[n] = both[n, 1 - core]
+
+
+def join_kernel(keep_right, other_right, keep_left, other_left, right, left):
+    right[...] = keep_right[0] + other_right[0]
+    left[...] = keep_left[0] + other_left[0]
 
 
 def local(records, sources):
@@ -246,25 +258,24 @@
             pltpu.SemaphoreType.DMA((tiles,)),
             pltpu.SemaphoreType.DMA((tiles + 1,)),
         ],
+        compiler_params=pltpu.CompilerParams(vmem_limit_bytes=60 << 20),
         name="pack",
     )(sources, records)
     blocks = lax.all_to_all(packed, "chan", 0, 0, tiled=True)
 
-    forward = jnp.asarray(forward_tables(length))
-    band = jnp.asarray(band_tables(half, length // 32))
+    forward = jnp.asarray(front_tables(length, length // 32))
     inverse = jnp.asarray(inverse_tables(length, lag_count, factor))
     rows = 2 * LANES
     shape = jax.ShapeDtypeStruct
     white_re, white_im = pl.pallas_call(
         front_kernel,
         out_shape=(shape((rows, half), F32), shape((rows, half), F32)),
-        in_specs=[vmem] * 3,
+        in_specs=[vmem] * 2,
         out_specs=(vmem, vmem),
         scratch_shapes=[pltpu.VMEM((rows, length), F32)],
         compiler_params=pltpu.CompilerParams(vmem_limit_bytes=24 << 20),
-        cost_estimate=pl.CostEstimate(flops=2 << 30, bytes_accessed=10 << 20, transcendentals=0),
         name="front",
-    )(blocks, forward, band)
+    )(blocks, forward)
 
     def stack(slots, after=None, handed=None):
         part = shape((len(slots), LANES, lag_count), F32)
@@ -280,12 +291,14 @@
             out_shape=outs,
             in_specs=[vmem] * (3 + len(extra)),
             out_specs=[vmem] * len(outs),
-            scratch_shapes=[pltpu.VMEM((LANES, length), BF16), pltpu.VMEM((LANES, length), BF16)],
+            scratch_shapes=[
+                pltpu.VMEM((len(slots), 2 * LANES, length), BF16),
+                pltpu.VMEM((len(slots), 2 * LANES, length), BF16),
+                pltpu.VMEM((len(slots), 2, LANES, lag_count), F32),
+            ],
             input_output_aliases=aliases,
             compiler_params=pltpu.CompilerParams(vmem_limit_bytes=16 << 20),
-            cost_estimate=pl.CostEstimate(
-                flops=len(slots) << 30, bytes_accessed=len(slots) << 22, transcendentals=0
-            ),
+            cost_estimate=pl.CostEstimate(flops=1, bytes_accessed=1, transcendentals=0),
             name="stack",
         )(white_re, white_im, inverse, *extra)
 
@@ -295,18 +308,23 @@
     def across(value):
         return lax.ppermute(value, "win", [(i, i ^ 1) for i in range(8)])
 
-    mid = LANES // 2
     send_far, keep_far = stack((2,))
     keep_far, send_right, keep_right = stack((1,), handed=keep_far)
     far = keep_far[0] + across(send_far)[0]
-    from_left = shifted(far[:mid], 2)
-    from_right = shifted(far[mid:], -2)
-    keep_right, send, keep = stack((3, 0), after=far, handed=keep_right)
-    pair = keep + across(send)
-    right = keep_right[0] + across(send_right)[0]
-    right = jnp.concatenate([right[:mid] + from_left, right[mid:]], axis=0)
-    left = jnp.concatenate([pair[0, :mid], pair[0, mid:] + from_right], axis=0)
-    result = pair[1] + shifted(right, 2) + shifted(left, -2)
+    from_far = shifted(far, 4)
+    send_left, keep_left = stack((3,), after=far)
+    keep_left, send, keep = stack((0,), handed=keep_left)
+    right, left = pl.pallas_call(
+        join_kernel,
+        out_shape=[shape((LANES, lag_count), F32)] * 2,
+        in_specs=[vmem] * 4,
+        out_specs=[vmem] * 2,
+        compiler_params=pltpu.CompilerParams(vmem_limit_bytes=4 << 20),
+        name="join",
+    )(keep_right, across(send_right), keep_left, across(send_left))
+    from_left = shifted(right, 2)
+    from_right = shifted(left, -2)
+    result = (keep[0] + across(send)[0] + from_far) + (from_left + from_right)
     return jnp.transpose(result.reshape(4, 32, lag_count), (0, 2, 1))
 
 

time: 58.4 us -> 58.4 us (level)
  starting transfers between devices: 12.2 us -> 13.1 us
  waiting for transfers between devices: 7.97 us -> 7.2 us
    ppermute x4 -> x3, waiting for transfers between devices: 7.96 us -> 7.19 us  [shifted(): return lax.ppermute(value, 'win', [(i, (i + shift) % 8) for i in range(8)])]
    ppermute x4 -> x3, starting transfers between devices: 9.02 us -> 9.68 us  [shifted(): return lax.ppermute(value, 'win', [(i, (i + shift) % 8) for i in range(8)])]
    pallas_call x3 -> x4, Pallas kernels: 4.96 us -> 5.29 us  [stack(): pl.pallas_call(functools.partial(stack_kernel, slots), out_shape=outs, in...]
    ppermute x3 -> x4, starting transfers between devices: 3.2 us -> 3.37 us  [across(): return lax.ppermute(value, 'win', [(i, i ^ 1) for i in range(8)])]
  transfers between devices with their start and end apart: 7 -> 7, of which waited for: 3 -> 2; matrix products, arithmetic and copies ran while one was open for 0% -> 0% of each run, Pallas kernels for 6% -> 7%
where the time goes in v3:
time: 58.4 us; the launch traced here: 58.1 us
  blocking collectives  26 us (45%)
  starting transfers between devices  13.1 us (22%)
  Pallas kernels  11.1 us (19%)
  waiting for transfers between devices  7.2 us (12%)
  other arithmetic  0.72 us (1%)
    all_to_all x1, blocking collectives, local(): blocks = lax.all_to_all(packed, 'chan', 0, 0, tiled=True)  26 us
    ppermute x3, starting transfers between devices, shifted(): return lax.ppermute(value, 'win', [(i, (i + shift) % 8) for i in range(8)])  9.68 us
    ppermute x3, waiting for transfers between devices, shifted(): return lax.ppermute(value, 'win', [(i, (i + shift) % 8) for i in range(8)])  7.19 us
    pallas_call x4, Pallas kernels, stack(): pl.pallas_call(functools.partial(stack_kernel, slots), out_shape=outs, in...  5.29 us
    pallas_call x1, Pallas kernels, local(): pl.pallas_call(pack_kernel, out_shape=jax.ShapeDtypeStruct((chan_count, 2...  3.76 us
    ppermute x4, starting transfers between devices, across(): return lax.ppermute(value, 'win', [(i, i ^ 1) for i in range(8)])  3.37 us
    pallas_call x1, Pallas kernels, local(): pl.pallas_call(front_kernel, out_shape=(shape((rows, half), F32), shape((...  1.98 us
  transfers between devices with their start and end apart: 7, of which 2 were waited for; matrix products, arithmetic and copies ran while one was open for 0% of the time, Pallas kernels for 7%

profile of v3, /device:TPU:1, one launch (start us, length us, event | category | flops | bytes accessed | tf_op | source)
XLA Modules:
  0.0 58.1 jit_solution(4176610610285299676)
XLA Ops:
  0.0 3.8 %pack.1 = f32[32,64,128]{2,1,0:T(8,128)} custom-call(s32[32]{0:T(128)} %sources.1, f32[4,32,1024]{2,1,0:T(8,128)} %records.1), custom_call_target="tpu_custom_call" | custom-call | tf_op jit(solution)/shard_map/pack/pallas_call | solution.py:249
  3.8 0.0 copy-start
  3.8 26.0 %all_to_all.5.blocks = f32[32,64,128]{2,1,0:T(8,128)S(1)} all-to-all(f32[32,64,128]{2,1,0:T(8,128)} %pack.1), channel_id=1, replica_groups=mesh['chan'=32,'win'=8] {'chan'}, dimensions={0} | all-to-all | bytes 2097152 | tf_op jit(solution)/shard_map/all_to_all | solution.py:264
  29.8 0.0 copy-done.1
  29.8 2.0 %front.1 = (f32[256,512]{1,0:T(8,128)S(1)}, f32[256,512]{1,0:T(8,128)S(1)}) custom-call(f32[32,64,128]{2,1,0:T(8,128)S(1)} %all_to_all.5.blocks, bf16[2304,512]{1,0:T(8,128)(2,1)S(1)} %copy-done.1), custom_call_target="tpu_custom_call" | custom-call | tf_op jit(solution)/shard_map/front/pallas_call | solution.py:270
  31.8 1.3 %stack.4 = (f32[1,128,256]{2,1,0:T(8,128)S(1)}, f32[1,128,256]{2,1,0:T(8,128)S(1)}) custom-call(f32[256,512]{1,0:T(8,128)S(1)} %get-tuple-element.19.white_re, f32[256,512]{1,0:T(8,128)S(1)} %get-tuple-element.20.white_im, bf16[2,512,512]{2,1,0:T(8,128)(2,1)S(1)} %copy-done), custom_call_target="tpu_custom_call" | custom-call | flops 1 | bytes 1 | tf_op jit(solution)/shard_map/stack/pallas_call | solution.py:289
  33.1 2.2 %collective-permute-start = (f32[1,128,256]{2,1,0:T(8,128)S(1)}, f32[1,128,256]{2,1,0:T(8,128)S(1)}, u32[]{:S(2)}, u32[]{:S(2)}) collective-permute-start(f32[1,128,256]{2,1,0:T(8,128)S(1)} %get-tuple-element.23), channel_id=1, source_target_pairs={{0,1},{1,0},{2,3},{3,2},{4,5},{5,4},{6,7},{7,6},{8,9},{9,8},{10,11... | collective-permute-start | bytes 393224 | tf_op jit(solution)/shard_map/ppermute | solution.py:309
  35.4 1.3 %stack.5 = (f32[1,128,256]{2,1,0:T(8,128)S(1)}, f32[1,128,256]{2,1,0:T(8,128)S(1)}, f32[1,128,256]{2,1,0:T(8,128)S(1)}) custom-call(f32[256,512]{1,0:T(8,128)S(1)} %get-tuple-element.19.white_re, f32[256,512]{1,0:T(8,128)S(1)} %get-tuple-element.20.white_im, bf16[2,512,512]{2,1,0:T(8,128)(2,1)S(1)} %copy-done, ...), custom_call_target="tpu_custom_call", output_to_operand_aliasing={{0}: (3, {})} | custom-call | flops 1 | bytes 1 | tf_op jit(solution)/shard_map/stack/pallas_call | solution.py:289
  36.7 0.0 collective-permute-done
  36.8 0.1 collective-permute-start.3
  36.9 1.3 %stack.6 = (f32[1,128,256]{2,1,0:T(8,128)S(1)}, f32[1,128,256]{2,1,0:T(8,128)S(1)}) custom-call(f32[256,512]{1,0:T(8,128)S(1)} %get-tuple-element.19.white_re, f32[256,512]{1,0:T(8,128)S(1)} %get-tuple-element.20.white_im, bf16[2,512,512]{2,1,0:T(8,128)(2,1)S(1)} %copy-done, f32[128,256]{1,0:T(8,128)S(1)} %add_bitcast_fusion.refs_0_), custom_call_target="tpu_custom_call" | custom-call | flops 1 | bytes 1 | tf_op jit(solution)/shard_map/stack/pallas_call | solution.py:289
  38.2 0.6 collective-permute-start.4
  38.8 6.0 %collective-permute-start.2 = (f32[128,256]{1,0:T(8,128)S(1)}, f32[128,256]{1,0:T(8,128)S(1)}, u32[]{:S(2)}, u32[]{:S(2)}) collective-permute-start(f32[128,256]{1,0:T(8,128)S(1)} %add_bitcast_fusion.refs_0_), channel_id=1, source_target_pairs={{0,4},{1,5},{2,6},{3,7},{4,0},{5,1},{6,2},{7,3},{8,12},{9,13},{10,... | collective-permute-start | bytes 393224 | tf_op jit(solution)/shard_map/ppermute | solution.py:306
  44.8 1.3 %stack.7 = (f32[1,128,256]{2,1,0:T(8,128)S(1)}, f32[1,128,256]{2,1,0:T(8,128)S(1)}, f32[1,128,256]{2,1,0:T(8,128)S(1)}) custom-call(f32[256,512]{1,0:T(8,128)S(1)} %get-tuple-element.19.white_re, f32[256,512]{1,0:T(8,128)S(1)} %get-tuple-element.20.white_im, bf16[2,512,512]{2,1,0:T(8,128)(2,1)S(1)} %copy-done, ...), custom_call_target="tpu_custom_call", output_to_operand_aliasing={{0}: (3, {})} | custom-call | flops 1 | bytes 1 | tf_op jit(solution)/shard_map/stack/pallas_call | solution.py:289
  46.1 0.4 collective-permute-start.1
  46.6 0.0 collective-permute-done.3.other_right
  46.6 0.0 collective-permute-done.4.other_left
  46.6 1.3 %collective-permute-start.5 = (f32[128,256]{1,0:T(8,128)S(1)}, f32[128,256]{1,0:T(8,128)S(1)}, u32[]{:S(2)}, u32[]{:S(2)}) collective-permute-start(f32[128,256]{1,0:T(8,128)S(1)} %get-tuple-element.31), channel_id=1, source_target_pairs={{0,2},{1,3},{2,4},{3,5},{4,6},{5,7},{6,0},{7,1},{8,10},{9,11},{10,... | collective-permute-start | bytes 393224 | tf_op jit(solution)/shard_map/ppermute | solution.py:306
  47.9 2.4 %collective-permute-start.6 = (f32[128,256]{1,0:T(8,128)S(1)}, f32[128,256]{1,0:T(8,128)S(1)}, u32[]{:S(2)}, u32[]{:S(2)}) collective-permute-start(f32[128,256]{1,0:T(8,128)S(1)} %get-tuple-element.32), channel_id=1, source_target_pairs={{0,6},{1,7},{2,0},{3,1},{4,2},{5,3},{6,4},{7,5},{8,14},{9,15},{10,... | collective-permute-start | bytes 393224 | tf_op jit(solution)/shard_map/ppermute | solution.py:306
  50.3 0.0 collective-permute-done.2
  50.3 0.0 collective-permute-done.1
  50.3 5.0 %collective-permute-done.5 = f32[128,256]{1,0:T(8,128)S(1)} collective-permute-done((f32[128,256]{1,0:T(8,128)S(1)}, f32[128,256]{1,0:T(8,128)S(1)}, u32[]{:S(2)}, u32[]{:S(2)}) %collective-permute-start.5) | collective-permute-done | bytes 131104 | tf_op jit(solution)/shard_map/ppermute | solution.py:306
  55.3 2.2 %collective-permute-done.6 = f32[128,256]{1,0:T(8,128)S(1)} collective-permute-done((f32[128,256]{1,0:T(8,128)S(1)}, f32[128,256]{1,0:T(8,128)S(1)}, u32[]{:S(2)}, u32[]{:S(2)}) %collective-permute-start.6) | collective-permute-done | bytes 131104 | tf_op jit(solution)/shard_map/ppermute | solution.py:306
  57.4 0.7 %fusion = f32[128,256]{1,0:T(8,128)} fusion(f32[128,256]{1,0:T(8,128)S(1)} %collective-permute-done.2, f32[128,256]{1,0:T(8,128)S(1)} %collective-permute-done.5, f32[128,256]{1,0:T(8,128)S(1)} %collective-permute-done.6, f32[1,128,256]{2,1,0:T(8,128)S(1)} %get-tuple-element.25, f32[1,128,256]{2,1,0:T(8,128)S(1)} %collective-permute-done.1), kind=kLoop, calls=%fused_computation.1 | loop fusion | flops 131072 | bytes 786432 | tf_op jit(solution)/shard_map/add | solution.py:327
  (4 shorter events, 0.1 us)
Async XLA Ops:
  0.0 29.8 %copy-start.1 = (bf16[2304,512]{1,0:T(8,128)(2,1)S(1)}, bf16[2304,512]{1,0:T(8,128)(2,1)}, u32[]{:S(2)}) copy-start(bf16[2304,512]{1,0:T(8,128)(2,1)} %constant.4.clone.tables) | copy-start | bytes 7077892
  3.8 28.0 %copy-start = (bf16[2,512,512]{2,1,0:T(8,128)(2,1)S(1)}, bf16[2,512,512]{2,1,0:T(8,128)(2,1)}, u32[]{:S(2)}) copy-start(bf16[2,512,512]{2,1,0:T(8,128)(2,1)} %constant.5.clone.tables) | copy-start | bytes 3145732
  33.1 3.6 %collective-permute-start = (f32[1,128,256]{2,1,0:T(8,128)S(1)}, f32[1,128,256]{2,1,0:T(8,128)S(1)}, u32[]{:S(2)}, u32[]{:S(2)}) collective-permute-start(f32[1,128,256]{2,1,0:T(8,128)S(1)} %get-tuple-element.23), channel_id=1, source_target_pairs={{0,1},{1,0},{2,3},{3,2},{4,5},{5,4},{6,7},{7,6},{8,9},{9,8},{10,11... | collective-permute-start | bytes 393224 | tf_op jit(solution)/shard_map/ppermute | solution.py:309
  36.8 9.8 %collective-permute-start.3 = (f32[1,128,256]{2,1,0:T(8,128)S(1)}, f32[1,128,256]{2,1,0:T(8,128)S(1)}, u32[]{:S(2)}, u32[]{:S(2)}) collective-permute-start(f32[1,128,256]{2,1,0:T(8,128)S(1)} %get-tuple-element.28), channel_id=1, source_target_pairs={{0,1},{1,0},{2,3},{3,2},{4,5},{5,4},{6,7},{7,6},{8,9},{9,8},{10,11... | collective-permute-start | bytes 393224 | tf_op jit(solution)/shard_map/ppermute | solution.py:309
  38.2 8.4 %collective-permute-start.4 = (f32[1,128,256]{2,1,0:T(8,128)S(1)}, f32[1,128,256]{2,1,0:T(8,128)S(1)}, u32[]{:S(2)}, u32[]{:S(2)}) collective-permute-start(f32[1,128,256]{2,1,0:T(8,128)S(1)} %get-tuple-element.30), channel_id=1, source_target_pairs={{0,1},{1,0},{2,3},{3,2},{4,5},{5,4},{6,7},{7,6},{8,9},{9,8},{10,11... | collective-permute-start | bytes 393224 | tf_op jit(solution)/shard_map/ppermute | solution.py:309
  38.8 11.5 %collective-permute-start.2 = (f32[128,256]{1,0:T(8,128)S(1)}, f32[128,256]{1,0:T(8,128)S(1)}, u32[]{:S(2)}, u32[]{:S(2)}) collective-permute-start(f32[128,256]{1,0:T(8,128)S(1)} %add_bitcast_fusion.refs_0_), channel_id=1, source_target_pairs={{0,4},{1,5},{2,6},{3,7},{4,0},{5,1},{6,2},{7,3},{8,12},{9,13},{10,... | collective-permute-start | bytes 393224 | tf_op jit(solution)/shard_map/ppermute | solution.py:306
  46.1 4.1 %collective-permute-start.1 = (f32[1,128,256]{2,1,0:T(8,128)S(1)}, f32[1,128,256]{2,1,0:T(8,128)S(1)}, u32[]{:S(2)}, u32[]{:S(2)}) collective-permute-start(f32[1,128,256]{2,1,0:T(8,128)S(1)} %get-tuple-element.26), channel_id=1, source_target_pairs={{0,1},{1,0},{2,3},{3,2},{4,5},{5,4},{6,7},{7,6},{8,9},{9,8},{10,11... | collective-permute-start | bytes 393224 | tf_op jit(solution)/shard_map/ppermute | solution.py:309
  46.6 8.7 %collective-permute-start.5 = (f32[128,256]{1,0:T(8,128)S(1)}, f32[128,256]{1,0:T(8,128)S(1)}, u32[]{:S(2)}, u32[]{:S(2)}) collective-permute-start(f32[128,256]{1,0:T(8,128)S(1)} %get-tuple-element.31), channel_id=1, source_target_pairs={{0,2},{1,3},{2,4},{3,5},{4,6},{5,7},{6,0},{7,1},{8,10},{9,11},{10,... | collective-permute-start | bytes 393224 | tf_op jit(solution)/shard_map/ppermute | solution.py:306
  47.9 9.6 %collective-permute-start.6 = (f32[128,256]{1,0:T(8,128)S(1)}, f32[128,256]{1,0:T(8,128)S(1)}, u32[]{:S(2)}, u32[]{:S(2)}) collective-permute-start(f32[128,256]{1,0:T(8,128)S(1)} %get-tuple-element.32), channel_id=1, source_target_pairs={{0,6},{1,7},{2,0},{3,1},{4,2},{5,3},{6,4},{7,5},{8,14},{9,15},{10,... | collective-permute-start | bytes 393224 | tf_op jit(solution)/shard_map/ppermute | solution.py:306

commit v4 on v3

--- a/solution.py
+++ b/solution.py
@@ -72,53 +72,32 @@
     return lax.dot_general(left, right, (((1,), (1,)), ((), ())), preferred_element_type=F32)
 
 
-def pack_kernel(sources, records, packed, taken, blocks, chosen, sems_in, sems_out):
+def pack_kernel(sources, records, packed):
     windows, times, channels = records.shape
     dests = packed.shape[0]
     width = channels // dests
     per_tile = LANES // width
-    tiles = channels // LANES
-    loads = []
-    for tile in range(tiles):
-        load = pltpu.make_async_copy(
-            records.at[:, :, tile * LANES : (tile + 1) * LANES], taken.at[tile], sems_in.at[tile]
-        )
-        load.start()
-        loads.append(load)
-    stores = []
     lane = lax.broadcasted_iota(jnp.int32, (times, LANES), 1)
-    pick = jnp.zeros((times, LANES), F32)
     column = lax.rem(lane, dests)
     place = jnp.zeros((times, LANES), jnp.int32)
     for s in range(dests):
         place = jnp.where(column == s, sources[s] - s * width // LANES * LANES, place)
-    for tile in range(tiles):
-        loads[tile].wait()
-        loaded = [taken[tile, w] for w in range(windows)]
+    pick = jnp.zeros((times, LANES), F32)
+    for tile in range(channels // LANES):
+        loaded = [records[w, :, tile * LANES : (tile + 1) * LANES] for w in range(windows)]
         for e in range(per_tile):
             block = None
             for w in range(windows):
                 shift = (w - e) * width % LANES
                 moved = pltpu.roll(loaded[w], shift, 1) if shift else loaded[w]
                 block = moved if block is None else jnp.where(lane >= w * width, moved, block)
-            blocks[tile * per_tile + e] = block
-        span = pl.ds(tile * per_tile, per_tile)
-        store = pltpu.make_async_copy(
-            blocks.at[span], packed.at[span, 0:times, :], sems_out.at[tile]
-        )
-        store.start()
-        stores.append(store)
+            packed[tile * per_tile + e, 0:times, :] = block
         for w in range(windows):
             moved = jnp.take_along_axis(loaded[w], place, axis=1)
             low = w * dests + tile * per_tile
             pick = jnp.where((lane >= low) & (lane < low + per_tile), moved, pick)
     for d in range(dests):
-        chosen[d] = pick
-    store = pltpu.make_async_copy(chosen, packed.at[:, times : 2 * times, :], sems_out.at[tiles])
-    store.start()
-    stores.append(store)
-    for store in stores:
-        store.wait()
+        packed[d, times : 2 * times, :] = pick
 
 
 def correlate(white_re, white_im, cross_high, cross_low, target, width):
@@ -135,17 +114,20 @@
         chan_im = [white_im[w * width : (w + 1) * width, span] for w in range(windows)]
         from_re = [white_re[at, span] for at in rows8]
         from_im = [white_im[at, span] for at in rows8]
+        chan_sum = [a + b for a, b in zip(chan_re, chan_im)]
+        from_sum = [a + b for a, b in zip(from_re, from_im)]
+        from_less = [a - b for a, b in zip(from_re, from_im)]
         for i in range(8):
             for w in range(windows):
-                src_re = jnp.broadcast_to(from_re[w][i : i + 1], (width, LANES))
-                src_im = jnp.broadcast_to(from_im[w][i : i + 1], (width, LANES))
-                add_re = src_re * chan_re[w] + src_im * chan_im[w]
-                add_im = src_re * chan_im[w] - src_im * chan_re[w]
-                out_re = add_re if w == 0 else out_re + add_re
-                out_im = add_im if w == 0 else out_im + add_im
+                one = jnp.broadcast_to(from_re[w][i : i + 1], (width, LANES)) * chan_sum[w]
+                two = jnp.broadcast_to(from_less[w][i : i + 1], (width, LANES)) * chan_im[w]
+                three = jnp.broadcast_to(from_sum[w][i : i + 1], (width, LANES)) * chan_re[w]
+                ones = one if w == 0 else ones + one
+                twos = two if w == 0 else twos + two
+                threes = three if w == 0 else threes + three
             at = slice(i * width, (i + 1) * width)
-            cross_high[at, span], cross_low[at, span] = split(out_re)
-            cross_high[at, span2], cross_low[at, span2] = split(out_im)
+            cross_high[at, span], cross_low[at, span] = split(ones - twos)
+            cross_high[at, span2], cross_low[at, span2] = split(ones - threes)
 
 
 def invert(cross_high, cross_low, tables):
@@ -214,23 +196,30 @@
         white_im[:, near] = im[:, near] * gain
 
 
-def stack_kernel(slots, white_re, white_im, tables, *refs):
-    send, keep, cross_high, cross_low, both = refs[-5:]
+def stack_kernel(kind, white_re, white_im, tables, *refs):
+    cross_high, cross_low, both = refs[-3:]
     win = lax.axis_index("win")
     z_hi, core = lax.div(win, 2), lax.rem(win, 2)
-    for n, slot in enumerate(slots):
-        target = lax.rem(z_hi + slot, 4)
-        correlate(white_re, white_im, cross_high.at[n], cross_low.at[n], target, 32)
-        result = invert(cross_high.at[n], cross_low.at[n], tables)
-        both[n] = result.reshape(both.shape[1:])
-    for n in range(len(slots)):
-        keep[n] = both[n, core]
-        send[n] = both[n, 1 - core]
-
-
-def join_kernel(keep_right, other_right, keep_left, other_left, right, left):
-    right[...] = keep_right[0] + other_right[0]
-    left[...] = keep_left[0] + other_left[0]
+    step = {"far": 2, "ahead": 1 + 2 * core, "behind": 3 - 2 * core, "here": 0}[kind]
+    correlate(white_re, white_im, cross_high, cross_low, lax.rem(z_hi + step, 4), 32)
+    both[...] = invert(cross_high, cross_low, tables).reshape(both.shape)
+    if kind == "behind":
+        refs[-4][0] = both[1 - core]
+        refs[-4][1] = both[core]
+    else:
+        refs[-5][...] = both[core]
+        refs[-4][...] = both[1 - core]
+
+
+def add_kernel(*refs):
+    half = len(refs) // 3
+    for left, right, out in zip(refs[:half], refs[half : 2 * half], refs[2 * half :]):
+        out[...] = left[...] + right[...]
+
+
+def join_kernel(own, other, received, own_sum, other_sum):
+    own_sum[...] = own[...] + received[0]
+    other_sum[...] = other[...] + received[1]
 
 
 def local(records, sources):
@@ -249,16 +238,9 @@
     packed = pl.pallas_call(
         pack_kernel,
         out_shape=jax.ShapeDtypeStruct((chan_count, 2 * times, LANES), F32),
-        in_specs=[smem, hbm],
-        out_specs=hbm,
-        scratch_shapes=[
-            pltpu.VMEM((tiles, windows, times, LANES), F32),
-            pltpu.VMEM((chan_count, times, LANES), F32),
-            pltpu.VMEM((chan_count, times, LANES), F32),
-            pltpu.SemaphoreType.DMA((tiles,)),
-            pltpu.SemaphoreType.DMA((tiles + 1,)),
-        ],
-        compiler_params=pltpu.CompilerParams(vmem_limit_bytes=60 << 20),
+        in_specs=[smem, vmem],
+        out_specs=vmem,
+        compiler_params=pltpu.CompilerParams(vmem_limit_bytes=4 << 20),
         name="pack",
     )(sources, records)
     blocks = lax.all_to_all(packed, "chan", 0, 0, tiled=True)
@@ -277,54 +259,61 @@
         name="front",
     )(blocks, forward)
 
-    def stack(slots, after=None, handed=None):
-        part = shape((len(slots), LANES, lag_count), F32)
+    piece = shape((LANES, lag_count), F32)
+
+    def stack(kind, after=None, handed=None):
         extra = [] if after is None else [after]
-        outs = [part, part]
+        outs = [shape((2, LANES, lag_count), F32)] if kind == "behind" else [piece, piece]
         aliases = {}
         if handed is not None:
             aliases = {3 + len(extra): 0}
             extra.append(handed)
             outs.insert(0, shape(handed.shape, F32))
         return pl.pallas_call(
-            functools.partial(stack_kernel, slots),
+            functools.partial(stack_kernel, kind),
             out_shape=outs,
             in_specs=[vmem] * (3 + len(extra)),
             out_specs=[vmem] * len(outs),
             scratch_shapes=[
-                pltpu.VMEM((len(slots), 2 * LANES, length), BF16),
-                pltpu.VMEM((len(slots), 2 * LANES, length), BF16),
-                pltpu.VMEM((len(slots), 2, LANES, lag_count), F32),
+                pltpu.VMEM((2 * LANES, length), BF16),
+                pltpu.VMEM((2 * LANES, length), BF16),
+                pltpu.VMEM((2, LANES, lag_count), F32),
             ],
             input_output_aliases=aliases,
             compiler_params=pltpu.CompilerParams(vmem_limit_bytes=16 << 20),
-            cost_estimate=pl.CostEstimate(flops=1, bytes_accessed=1, transcendentals=0),
-            name="stack",
+            cost_estimate=pl.CostEstimate(flops=1 << 32, bytes_accessed=1 << 24, transcendentals=0),
+            name="stack_" + kind,
         )(white_re, white_im, inverse, *extra)
 
-    def shifted(value, shift):
-        return lax.ppermute(value, "win", [(i, (i + shift) % 8) for i in range(8)])
+    def small(kernel, outs, name, *operands):
+        return pl.pallas_call(
+            kernel,
+            out_shape=[piece] * outs,
+            in_specs=[vmem] * len(operands),
+            out_specs=[vmem] * outs,
+            compiler_params=pltpu.CompilerParams(vmem_limit_bytes=4 << 20),
+            name=name,
+        )(*operands)
+
+    def onward(value):
+        pairs = [(i, (i + (2 if i % 2 == 0 else -2)) % 8) for i in range(8)]
+        return lax.ppermute(value, "win", pairs)
 
     def across(value):
         return lax.ppermute(value, "win", [(i, i ^ 1) for i in range(8)])
 
-    send_far, keep_far = stack((2,))
-    keep_far, send_right, keep_right = stack((1,), handed=keep_far)
-    far = keep_far[0] + across(send_far)[0]
-    from_far = shifted(far, 4)
-    send_left, keep_left = stack((3,), after=far)
-    keep_left, send, keep = stack((0,), handed=keep_left)
-    right, left = pl.pallas_call(
-        join_kernel,
-        out_shape=[shape((LANES, lag_count), F32)] * 2,
-        in_specs=[vmem] * 4,
-        out_specs=[vmem] * 2,
-        compiler_params=pltpu.CompilerParams(vmem_limit_bytes=4 << 20),
-        name="join",
-    )(keep_right, across(send_right), keep_left, across(send_left))
-    from_left = shifted(right, 2)
-    from_right = shifted(left, -2)
-    result = (keep[0] + across(send)[0] + from_far) + (from_left + from_right)
+    keep_far, send_far = stack("far")
+    keep_far, behind = stack("behind", handed=keep_far)
+    (far,) = small(add_kernel, 1, "add_far", keep_far, across(send_far))
+    passing = onward(far)
+    own, other = stack("ahead", after=far)
+    own, other = small(join_kernel, 2, "join", own, other, across(behind))
+    early = onward(other)
+    own, here_own, here_other = stack("here", after=other, handed=own)
+    (own,) = small(add_kernel, 1, "add_passing", own, passing)
+    late = onward(own)
+    turned = across(here_other + early)
+    result = (here_own + late) + turned
     return jnp.transpose(result.reshape(4, 32, lag_count), (0, 2, 1))
 
 

time: 58.4 us -> 53.3 us (0.913)
  waiting for transfers between devices: 7.2 us -> 3.07 us
  Pallas kernels: 11.1 us -> 8.21 us
  local copies, waits for them, and re-layouts: 0.01 us -> 1.86 us
    ppermute x3, waiting for transfers between devices: 7.19 us -> 3.07 us  [onward(): return lax.ppermute(value, 'win', pairs)]
    pallas_call x1, Pallas kernels: 3.76 us -> 1.19 us  [local(): pl.pallas_call(pack_kernel, out_shape=jax.ShapeDtypeStruct((chan_count, 2...]
    unnamed x4 -> x8, local copies, waits for them, and re-layouts: 0.01 us -> 1.86 us
    ppermute x3, starting transfers between devices: 9.68 us -> 10.9 us  [onward(): return lax.ppermute(value, 'win', pairs)]
    ppermute x4 -> x3, starting transfers between devices: 3.37 us -> 2.53 us  [across(): return lax.ppermute(value, 'win', [(i, i ^ 1) for i in range(8)])]
    pallas_call x5 -> x7, Pallas kernels: 5.32 us -> 5.04 us  [the longest x4 4.97 us: stack(): pl.pallas_call(functools.partial(stack_kernel, kind), out_shape=outs, in_...]
  transfers between devices with their start and end apart: 7 -> 6, of which waited for: 2 -> 1; matrix products, arithmetic and copies ran while one was open for 0% -> 0% of each run, Pallas kernels for 7% -> 7%
where the time goes in v4:
time: 53.3 us; the launch traced here: 53.2 us
  blocking collectives  25.8 us (48%)
  starting transfers between devices  13.4 us (25%)
  Pallas kernels  8.21 us (15%)
  waiting for transfers between devices  3.07 us (6%)
  local copies, waits for them, and re-layouts  1.86 us (3%)
  other arithmetic  0.7 us (1%)
    all_to_all x1, blocking collectives, local(): blocks = lax.all_to_all(packed, 'chan', 0, 0, tiled=True)  25.8 us
    ppermute x3, starting transfers between devices, onward(): return lax.ppermute(value, 'win', pairs)  10.9 us
    pallas_call x4, Pallas kernels, stack(): pl.pallas_call(functools.partial(stack_kernel, kind), out_shape=outs, in_...  4.97 us
    ppermute x3, waiting for transfers between devices, onward(): return lax.ppermute(value, 'win', pairs)  3.07 us
    ppermute x3, starting transfers between devices, across(): return lax.ppermute(value, 'win', [(i, i ^ 1) for i in range(8)])  2.53 us
    pallas_call x1, Pallas kernels, local(): pl.pallas_call(front_kernel, out_shape=(shape((rows, half), F32), shape((...  1.98 us
    unnamed x8, local copies, waits for them, and re-layouts  1.86 us
    pallas_call x1, Pallas kernels, local(): pl.pallas_call(pack_kernel, out_shape=jax.ShapeDtypeStruct((chan_count, 2...  1.19 us
  transfers between devices with their start and end apart: 6, of which 1 were waited for; matrix products, arithmetic and copies ran while one was open for 0% of the time, Pallas kernels for 7%

profile of v4, /device:TPU:1, one launch (start us, length us, event | category | flops | bytes accessed | tf_op | source)
XLA Modules:
  0.0 53.2 jit_solution(14415119219288738646)
XLA Ops:
  0.0 1.2 %copy-done.1 = f32[4,32,1024]{2,1,0:T(8,128)S(1)} copy-done((f32[4,32,1024]{2,1,0:T(8,128)S(1)}, f32[4,32,1024]{2,1,0:T(8,128)}, u32[]{:S(2)}) %copy-start.1) | copy-done | bytes 524312
  1.2 0.7 %copy-done.2 = s32[32]{0:T(128)S(1)} copy-done((s32[32]{0:T(128)S(1)}, s32[32]{0:T(128)}, u32[]{:S(2)}) %copy-start.2) | copy-done | bytes 152
  1.9 1.2 %pack.1 = f32[32,64,128]{2,1,0:T(8,128)S(1)} custom-call(s32[32]{0:T(128)S(1)} %copy-done.2, f32[4,32,1024]{2,1,0:T(8,128)S(1)} %copy-done.1), custom_call_target="tpu_custom_call" | custom-call | tf_op jit(solution)/shard_map/pack/pallas_call | solution.py:238
  3.1 0.0 copy-start.3
  3.1 25.8 %all_to_all.5.blocks = f32[32,64,128]{2,1,0:T(8,128)S(1)} all-to-all(f32[32,64,128]{2,1,0:T(8,128)S(1)} %pack.1), channel_id=1, replica_groups=mesh['chan'=32,'win'=8] {'chan'}, dimensions={0} | all-to-all | bytes 2097152 | tf_op jit(solution)/shard_map/all_to_all | solution.py:246
  28.9 0.0 copy-done
  28.9 2.0 %front.1 = (f32[256,512]{1,0:T(8,128)S(1)}, f32[256,512]{1,0:T(8,128)S(1)}) custom-call(f32[32,64,128]{2,1,0:T(8,128)S(1)} %all_to_all.5.blocks, bf16[2304,512]{1,0:T(8,128)(2,1)S(1)} %copy-done), custom_call_target="tpu_custom_call" | custom-call | tf_op jit(solution)/shard_map/front/pallas_call | solution.py:252
  30.9 1.2 %stack_far.1 = (f32[128,256]{1,0:T(8,128)S(1)}, f32[128,256]{1,0:T(8,128)S(1)}) custom-call(f32[256,512]{1,0:T(8,128)S(1)} %get-tuple-element.18.white_re, f32[256,512]{1,0:T(8,128)S(1)} %get-tuple-element.19.white_im, bf16[2,512,512]{2,1,0:T(8,128)(2,1)S(1)} %copy-done.3), custom_call_target="tpu_custom_call" | custom-call | flops 4294967296 | bytes 16777216 | tf_op jit(solution)/shard_map/stack_far/pallas_call | solution.py:272
  32.1 2.3 %collective-permute-start = (f32[128,256]{1,0:T(8,128)S(1)}, f32[128,256]{1,0:T(8,128)S(1)}, u32[]{:S(2)}, u32[]{:S(2)}) collective-permute-start(f32[128,256]{1,0:T(8,128)S(1)} %get-tuple-element.22), channel_id=1, source_target_pairs={{0,1},{1,0},{2,3},{3,2},{4,5},{5,4},{6,7},{7,6},{8,9},{9,8},{10,11... | collective-permute-start | bytes 393224 | tf_op jit(solution)/shard_map/ppermute | solution.py:303
  34.4 1.2 %stack_behind.1 = (f32[128,256]{1,0:T(8,128)S(1)}, f32[2,128,256]{2,1,0:T(8,128)S(1)}) custom-call(f32[256,512]{1,0:T(8,128)S(1)} %get-tuple-element.18.white_re, f32[256,512]{1,0:T(8,128)S(1)} %get-tuple-element.19.white_im, bf16[2,512,512]{2,1,0:T(8,128)(2,1)S(1)} %copy-done.3, ...), custom_call_target="tpu_custom_call", output_to_operand_aliasing={{0}: (3, {})} | custom-call | flops 4294967296 | bytes 16777216 | tf_op jit(solution)/shard_map/stack_behind/pallas_call | solution.py:272
  35.6 0.1 collective-permute-start.1
  35.7 0.0 collective-permute-done.refs_1_
  35.8 5.2 %collective-permute-start.2 = (f32[128,256]{1,0:T(8,128)S(1)}, f32[128,256]{1,0:T(8,128)S(1)}, u32[]{:S(2)}, u32[]{:S(2)}) collective-permute-start(f32[128,256]{1,0:T(8,128)S(1)} %add_far.1.refs_0_), channel_id=1, source_target_pairs={{0,2},{1,7},{2,4},{3,1},{4,6},{5,3},{6,0},{7,5},{8,10},{9,15},{10,... | collective-permute-start | bytes 393224 | tf_op jit(solution)/shard_map/ppermute | solution.py:300
  41.0 1.2 %stack_ahead.1 = (f32[128,256]{1,0:T(8,128)S(1)}, f32[128,256]{1,0:T(8,128)S(1)}) custom-call(f32[256,512]{1,0:T(8,128)S(1)} %get-tuple-element.18.white_re, f32[256,512]{1,0:T(8,128)S(1)} %get-tuple-element.19.white_im, bf16[2,512,512]{2,1,0:T(8,128)(2,1)S(1)} %copy-done.3, f32[128,256]{1,0:T(8,128)S(1)} %add_far.1.refs_0_), custom_call_target="tpu_custom_call" | custom-call | flops 4294967296 | bytes 16777216 | tf_op jit(solution)/shard_map/stack_ahead/pallas_call | solution.py:272
  42.2 0.0 collective-permute-done.1.received
  42.3 1.2 %collective-permute-start.4 = (f32[128,256]{1,0:T(8,128)S(1)}, f32[128,256]{1,0:T(8,128)S(1)}, u32[]{:S(2)}, u32[]{:S(2)}) collective-permute-start(f32[128,256]{1,0:T(8,128)S(1)} %get-tuple-element.26.refs_0_), channel_id=1, source_target_pairs={{0,2},{1,7},{2,4},{3,1},{4,6},{5,3},{6,0},{7,5},{8,10},{9,15},{10,... | collective-permute-start | bytes 393224 | tf_op jit(solution)/shard_map/ppermute | solution.py:300
  43.5 1.2 %stack_here.1 = (f32[128,256]{1,0:T(8,128)S(1)}, f32[128,256]{1,0:T(8,128)S(1)}, f32[128,256]{1,0:T(8,128)S(1)}) custom-call(f32[256,512]{1,0:T(8,128)S(1)} %get-tuple-element.18.white_re, f32[256,512]{1,0:T(8,128)S(1)} %get-tuple-element.19.white_im, bf16[2,512,512]{2,1,0:T(8,128)(2,1)S(1)} %copy-done.3, ...), custom_call_target="tpu_custom_call", output_to_operand_aliasing={{0}: (4, {})} | custom-call | flops 4294967296 | bytes 16777216 | tf_op jit(solution)/shard_map/stack_here/pallas_call | solution.py:272
  44.8 0.0 collective-permute-done.2.refs_1_
  44.8 4.4 %collective-permute-start.3 = (f32[128,256]{1,0:T(8,128)S(1)}, f32[128,256]{1,0:T(8,128)S(1)}, u32[]{:S(2)}, u32[]{:S(2)}) collective-permute-start(f32[128,256]{1,0:T(8,128)S(1)} %add_passing.1), channel_id=1, source_target_pairs={{0,2},{1,7},{2,4},{3,1},{4,6},{5,3},{6,0},{7,5},{8,10},{9,15},{10,... | collective-permute-start | bytes 393224 | tf_op jit(solution)/shard_map/ppermute | solution.py:300
  49.2 0.0 collective-permute-done.4
  49.3 0.2 collective-permute-start.5
  49.4 3.1 %collective-permute-done.3 = f32[128,256]{1,0:T(8,128)S(1)} collective-permute-done((f32[128,256]{1,0:T(8,128)S(1)}, f32[128,256]{1,0:T(8,128)S(1)}, u32[]{:S(2)}, u32[]{:S(2)}) %collective-permute-start.3) | collective-permute-done | bytes 131104 | tf_op jit(solution)/shard_map/ppermute | solution.py:300
  52.5 0.0 collective-permute-done.5
  52.5 0.7 %add_add_fusion = f32[128,256]{1,0:T(8,128)} fusion(f32[128,256]{1,0:T(8,128)S(1)} %collective-permute-done.5, f32[128,256]{1,0:T(8,128)S(1)} %get-tuple-element.28, f32[128,256]{1,0:T(8,128)S(1)} %collective-permute-done.3), kind=kLoop, calls=%fused_computation | loop fusion | flops 65536 | bytes 524288 | tf_op jit(solution)/shard_map/add | solution.py:316
  (8 shorter events, 0.1 us)
Async XLA Ops:
  0.0 28.9 %copy-start = (bf16[2304,512]{1,0:T(8,128)(2,1)S(1)}, bf16[2304,512]{1,0:T(8,128)(2,1)}, u32[]{:S(2)}) copy-start(bf16[2304,512]{1,0:T(8,128)(2,1)} %constant.4.clone.tables) | copy-start | bytes 7077892
  0.0 1.2 %copy-start.1 = (f32[4,32,1024]{2,1,0:T(8,128)S(1)}, f32[4,32,1024]{2,1,0:T(8,128)}, u32[]{:S(2)}) copy-start(f32[4,32,1024]{2,1,0:T(8,128)} %records.1) | copy-start | bytes 1572868
  1.2 0.7 %copy-start.2 = (s32[32]{0:T(128)S(1)}, s32[32]{0:T(128)}, u32[]{:S(2)}) copy-start(s32[32]{0:T(128)} %sources.1) | copy-start | bytes 388
  3.1 27.8 %copy-start.3 = (bf16[2,512,512]{2,1,0:T(8,128)(2,1)S(1)}, bf16[2,512,512]{2,1,0:T(8,128)(2,1)}, u32[]{:S(2)}) copy-start(bf16[2,512,512]{2,1,0:T(8,128)(2,1)} %constant.5.clone.tables) | copy-start | bytes 3145732
  32.1 3.6 %collective-permute-start = (f32[128,256]{1,0:T(8,128)S(1)}, f32[128,256]{1,0:T(8,128)S(1)}, u32[]{:S(2)}, u32[]{:S(2)}) collective-permute-start(f32[128,256]{1,0:T(8,128)S(1)} %get-tuple-element.22), channel_id=1, source_target_pairs={{0,1},{1,0},{2,3},{3,2},{4,5},{5,4},{6,7},{7,6},{8,9},{9,8},{10,11... | collective-permute-start | bytes 393224 | tf_op jit(solution)/shard_map/ppermute | solution.py:303
  35.6 6.6 %collective-permute-start.1 = (f32[2,128,256]{2,1,0:T(8,128)S(1)}, f32[2,128,256]{2,1,0:T(8,128)S(1)}, u32[]{:S(2)}, u32[]{:S(2)}) collective-permute-start(f32[2,128,256]{2,1,0:T(8,128)S(1)} %get-tuple-element.25), channel_id=1, source_target_pairs={{0,1},{1,0},{2,3},{3,2},{4,5},{5,4},{6,7},{7,6},{8,9},{9,8},{10,11... | collective-permute-start | bytes 786440 | tf_op jit(solution)/shard_map/ppermute | solution.py:303
  35.8 9.0 %collective-permute-start.2 = (f32[128,256]{1,0:T(8,128)S(1)}, f32[128,256]{1,0:T(8,128)S(1)}, u32[]{:S(2)}, u32[]{:S(2)}) collective-permute-start(f32[128,256]{1,0:T(8,128)S(1)} %add_far.1.refs_0_), channel_id=1, source_target_pairs={{0,2},{1,7},{2,4},{3,1},{4,6},{5,3},{6,0},{7,5},{8,10},{9,15},{10,... | collective-permute-start | bytes 393224 | tf_op jit(solution)/shard_map/ppermute | solution.py:300
  42.3 7.0 %collective-permute-start.4 = (f32[128,256]{1,0:T(8,128)S(1)}, f32[128,256]{1,0:T(8,128)S(1)}, u32[]{:S(2)}, u32[]{:S(2)}) collective-permute-start(f32[128,256]{1,0:T(8,128)S(1)} %get-tuple-element.26.refs_0_), channel_id=1, source_target_pairs={{0,2},{1,7},{2,4},{3,1},{4,6},{5,3},{6,0},{7,5},{8,10},{9,15},{10,... | collective-permute-start | bytes 393224 | tf_op jit(solution)/shard_map/ppermute | solution.py:300
  44.8 7.7 %collective-permute-start.3 = (f32[128,256]{1,0:T(8,128)S(1)}, f32[128,256]{1,0:T(8,128)S(1)}, u32[]{:S(2)}, u32[]{:S(2)}) collective-permute-start(f32[128,256]{1,0:T(8,128)S(1)} %add_passing.1), channel_id=1, source_target_pairs={{0,2},{1,7},{2,4},{3,1},{4,6},{5,3},{6,0},{7,5},{8,10},{9,15},{10,... | collective-permute-start | bytes 393224 | tf_op jit(solution)/shard_map/ppermute | solution.py:300
  49.3 3.2 %collective-permute-start.5 = (f32[128,256]{1,0:T(8,128)S(1)}, f32[128,256]{1,0:T(8,128)S(1)}, u32[]{:S(2)}, u32[]{:S(2)}) collective-permute-start(f32[128,256]{1,0:T(8,128)S(1)} %add.10), channel_id=1, source_target_pairs={{0,1},{1,0},{2,3},{3,2},{4,5},{5,4},{6,7},{7,6},{8,9},{9,8},{10,11... | collective-permute-start | bytes 393224 | tf_op jit(solution)/shard_map/ppermute | solution.py:303

commit v5 on v4

--- a/solution.py
+++ b/solution.py
@@ -25,27 +25,22 @@
 
 
 def bin_order(half):
-    return np.concatenate([np.arange(0, half, 2), np.arange(1, half, 2)])
-
-
-def forward_tables(length):
-    half = length // 2
-    times = np.arange(half)[:, None]
-    tables = []
-    for parity in range(2):
-        bins = np.arange(parity, half, 2)[None, :]
-        angles = (bins * times % length) * (2.0 * math.pi / length)
-        tables += split_table(np.concatenate([np.cos(angles), -np.sin(angles)], axis=1))
-    return np.stack(tables)
+    return np.concatenate([np.arange(0, half, 4), np.arange(2, half, 4), np.arange(1, half, 2)])
+
+
+def wave_table(length, bins, samples):
+    angles = (np.arange(samples)[:, None] * bins[None, :] % length) * (2.0 * math.pi / length)
+    return np.concatenate([np.cos(angles), -np.sin(angles)], axis=1)
 
 
 def front_tables(length, reach):
     half = length // 2
-    mid = half // 2
+    odd = wave_table(length, np.arange(1, half, 2), half)
+    even = [wave_table(length, np.arange(start, half, 4), half // 2) for start in (0, 2)]
     bins = bin_order(half)
-    table = (np.abs(bins[:, None] - bins[None, :]) <= reach).astype(ml_dtypes.bfloat16)
-    band = np.concatenate([table[:mid, :mid], table[mid:, :mid]], axis=1)
-    return np.concatenate([*forward_tables(length), band], axis=0)
+    band = (np.abs(bins[:, None] - bins[None, :]) <= reach).astype(ml_dtypes.bfloat16)
+    waves = [*split_table(odd), *split_table(np.concatenate(even, axis=1))]
+    return np.concatenate([*waves, band], axis=0)
 
 
 def inverse_tables(length, lag_count, factor):
@@ -68,11 +63,24 @@
     return jnp.dot(left, right, preferred_element_type=F32)
 
 
-def mm_turned(left, right):
-    return lax.dot_general(left, right, (((1,), (1,)), ((), ())), preferred_element_type=F32)
-
-
-def pack_kernel(sources, records, packed):
+def pack_kernel(records, packed):
+    windows, times, channels = records.shape
+    dests = packed.shape[0]
+    width = channels // dests
+    per_tile = LANES // width
+    lane = lax.broadcasted_iota(jnp.int32, (times, LANES), 1)
+    for tile in range(channels // LANES):
+        loaded = [records[w, :, tile * LANES : (tile + 1) * LANES] for w in range(windows)]
+        for e in range(per_tile):
+            block = None
+            for w in range(windows):
+                shift = (w - e) * width % LANES
+                moved = pltpu.roll(loaded[w], shift, 1) if shift else loaded[w]
+                block = moved if block is None else jnp.where(lane >= w * width, moved, block)
+            packed[tile * per_tile + e, 0:times, :] = block
+
+
+def pick_kernel(sources, records, packed_in, packed):
     windows, times, channels = records.shape
     dests = packed.shape[0]
     width = channels // dests
@@ -84,23 +92,16 @@
         place = jnp.where(column == s, sources[s] - s * width // LANES * LANES, place)
     pick = jnp.zeros((times, LANES), F32)
     for tile in range(channels // LANES):
-        loaded = [records[w, :, tile * LANES : (tile + 1) * LANES] for w in range(windows)]
-        for e in range(per_tile):
-            block = None
-            for w in range(windows):
-                shift = (w - e) * width % LANES
-                moved = pltpu.roll(loaded[w], shift, 1) if shift else loaded[w]
-                block = moved if block is None else jnp.where(lane >= w * width, moved, block)
-            packed[tile * per_tile + e, 0:times, :] = block
         for w in range(windows):
-            moved = jnp.take_along_axis(loaded[w], place, axis=1)
+            loaded = records[w, :, tile * LANES : (tile + 1) * LANES]
+            moved = jnp.take_along_axis(loaded, place, axis=1)
             low = w * dests + tile * per_tile
             pick = jnp.where((lane >= low) & (lane < low + per_tile), moved, pick)
     for d in range(dests):
         packed[d, times : 2 * times, :] = pick
 
 
-def correlate(white_re, white_im, cross_high, cross_low, target, width):
+def correlate(white_re, white_im, cross_high, cross_low, target, width, core=None):
     rows, half = white_re.shape
     lanes = rows // 2
     windows = lanes // width
@@ -114,10 +115,14 @@
         chan_im = [white_im[w * width : (w + 1) * width, span] for w in range(windows)]
         from_re = [white_re[at, span] for at in rows8]
         from_im = [white_im[at, span] for at in rows8]
+        if core is not None:
+            turn = lax.rem(8 - 4 * core, 8)
+            from_re = [pltpu.roll(rows, turn, 0) for rows in from_re]
+            from_im = [pltpu.roll(rows, turn, 0) for rows in from_im]
         chan_sum = [a + b for a, b in zip(chan_re, chan_im)]
         from_sum = [a + b for a, b in zip(from_re, from_im)]
         from_less = [a - b for a, b in zip(from_re, from_im)]
-        for i in range(8):
+        for i in range(cross_high.shape[0] // width):
             for w in range(windows):
                 one = jnp.broadcast_to(from_re[w][i : i + 1], (width, LANES)) * chan_sum[w]
                 two = jnp.broadcast_to(from_less[w][i : i + 1], (width, LANES)) * chan_im[w]
@@ -144,14 +149,10 @@
     return total
 
 
-def front_kernel(
-    blocks, tables, white_re, white_im, turned
-):
+def level_kernel(blocks, turned):
     devices, double, lanes = blocks.shape
     times = double // 2
     length = devices * times
-    half = length // 2
-    quarter = half // 2
     for part in range(2):
         data = blocks[:, part * times : (part + 1) * times, :].reshape(length, lanes)
         level = jnp.abs(data)
@@ -161,46 +162,52 @@
         size = length + 2 * HALF
         for step in (1, 2, 4, 8, 16):
             total = total + pltpu.roll(total, size - step, 0)
-        amplitude = (total[:length] + tail[HALF:]) / (2 * HALF + 1)
+        amplitude = (total[:length] + tail[HALF:]) * (1.0 / (2 * HALF + 1))
         normal = data / jnp.maximum(amplitude, AMPLITUDE_FLOOR)
         turned[part * lanes : (part + 1) * lanes, :] = normal.T
-    waves = [tables[n * half : (n + 1) * half, :] for n in range(4)]
-    band = [tables[4 * half :, :quarter], tables[4 * half :, quarter:]]
-    first = turned[:, :half]
-    second = turned[:, half:]
-    for parity in range(2):
-        folded = first + second if parity == 0 else first - second
-        high, low = split(folded)
-        spectrum = (
-            mm(high, waves[2 * parity])
-            + mm(low, waves[2 * parity])
-            + mm(high, waves[2 * parity + 1])
-        )
-        white_re[:, parity * quarter : (parity + 1) * quarter] = spectrum[:, :quarter]
-        white_im[:, parity * quarter : (parity + 1) * quarter] = spectrum[:, quarter:]
-    re = white_re[...]
-    im = white_im[...]
+
+
+def spectra_kernel(turned, tables, white_re, white_im):
+    length = turned.shape[1]
+    half = length // 2
+    quarter = half // 2
+    eighth = quarter // 2
+
+    def waves(row, rows, columns):
+        return tables[row : row + rows, columns], tables[row + rows : row + 2 * rows, columns]
+
+    def transform(data, table):
+        high, low = split(data)
+        return mm(high, table[0]) + mm(low, table[0]) + mm(high, table[1])
+
+    first, second = turned[:, :half], turned[:, half:]
+    odd = transform(first - second, waves(0, half, slice(0, half)))
+    folded = first + second
+    first, second = folded[:, :quarter], folded[:, quarter:]
+    zero = transform(first + second, waves(length, quarter, slice(0, quarter)))
+    two = transform(first - second, waves(length, quarter, slice(quarter, half)))
+    re = jnp.concatenate([zero[:, :eighth], two[:, :eighth], odd[:, :quarter]], axis=1)
+    im = jnp.concatenate([zero[:, eighth:], two[:, eighth:], odd[:, quarter:]], axis=1)
     high, low = split(jnp.sqrt(re * re + im * im))
-    for parity in range(2):
-        near = slice(parity * quarter, (parity + 1) * quarter)
-        other = slice((1 - parity) * quarter, (2 - parity) * quarter)
-        cross_mm = mm_turned if parity else mm
-        smooth = (
-            mm(high[:, near], band[0])
-            + mm(low[:, near], band[0])
-            + cross_mm(high[:, other], band[1])
-            + cross_mm(low[:, other], band[1])
-        )
-        gain = 1.0 / (smooth / (2 * (length // 32) + 1) + WHITE_EPSILON)
-        white_re[:, near] = re[:, near] * gain
-        white_im[:, near] = im[:, near] * gain
+    band = tables[length + half :, :]
+    smooth = (mm(high, band) + mm(low, band)) * (1.0 / (2 * (length // 32) + 1))
+    gain = 1.0 / (smooth + WHITE_EPSILON)
+    white_re[...] = re * gain
+    white_im[...] = im * gain
 
 
 def stack_kernel(kind, white_re, white_im, tables, *refs):
-    cross_high, cross_low, both = refs[-3:]
     win = lax.axis_index("win")
     z_hi, core = lax.div(win, 2), lax.rem(win, 2)
-    step = {"far": 2, "ahead": 1 + 2 * core, "behind": 3 - 2 * core, "here": 0}[kind]
+    if kind.startswith("far"):
+        result, cross_high, cross_low = refs[-3:]
+        which = core if kind == "far_keep" else 1 - core
+        target = lax.rem(z_hi + 2, 4)
+        correlate(white_re, white_im, cross_high, cross_low, target, 32, which)
+        result[...] = invert(cross_high, cross_low, tables)
+        return
+    cross_high, cross_low, both = refs[-3:]
+    step = {"ahead": 1 + 2 * core, "behind": 3 - 2 * core, "here": 0}[kind]
     correlate(white_re, white_im, cross_high, cross_low, lax.rem(z_hi + step, 4), 32)
     both[...] = invert(cross_high, cross_low, tables).reshape(both.shape)
     if kind == "behind":
@@ -232,38 +239,64 @@
     factor = 1.0 / math.sqrt(total_windows * half)
     vmem = pl.BlockSpec(memory_space=pltpu.VMEM)
     smem = pl.BlockSpec(memory_space=pltpu.SMEM)
-    hbm = pl.BlockSpec(memory_space=pltpu.HBM)
-    tiles = channels // LANES
-
+
+    block_shape = jax.ShapeDtypeStruct((chan_count, 2 * times, LANES), F32)
     packed = pl.pallas_call(
         pack_kernel,
-        out_shape=jax.ShapeDtypeStruct((chan_count, 2 * times, LANES), F32),
-        in_specs=[smem, vmem],
+        out_shape=block_shape,
+        in_specs=[vmem],
         out_specs=vmem,
         compiler_params=pltpu.CompilerParams(vmem_limit_bytes=4 << 20),
+        cost_estimate=pl.CostEstimate(flops=1 << 31, bytes_accessed=1 << 20, transcendentals=0),
         name="pack",
-    )(sources, records)
+    )(records)
+    packed = pl.pallas_call(
+        pick_kernel,
+        out_shape=block_shape,
+        in_specs=[smem, vmem, vmem],
+        out_specs=vmem,
+        input_output_aliases={2: 0},
+        compiler_params=pltpu.CompilerParams(vmem_limit_bytes=4 << 20),
+        name="pick",
+    )(sources, records, packed)
     blocks = lax.all_to_all(packed, "chan", 0, 0, tiled=True)
 
     forward = jnp.asarray(front_tables(length, length // 32))
     inverse = jnp.asarray(inverse_tables(length, lag_count, factor))
     rows = 2 * LANES
     shape = jax.ShapeDtypeStruct
+    turned = pl.pallas_call(
+        level_kernel,
+        out_shape=shape((rows, length), F32),
+        in_specs=[vmem],
+        out_specs=vmem,
+        compiler_params=pltpu.CompilerParams(vmem_limit_bytes=16 << 20),
+        cost_estimate=pl.CostEstimate(flops=1 << 28, bytes_accessed=1 << 20, transcendentals=0),
+        name="level",
+    )(blocks)
     white_re, white_im = pl.pallas_call(
-        front_kernel,
+        spectra_kernel,
         out_shape=(shape((rows, half), F32), shape((rows, half), F32)),
         in_specs=[vmem] * 2,
         out_specs=(vmem, vmem),
-        scratch_shapes=[pltpu.VMEM((rows, length), F32)],
         compiler_params=pltpu.CompilerParams(vmem_limit_bytes=24 << 20),
-        name="front",
-    )(blocks, forward)
+        cost_estimate=pl.CostEstimate(flops=1 << 32, bytes_accessed=1 << 24, transcendentals=0),
+        name="spectra",
+    )(turned, forward)
 
     piece = shape((LANES, lag_count), F32)
 
     def stack(kind, after=None, handed=None):
         extra = [] if after is None else [after]
-        outs = [shape((2, LANES, lag_count), F32)] if kind == "behind" else [piece, piece]
+        outs = {
+            "behind": [shape((2, LANES, lag_count), F32)],
+            "far_send": [piece],
+            "far_keep": [piece],
+        }.get(kind, [piece, piece])
+        rows = LANES if kind.startswith("far") else 2 * LANES
+        scratch = [pltpu.VMEM((rows, length), BF16), pltpu.VMEM((rows, length), BF16)]
+        if rows > LANES:
+            scratch.append(pltpu.VMEM((2, LANES, lag_count), F32))
         aliases = {}
         if handed is not None:
             aliases = {3 + len(extra): 0}
@@ -274,11 +307,7 @@
             out_shape=outs,
             in_specs=[vmem] * (3 + len(extra)),
             out_specs=[vmem] * len(outs),
-            scratch_shapes=[
-                pltpu.VMEM((2 * LANES, length), BF16),
-                pltpu.VMEM((2 * LANES, length), BF16),
-                pltpu.VMEM((2, LANES, lag_count), F32),
-            ],
+            scratch_shapes=scratch,
             input_output_aliases=aliases,
             compiler_params=pltpu.CompilerParams(vmem_limit_bytes=16 << 20),
             cost_estimate=pl.CostEstimate(flops=1 << 32, bytes_accessed=1 << 24, transcendentals=0),
@@ -302,11 +331,12 @@
     def across(value):
         return lax.ppermute(value, "win", [(i, i ^ 1) for i in range(8)])
 
-    keep_far, send_far = stack("far")
-    keep_far, behind = stack("behind", handed=keep_far)
+    (send_far,) = stack("far_send")
+    (keep_far,) = stack("far_keep", after=send_far)
     (far,) = small(add_kernel, 1, "add_far", keep_far, across(send_far))
     passing = onward(far)
-    own, other = stack("ahead", after=far)
+    (behind,) = stack("behind", after=far)
+    own, other = stack("ahead", after=behind)
     own, other = small(join_kernel, 2, "join", own, other, across(behind))
     early = onward(other)
     own, here_own, here_other = stack("here", after=other, handed=own)

time: 53.3 us -> 52.5 us (0.985)
  starting transfers between devices: 13.4 us -> 12.4 us
  waiting for transfers between devices: 3.07 us -> 3.74 us
  local copies, waits for them, and re-layouts: 1.86 us -> 1.23 us
    ppermute x3, starting transfers between devices: 10.9 us -> 8.46 us  [onward(): return lax.ppermute(value, 'win', pairs)]
    ppermute x3, starting transfers between devices: 2.53 us -> 3.9 us  [across(): return lax.ppermute(value, 'win', [(i, i ^ 1) for i in range(8)])]
    unnamed x8, local copies, waits for them, and re-layouts: 1.86 us -> 1.23 us
    ppermute x3, waiting for transfers between devices: 0.01 us -> 0.57 us  [across(): return lax.ppermute(value, 'win', [(i, i ^ 1) for i in range(8)])]
    pallas_call x4 -> x5, Pallas kernels: 4.97 us -> 5.11 us  [stack(): pl.pallas_call(functools.partial(stack_kernel, kind), out_shape=outs, in_...]
    pallas_call x2 -> x4, Pallas kernels: 3.17 us -> 3.17 us  [the longest x1 1.22 us: local(): pl.pallas_call(spectra_kernel, out_shape=(shape((rows, half), F32), shape...]
  transfers between devices with their start and end apart: 6 -> 6, of which waited for: 1 -> 4; matrix products, arithmetic and copies ran while one was open for 0% -> 0% of each run, Pallas kernels for 7% -> 9%
where the time goes in v5:
time: 52.5 us; the launch traced here: 52.3 us
  blocking collectives  25.8 us (49%)
  starting transfers between devices  12.4 us (24%)
  Pallas kernels  8.34 us (16%)
  waiting for transfers between devices  3.74 us (7%)
  local copies, waits for them, and re-layouts  1.23 us (2%)
  other arithmetic  0.7 us (1%)
    all_to_all x1, blocking collectives, local(): blocks = lax.all_to_all(packed, 'chan', 0, 0, tiled=True)  25.8 us
    ppermute x3, starting transfers between devices, onward(): return lax.ppermute(value, 'win', pairs)  8.46 us
    pallas_call x5, Pallas kernels, stack(): pl.pallas_call(functools.partial(stack_kernel, kind), out_shape=outs, in_...  5.11 us
    ppermute x3, starting transfers between devices, across(): return lax.ppermute(value, 'win', [(i, i ^ 1) for i in range(8)])  3.9 us
    ppermute x3, waiting for transfers between devices, onward(): return lax.ppermute(value, 'win', pairs)  3.18 us
    unnamed x8, local copies, waits for them, and re-layouts  1.23 us
    pallas_call x1, Pallas kernels, local(): pl.pallas_call(spectra_kernel, out_shape=(shape((rows, half), F32), shape...  1.22 us
  transfers between devices with their start and end apart: 6, of which 4 were waited for; matrix products, arithmetic and copies ran while one was open for 0% of the time, Pallas kernels for 9%

profile of v5, /device:TPU:1, one launch (start us, length us, event | category | flops | bytes accessed | tf_op | source)
XLA Modules:
  0.0 52.3 jit_solution(17932050666321960626)
XLA Ops:
  0.0 1.0 %copy-done = f32[4,32,1024]{2,1,0:T(8,128)S(1)} copy-done((f32[4,32,1024]{2,1,0:T(8,128)S(1)}, f32[4,32,1024]{2,1,0:T(8,128)}, u32[]{:S(2)}) %copy-start) | copy-done | bytes 524312
  1.0 0.5 pack.1.packed_in
  1.5 0.2 copy-done.1
  1.7 0.8 %pick.1 = f32[32,64,128]{2,1,0:T(8,128)S(1)} custom-call(s32[32]{0:T(128)S(1)} %copy-done.1, f32[4,32,1024]{2,1,0:T(8,128)S(1)} %copy-done, f32[32,64,128]{2,1,0:T(8,128)S(1)} %pack.1.packed_in), custom_call_target="tpu_custom_call", output_to_operand_aliasing={{}: (2, {})} | custom-call | tf_op jit(solution)/shard_map/pick/pallas_call | solution.py:253
  2.5 0.0 copy-start.2
  2.5 25.8 %all_to_all.5.blocks = f32[32,64,128]{2,1,0:T(8,128)S(1)} all-to-all(f32[32,64,128]{2,1,0:T(8,128)S(1)} %pick.1), channel_id=1, replica_groups=mesh['chan'=32,'win'=8] {'chan'}, dimensions={0} | all-to-all | bytes 2097152 | tf_op jit(solution)/shard_map/all_to_all | solution.py:262
  28.4 0.7 %level.1.turned = f32[256,1024]{1,0:T(8,128)S(1)} custom-call(f32[32,64,128]{2,1,0:T(8,128)S(1)} %all_to_all.5.blocks), custom_call_target="tpu_custom_call" | custom-call | flops 268435456 | bytes 1048576 | tf_op jit(solution)/shard_map/level/pallas_call | solution.py:268
  29.1 1.2 %spectra.1 = (f32[256,512]{1,0:T(8,128)S(1)}, f32[256,512]{1,0:T(8,128)S(1)}) custom-call(f32[256,1024]{1,0:T(8,128)S(1)} %level.1.turned, bf16[2048,512]{1,0:T(8,128)(2,1)S(1)} %copy-done.2), custom_call_target="tpu_custom_call" | custom-call | flops 4294967296 | bytes 16777216 | tf_op jit(solution)/shard_map/spectra/pallas_call | solution.py:277
  30.3 0.7 %stack_far_send.1.refs_0_ = f32[128,256]{1,0:T(8,128)S(1)} custom-call(f32[256,512]{1,0:T(8,128)S(1)} %get-tuple-element.14.white_re, f32[256,512]{1,0:T(8,128)S(1)} %get-tuple-element.15.white_im, bf16[2,512,512]{2,1,0:T(8,128)(2,1)S(1)} %copy-done.3), custom_call_target="tpu_custom_call" | custom-call | flops 4294967296 | bytes 16777216 | tf_op jit(solution)/shard_map/stack_far_send/pallas_call | solution.py:305
  31.0 2.2 %collective-permute-start = (f32[128,256]{1,0:T(8,128)S(1)}, f32[128,256]{1,0:T(8,128)S(1)}, u32[]{:S(2)}, u32[]{:S(2)}) collective-permute-start(f32[128,256]{1,0:T(8,128)S(1)} %stack_far_send.1.refs_0_), channel_id=1, source_target_pairs={{0,1},{1,0},{2,3},{3,2},{4,5},{5,4},{6,7},{7,6},{8,9},{9,8},{10,11... | collective-permute-start | bytes 393224 | tf_op jit(solution)/shard_map/ppermute | solution.py:332
  33.2 0.7 %stack_far_keep.1.refs_0_ = f32[128,256]{1,0:T(8,128)S(1)} custom-call(f32[256,512]{1,0:T(8,128)S(1)} %get-tuple-element.14.white_re, f32[256,512]{1,0:T(8,128)S(1)} %get-tuple-element.15.white_im, bf16[2,512,512]{2,1,0:T(8,128)(2,1)S(1)} %copy-done.3, f32[128,256]{1,0:T(8,128)S(1)} %stack_far_send.1.refs_0_), custom_call_target="tpu_custom_call" | custom-call | flops 4294967296 | bytes 16777216 | tf_op jit(solution)/shard_map/stack_far_keep/pallas_call | solution.py:305
  33.9 0.3 collective-permute-done.refs_1_
  34.2 5.2 %collective-permute-start.2 = (f32[128,256]{1,0:T(8,128)S(1)}, f32[128,256]{1,0:T(8,128)S(1)}, u32[]{:S(2)}, u32[]{:S(2)}) collective-permute-start(f32[128,256]{1,0:T(8,128)S(1)} %add_far.1.refs_0_), channel_id=1, source_target_pairs={{0,2},{1,7},{2,4},{3,1},{4,6},{5,3},{6,0},{7,5},{8,10},{9,15},{10,... | collective-permute-start | bytes 393224 | tf_op jit(solution)/shard_map/ppermute | solution.py:329
  39.4 1.2 %stack_behind.1.refs_0_ = f32[2,128,256]{2,1,0:T(8,128)S(1)} custom-call(f32[256,512]{1,0:T(8,128)S(1)} %get-tuple-element.14.white_re, f32[256,512]{1,0:T(8,128)S(1)} %get-tuple-element.15.white_im, bf16[2,512,512]{2,1,0:T(8,128)(2,1)S(1)} %copy-done.3, f32[128,256]{1,0:T(8,128)S(1)} %add_far.1.refs_0_), custom_call_target="tpu_custom_call" | custom-call | flops 4294967296 | bytes 16777216 | tf_op jit(solution)/shard_map/stack_behind/pallas_call | solution.py:305
  40.7 0.1 collective-permute-start.1
  40.8 1.2 %stack_ahead.1 = (f32[128,256]{1,0:T(8,128)S(1)}, f32[128,256]{1,0:T(8,128)S(1)}) custom-call(f32[256,512]{1,0:T(8,128)S(1)} %get-tuple-element.14.white_re, f32[256,512]{1,0:T(8,128)S(1)} %get-tuple-element.15.white_im, bf16[2,512,512]{2,1,0:T(8,128)(2,1)S(1)} %copy-done.3, f32[2,128,256]{2,1,0:T(8,128)S(1)} %stack_behind.1.refs_0_), custom_call_target="tpu_custom_call" | custom-call | flops 4294967296 | bytes 16777216 | tf_op jit(solution)/shard_map/stack_ahead/pallas_call | solution.py:305
  42.0 0.3 collective-permute-done.1.received
  42.3 1.3 %collective-permute-start.4 = (f32[128,256]{1,0:T(8,128)S(1)}, f32[128,256]{1,0:T(8,128)S(1)}, u32[]{:S(2)}, u32[]{:S(2)}) collective-permute-start(f32[128,256]{1,0:T(8,128)S(1)} %get-tuple-element.18.refs_0_), channel_id=1, source_target_pairs={{0,2},{1,7},{2,4},{3,1},{4,6},{5,3},{6,0},{7,5},{8,10},{9,15},{10,... | collective-permute-start | bytes 393224 | tf_op jit(solution)/shard_map/ppermute | solution.py:329
  43.6 1.2 %stack_here.1 = (f32[128,256]{1,0:T(8,128)S(1)}, f32[128,256]{1,0:T(8,128)S(1)}, f32[128,256]{1,0:T(8,128)S(1)}) custom-call(f32[256,512]{1,0:T(8,128)S(1)} %get-tuple-element.14.white_re, f32[256,512]{1,0:T(8,128)S(1)} %get-tuple-element.15.white_im, bf16[2,512,512]{2,1,0:T(8,128)(2,1)S(1)} %copy-done.3, ...), custom_call_target="tpu_custom_call", output_to_operand_aliasing={{0}: (4, {})} | custom-call | flops 4294967296 | bytes 16777216 | tf_op jit(solution)/shard_map/stack_here/pallas_call | solution.py:305
  44.9 2.0 %collective-permute-start.3 = (f32[128,256]{1,0:T(8,128)S(1)}, f32[128,256]{1,0:T(8,128)S(1)}, u32[]{:S(2)}, u32[]{:S(2)}) collective-permute-start(f32[128,256]{1,0:T(8,128)S(1)} %add_passing.1), channel_id=1, source_target_pairs={{0,2},{1,7},{2,4},{3,1},{4,6},{5,3},{6,0},{7,5},{8,10},{9,15},{10,... | collective-permute-start | bytes 393224 | tf_op jit(solution)/shard_map/ppermute | solution.py:329
  46.9 2.0 %collective-permute-done.4 = f32[128,256]{1,0:T(8,128)S(1)} collective-permute-done((f32[128,256]{1,0:T(8,128)S(1)}, f32[128,256]{1,0:T(8,128)S(1)}, u32[]{:S(2)}, u32[]{:S(2)}) %collective-permute-start.4) | collective-permute-done | bytes 131104 | tf_op jit(solution)/shard_map/ppermute | solution.py:329
  48.9 1.6 %collective-permute-start.5 = (f32[128,256]{1,0:T(8,128)S(1)}, f32[128,256]{1,0:T(8,128)S(1)}, u32[]{:S(2)}, u32[]{:S(2)}) collective-permute-start(f32[128,256]{1,0:T(8,128)S(1)} %add.10), channel_id=1, source_target_pairs={{0,1},{1,0},{2,3},{3,2},{4,5},{5,4},{6,7},{7,6},{8,9},{9,8},{10,11... | collective-permute-start | bytes 393224 | tf_op jit(solution)/shard_map/ppermute | solution.py:332
  50.4 1.2 %collective-permute-done.3 = f32[128,256]{1,0:T(8,128)S(1)} collective-permute-done((f32[128,256]{1,0:T(8,128)S(1)}, f32[128,256]{1,0:T(8,128)S(1)}, u32[]{:S(2)}, u32[]{:S(2)}) %collective-permute-start.3) | collective-permute-done | bytes 131104 | tf_op jit(solution)/shard_map/ppermute | solution.py:329
  51.6 0.7 %add_add_fusion = f32[128,256]{1,0:T(8,128)} fusion(f32[128,256]{1,0:T(8,128)S(1)} %collective-permute-done.5, f32[128,256]{1,0:T(8,128)S(1)} %get-tuple-element.20, f32[128,256]{1,0:T(8,128)S(1)} %collective-permute-done.3), kind=kLoop, calls=%fused_computation | loop fusion | flops 65536 | bytes 524288 | tf_op jit(solution)/shard_map/add | solution.py:346
  (11 shorter events, 0.1 us)
Async XLA Ops:
  0.0 1.0 %copy-start = (f32[4,32,1024]{2,1,0:T(8,128)S(1)}, f32[4,32,1024]{2,1,0:T(8,128)}, u32[]{:S(2)}) copy-start(f32[4,32,1024]{2,1,0:T(8,128)} %records.3) | copy-start | bytes 1572868
  1.0 0.7 %copy-start.1 = (s32[32]{0:T(128)S(1)}, s32[32]{0:T(128)}, u32[]{:S(2)}) copy-start(s32[32]{0:T(128)} %sources.1) | copy-start | bytes 388
  2.5 26.5 %copy-start.2 = (bf16[2048,512]{1,0:T(8,128)(2,1)S(1)}, bf16[2048,512]{1,0:T(8,128)(2,1)}, u32[]{:S(2)}) copy-start(bf16[2048,512]{1,0:T(8,128)(2,1)} %constant.4.clone.tables) | copy-start | bytes 6291460
  29.0 1.2 %copy-start.3 = (bf16[2,512,512]{2,1,0:T(8,128)(2,1)S(1)}, bf16[2,512,512]{2,1,0:T(8,128)(2,1)}, u32[]{:S(2)}) copy-start(bf16[2,512,512]{2,1,0:T(8,128)(2,1)} %constant.5.clone.tables) | copy-start | bytes 3145732
  31.0 3.2 %collective-permute-start = (f32[128,256]{1,0:T(8,128)S(1)}, f32[128,256]{1,0:T(8,128)S(1)}, u32[]{:S(2)}, u32[]{:S(2)}) collective-permute-start(f32[128,256]{1,0:T(8,128)S(1)} %stack_far_send.1.refs_0_), channel_id=1, source_target_pairs={{0,1},{1,0},{2,3},{3,2},{4,5},{5,4},{6,7},{7,6},{8,9},{9,8},{10,11... | collective-permute-start | bytes 393224 | tf_op jit(solution)/shard_map/ppermute | solution.py:332
  34.2 10.6 %collective-permute-start.2 = (f32[128,256]{1,0:T(8,128)S(1)}, f32[128,256]{1,0:T(8,128)S(1)}, u32[]{:S(2)}, u32[]{:S(2)}) collective-permute-start(f32[128,256]{1,0:T(8,128)S(1)} %add_far.1.refs_0_), channel_id=1, source_target_pairs={{0,2},{1,7},{2,4},{3,1},{4,6},{5,3},{6,0},{7,5},{8,10},{9,15},{10,... | collective-permute-start | bytes 393224 | tf_op jit(solution)/shard_map/ppermute | solution.py:329
  40.7 1.6 %collective-permute-start.1 = (f32[2,128,256]{2,1,0:T(8,128)S(1)}, f32[2,128,256]{2,1,0:T(8,128)S(1)}, u32[]{:S(2)}, u32[]{:S(2)}) collective-permute-start(f32[2,128,256]{2,1,0:T(8,128)S(1)} %stack_behind.1.refs_0_), channel_id=1, source_target_pairs={{0,1},{1,0},{2,3},{3,2},{4,5},{5,4},{6,7},{7,6},{8,9},{9,8},{10,11... | collective-permute-start | bytes 786440 | tf_op jit(solution)/shard_map/ppermute | solution.py:332
  42.3 6.5 %collective-permute-start.4 = (f32[128,256]{1,0:T(8,128)S(1)}, f32[128,256]{1,0:T(8,128)S(1)}, u32[]{:S(2)}, u32[]{:S(2)}) collective-permute-start(f32[128,256]{1,0:T(8,128)S(1)} %get-tuple-element.18.refs_0_), channel_id=1, source_target_pairs={{0,2},{1,7},{2,4},{3,1},{4,6},{5,3},{6,0},{7,5},{8,10},{9,15},{10,... | collective-permute-start | bytes 393224 | tf_op jit(solution)/shard_map/ppermute | solution.py:329
  44.9 6.8 %collective-permute-start.3 = (f32[128,256]{1,0:T(8,128)S(1)}, f32[128,256]{1,0:T(8,128)S(1)}, u32[]{:S(2)}, u32[]{:S(2)}) collective-permute-start(f32[128,256]{1,0:T(8,128)S(1)} %add_passing.1), channel_id=1, source_target_pairs={{0,2},{1,7},{2,4},{3,1},{4,6},{5,3},{6,0},{7,5},{8,10},{9,15},{10,... | collective-permute-start | bytes 393224 | tf_op jit(solution)/shard_map/ppermute | solution.py:329
  48.9 2.8 %collective-permute-start.5 = (f32[128,256]{1,0:T(8,128)S(1)}, f32[128,256]{1,0:T(8,128)S(1)}, u32[]{:S(2)}, u32[]{:S(2)}) collective-permute-start(f32[128,256]{1,0:T(8,128)S(1)} %add.10), channel_id=1, source_target_pairs={{0,1},{1,0},{2,3},{3,2},{4,5},{5,4},{6,7},{7,6},{8,9},{9,8},{10,11... | collective-permute-start | bytes 393224 | tf_op jit(solution)/shard_map/ppermute | solution.py:332

commit v6 on v5

--- a/solution.py
+++ b/solution.py
@@ -86,10 +86,8 @@
     width = channels // dests
     per_tile = LANES // width
     lane = lax.broadcasted_iota(jnp.int32, (times, LANES), 1)
-    column = lax.rem(lane, dests)
-    place = jnp.zeros((times, LANES), jnp.int32)
-    for s in range(dests):
-        place = jnp.where(column == s, sources[s] - s * width // LANES * LANES, place)
+    place = jnp.concatenate([sources[...]] * windows, axis=1) & (LANES - 1)
+    place = jnp.broadcast_to(place, (times, LANES))
     pick = jnp.zeros((times, LANES), F32)
     for tile in range(channels // LANES):
         for w in range(windows):
@@ -199,15 +197,15 @@
 def stack_kernel(kind, white_re, white_im, tables, *refs):
     win = lax.axis_index("win")
     z_hi, core = lax.div(win, 2), lax.rem(win, 2)
-    if kind.startswith("far"):
+    if kind.startswith(("far", "here")):
         result, cross_high, cross_low = refs[-3:]
-        which = core if kind == "far_keep" else 1 - core
-        target = lax.rem(z_hi + 2, 4)
+        which = core if kind.endswith("own") else 1 - core
+        target = lax.rem(z_hi + (2 if kind.startswith("far") else 0), 4)
         correlate(white_re, white_im, cross_high, cross_low, target, 32, which)
         result[...] = invert(cross_high, cross_low, tables)
         return
     cross_high, cross_low, both = refs[-3:]
-    step = {"ahead": 1 + 2 * core, "behind": 3 - 2 * core, "here": 0}[kind]
+    step = {"ahead": 1 + 2 * core, "behind": 3 - 2 * core}[kind]
     correlate(white_re, white_im, cross_high, cross_low, lax.rem(z_hi + step, 4), 32)
     both[...] = invert(cross_high, cross_low, tables).reshape(both.shape)
     if kind == "behind":
@@ -238,7 +236,6 @@
     total_windows = windows * lax.axis_size("win")
     factor = 1.0 / math.sqrt(total_windows * half)
     vmem = pl.BlockSpec(memory_space=pltpu.VMEM)
-    smem = pl.BlockSpec(memory_space=pltpu.SMEM)
 
     block_shape = jax.ShapeDtypeStruct((chan_count, 2 * times, LANES), F32)
     packed = pl.pallas_call(
@@ -253,12 +250,12 @@
     packed = pl.pallas_call(
         pick_kernel,
         out_shape=block_shape,
-        in_specs=[smem, vmem, vmem],
+        in_specs=[vmem, vmem, vmem],
         out_specs=vmem,
         input_output_aliases={2: 0},
         compiler_params=pltpu.CompilerParams(vmem_limit_bytes=4 << 20),
         name="pick",
-    )(sources, records, packed)
+    )(sources.reshape(1, -1), records, packed)
     blocks = lax.all_to_all(packed, "chan", 0, 0, tiled=True)
 
     forward = jnp.asarray(front_tables(length, length // 32))
@@ -290,10 +287,9 @@
         extra = [] if after is None else [after]
         outs = {
             "behind": [shape((2, LANES, lag_count), F32)],
-            "far_send": [piece],
-            "far_keep": [piece],
-        }.get(kind, [piece, piece])
-        rows = LANES if kind.startswith("far") else 2 * LANES
+            "ahead": [piece, piece],
+        }.get(kind, [piece])
+        rows = 2 * LANES if kind in ("behind", "ahead") else LANES
         scratch = [pltpu.VMEM((rows, length), BF16), pltpu.VMEM((rows, length), BF16)]
         if rows > LANES:
             scratch.append(pltpu.VMEM((2, LANES, lag_count), F32))
@@ -331,17 +327,18 @@
     def across(value):
         return lax.ppermute(value, "win", [(i, i ^ 1) for i in range(8)])
 
-    (send_far,) = stack("far_send")
-    (keep_far,) = stack("far_keep", after=send_far)
+    (send_far,) = stack("far_other")
+    (keep_far,) = stack("far_own", after=send_far)
     (far,) = small(add_kernel, 1, "add_far", keep_far, across(send_far))
     passing = onward(far)
     (behind,) = stack("behind", after=far)
     own, other = stack("ahead", after=behind)
     own, other = small(join_kernel, 2, "join", own, other, across(behind))
     early = onward(other)
-    own, here_own, here_other = stack("here", after=other, handed=own)
     (own,) = small(add_kernel, 1, "add_passing", own, passing)
     late = onward(own)
+    (here_own,) = stack("here_own", after=own)
+    (here_other,) = stack("here_other", after=early)
     turned = across(here_other + early)
     result = (here_own + late) + turned
     return jnp.transpose(result.reshape(4, 32, lag_count), (0, 2, 1))

time: 52.5 us -> 52.8 us (level)
  waiting for transfers between devices: 3.74 us -> 4.48 us
    ppermute x3, starting transfers between devices: 3.9 us -> 2.51 us  [across(): return lax.ppermute(value, 'win', [(i, i ^ 1) for i in range(8)])]
    ppermute x3, starting transfers between devices: 8.46 us -> 9.72 us  [onward(): return lax.ppermute(value, 'win', pairs)]
    ppermute x3, waiting for transfers between devices: 0.57 us -> 1.12 us  [across(): return lax.ppermute(value, 'win', [(i, i ^ 1) for i in range(8)])]
    pallas_call x5 -> x6, Pallas kernels: 5.11 us -> 5.25 us  [stack(): pl.pallas_call(functools.partial(stack_kernel, kind), out_shape=outs, in_...]
where the time goes in v6:
time: 52.8 us; the launch traced here: 52.6 us
  blocking collectives  25.8 us (49%)
  starting transfers between devices  12.2 us (23%)
  Pallas kernels  7.99 us (15%)
  waiting for transfers between devices  4.48 us (8%)
  local copies, waits for them, and re-layouts  1.23 us (2%)
  other arithmetic  0.7 us (1%)
    all_to_all x1, blocking collectives, local(): blocks = lax.all_to_all(packed, 'chan', 0, 0, tiled=True)  25.8 us
    ppermute x3, starting transfers between devices, onward(): return lax.ppermute(value, 'win', pairs)  9.72 us
    pallas_call x6, Pallas kernels, stack(): pl.pallas_call(functools.partial(stack_kernel, kind), out_shape=outs, in_...  5.25 us
    ppermute x3, waiting for transfers between devices, onward(): return lax.ppermute(value, 'win', pairs)  3.36 us
    ppermute x3, starting transfers between devices, across(): return lax.ppermute(value, 'win', [(i, i ^ 1) for i in range(8)])  2.51 us
    unnamed x8, local copies, waits for them, and re-layouts  1.23 us
    pallas_call x1, Pallas kernels, local(): pl.pallas_call(spectra_kernel, out_shape=(shape((rows, half), F32), shape...  1.22 us
    ppermute x3, waiting for transfers between devices, across(): return lax.ppermute(value, 'win', [(i, i ^ 1) for i in range(8)])  1.12 us
  transfers between devices with their start and end apart: 6, of which 4 were waited for; matrix products, arithmetic and copies ran while one was open for 0% of the time, Pallas kernels for 9%

profile of v6, /device:TPU:1, one launch (start us, length us, event | category | flops | bytes accessed | tf_op | source)
XLA Modules:
  0.0 52.6 jit_solution(7742854620678262310)
XLA Ops:
  0.0 1.0 %copy-done = f32[4,32,1024]{2,1,0:T(8,128)S(1)} copy-done((f32[4,32,1024]{2,1,0:T(8,128)S(1)}, f32[4,32,1024]{2,1,0:T(8,128)}, u32[]{:S(2)}) %copy-start) | copy-done | bytes 524312
  1.0 0.5 pack.1.packed_in
  1.5 0.2 copy-done.1
  1.7 0.3 pick.1
  2.0 25.8 %all_to_all.5.blocks = f32[32,64,128]{2,1,0:T(8,128)S(1)} all-to-all(f32[32,64,128]{2,1,0:T(8,128)S(1)} %pick.1), channel_id=1, replica_groups=mesh['chan'=32,'win'=8] {'chan'}, dimensions={0} | all-to-all | bytes 2097152 | tf_op jit(solution)/shard_map/all_to_all | solution.py:259
  27.9 0.7 %level.1.turned = f32[256,1024]{1,0:T(8,128)S(1)} custom-call(f32[32,64,128]{2,1,0:T(8,128)S(1)} %all_to_all.5.blocks), custom_call_target="tpu_custom_call" | custom-call | flops 268435456 | bytes 1048576 | tf_op jit(solution)/shard_map/level/pallas_call | solution.py:265
  28.6 1.2 %spectra.1 = (f32[256,512]{1,0:T(8,128)S(1)}, f32[256,512]{1,0:T(8,128)S(1)}) custom-call(f32[256,1024]{1,0:T(8,128)S(1)} %level.1.turned, bf16[2048,512]{1,0:T(8,128)(2,1)S(1)} %copy-done.2), custom_call_target="tpu_custom_call" | custom-call | flops 4294967296 | bytes 16777216 | tf_op jit(solution)/shard_map/spectra/pallas_call | solution.py:274
  29.8 0.7 %stack_far_other.1.refs_0_ = f32[128,256]{1,0:T(8,128)S(1)} custom-call(f32[256,512]{1,0:T(8,128)S(1)} %get-tuple-element.11.white_re, f32[256,512]{1,0:T(8,128)S(1)} %get-tuple-element.12.white_im, bf16[2,512,512]{2,1,0:T(8,128)(2,1)S(1)} %copy-done.3), custom_call_target="tpu_custom_call" | custom-call | flops 4294967296 | bytes 16777216 | tf_op jit(solution)/shard_map/stack_far_other/pallas_call | solution.py:301
  30.5 2.2 %collective-permute-start = (f32[128,256]{1,0:T(8,128)S(1)}, f32[128,256]{1,0:T(8,128)S(1)}, u32[]{:S(2)}, u32[]{:S(2)}) collective-permute-start(f32[128,256]{1,0:T(8,128)S(1)} %stack_far_other.1.refs_0_), channel_id=1, source_target_pairs={{0,1},{1,0},{2,3},{3,2},{4,5},{5,4},{6,7},{7,6},{8,9},{9,8},{10,11... | collective-permute-start | bytes 393224 | tf_op jit(solution)/shard_map/ppermute | solution.py:328
  32.8 0.7 %stack_far_own.1.refs_0_ = f32[128,256]{1,0:T(8,128)S(1)} custom-call(f32[256,512]{1,0:T(8,128)S(1)} %get-tuple-element.11.white_re, f32[256,512]{1,0:T(8,128)S(1)} %get-tuple-element.12.white_im, bf16[2,512,512]{2,1,0:T(8,128)(2,1)S(1)} %copy-done.3, f32[128,256]{1,0:T(8,128)S(1)} %stack_far_other.1.refs_0_), custom_call_target="tpu_custom_call" | custom-call | flops 4294967296 | bytes 16777216 | tf_op jit(solution)/shard_map/stack_far_own/pallas_call | solution.py:301
  33.4 0.3 collective-permute-done.refs_1_
  33.8 5.2 %collective-permute-start.2 = (f32[128,256]{1,0:T(8,128)S(1)}, f32[128,256]{1,0:T(8,128)S(1)}, u32[]{:S(2)}, u32[]{:S(2)}) collective-permute-start(f32[128,256]{1,0:T(8,128)S(1)} %add_far.1.refs_0_), channel_id=1, source_target_pairs={{0,2},{1,7},{2,4},{3,1},{4,6},{5,3},{6,0},{7,5},{8,10},{9,15},{10,... | collective-permute-start | bytes 393224 | tf_op jit(solution)/shard_map/ppermute | solution.py:325
  39.0 1.2 %stack_behind.1.refs_0_ = f32[2,128,256]{2,1,0:T(8,128)S(1)} custom-call(f32[256,512]{1,0:T(8,128)S(1)} %get-tuple-element.11.white_re, f32[256,512]{1,0:T(8,128)S(1)} %get-tuple-element.12.white_im, bf16[2,512,512]{2,1,0:T(8,128)(2,1)S(1)} %copy-done.3, f32[128,256]{1,0:T(8,128)S(1)} %add_far.1.refs_0_), custom_call_target="tpu_custom_call" | custom-call | flops 4294967296 | bytes 16777216 | tf_op jit(solution)/shard_map/stack_behind/pallas_call | solution.py:301
  40.2 0.1 collective-permute-start.1
  40.3 1.2 %stack_ahead.1 = (f32[128,256]{1,0:T(8,128)S(1)}, f32[128,256]{1,0:T(8,128)S(1)}) custom-call(f32[256,512]{1,0:T(8,128)S(1)} %get-tuple-element.11.white_re, f32[256,512]{1,0:T(8,128)S(1)} %get-tuple-element.12.white_im, bf16[2,512,512]{2,1,0:T(8,128)(2,1)S(1)} %copy-done.3, f32[2,128,256]{2,1,0:T(8,128)S(1)} %stack_behind.1.refs_0_), custom_call_target="tpu_custom_call" | custom-call | flops 4294967296 | bytes 16777216 | tf_op jit(solution)/shard_map/stack_ahead/pallas_call | solution.py:301
  41.5 0.3 collective-permute-done.1.received
  41.9 1.3 %collective-permute-start.4 = (f32[128,256]{1,0:T(8,128)S(1)}, f32[128,256]{1,0:T(8,128)S(1)}, u32[]{:S(2)}, u32[]{:S(2)}) collective-permute-start(f32[128,256]{1,0:T(8,128)S(1)} %get-tuple-element.16), channel_id=1, source_target_pairs={{0,2},{1,7},{2,4},{3,1},{4,6},{5,3},{6,0},{7,5},{8,10},{9,15},{10,... | collective-permute-start | bytes 393224 | tf_op jit(solution)/shard_map/ppermute | solution.py:325
  43.1 3.3 %collective-permute-start.3 = (f32[128,256]{1,0:T(8,128)S(1)}, f32[128,256]{1,0:T(8,128)S(1)}, u32[]{:S(2)}, u32[]{:S(2)}) collective-permute-start(f32[128,256]{1,0:T(8,128)S(1)} %add_passing.1.refs_0_), channel_id=1, source_target_pairs={{0,2},{1,7},{2,4},{3,1},{4,6},{5,3},{6,0},{7,5},{8,10},{9,15},{10,... | collective-permute-start | bytes 393224 | tf_op jit(solution)/shard_map/ppermute | solution.py:325
  46.4 3.4 %collective-permute-done.4.refs_0_ = f32[128,256]{1,0:T(8,128)S(1)} collective-permute-done((f32[128,256]{1,0:T(8,128)S(1)}, f32[128,256]{1,0:T(8,128)S(1)}, u32[]{:S(2)}, u32[]{:S(2)}) %collective-permute-start.4) | collective-permute-done | bytes 131104 | tf_op jit(solution)/shard_map/ppermute | solution.py:325
  49.7 0.7 %stack_here_other.1 = f32[128,256]{1,0:T(8,128)S(1)} custom-call(f32[256,512]{1,0:T(8,128)S(1)} %get-tuple-element.11.white_re, f32[256,512]{1,0:T(8,128)S(1)} %get-tuple-element.12.white_im, bf16[2,512,512]{2,1,0:T(8,128)(2,1)S(1)} %copy-done.3, f32[128,256]{1,0:T(8,128)S(1)} %collective-permute-done.4.refs_0_), custom_call_target="tpu_custom_call" | custom-call | flops 4294967296 | bytes 16777216 | tf_op jit(solution)/shard_map/stack_here_other/pallas_call | solution.py:301
  50.5 0.2 collective-permute-start.5
  50.6 0.7 %stack_here_own.1 = f32[128,256]{1,0:T(8,128)S(1)} custom-call(f32[256,512]{1,0:T(8,128)S(1)} %get-tuple-element.11.white_re, f32[256,512]{1,0:T(8,128)S(1)} %get-tuple-element.12.white_im, bf16[2,512,512]{2,1,0:T(8,128)(2,1)S(1)} %copy-done.3, f32[128,256]{1,0:T(8,128)S(1)} %add_passing.1.refs_0_), custom_call_target="tpu_custom_call" | custom-call | flops 4294967296 | bytes 16777216 | tf_op jit(solution)/shard_map/stack_here_own/pallas_call | solution.py:301
  51.4 0.6 %collective-permute-done.5 = f32[128,256]{1,0:T(8,128)S(1)} collective-permute-done((f32[128,256]{1,0:T(8,128)S(1)}, f32[128,256]{1,0:T(8,128)S(1)}, u32[]{:S(2)}, u32[]{:S(2)}) %collective-permute-start.5) | collective-permute-done | bytes 131104 | tf_op jit(solution)/shard_map/ppermute | solution.py:328
  51.9 0.7 %add_add_fusion = f32[128,256]{1,0:T(8,128)} fusion(f32[128,256]{1,0:T(8,128)S(1)} %collective-permute-done.5, f32[128,256]{1,0:T(8,128)S(1)} %stack_here_own.1, f32[128,256]{1,0:T(8,128)S(1)} %collective-permute-done.3), kind=kLoop, calls=%fused_computation | loop fusion | flops 65536 | bytes 524288 | tf_op jit(solution)/shard_map/add | solution.py:343
  (12 shorter events, 0.1 us)
Async XLA Ops:
  0.0 1.0 %copy-start = (f32[4,32,1024]{2,1,0:T(8,128)S(1)}, f32[4,32,1024]{2,1,0:T(8,128)}, u32[]{:S(2)}) copy-start(f32[4,32,1024]{2,1,0:T(8,128)} %records.3) | copy-start | bytes 1572868
  1.0 0.7 %copy-start.1 = (s32[32]{0:T(128)S(1)}, s32[32]{0:T(128)}, u32[]{:S(2)}) copy-start(s32[32]{0:T(128)} %param.5) | copy-start | bytes 388
  2.0 26.5 %copy-start.2 = (bf16[2048,512]{1,0:T(8,128)(2,1)S(1)}, bf16[2048,512]{1,0:T(8,128)(2,1)}, u32[]{:S(2)}) copy-start(bf16[2048,512]{1,0:T(8,128)(2,1)} %constant.4.clone.tables) | copy-start | bytes 6291460
  28.6 1.2 %copy-start.3 = (bf16[2,512,512]{2,1,0:T(8,128)(2,1)S(1)}, bf16[2,512,512]{2,1,0:T(8,128)(2,1)}, u32[]{:S(2)}) copy-start(bf16[2,512,512]{2,1,0:T(8,128)(2,1)} %constant.5.clone.tables) | copy-start | bytes 3145732
  30.5 3.2 %collective-permute-start = (f32[128,256]{1,0:T(8,128)S(1)}, f32[128,256]{1,0:T(8,128)S(1)}, u32[]{:S(2)}, u32[]{:S(2)}) collective-permute-start(f32[128,256]{1,0:T(8,128)S(1)} %stack_far_other.1.refs_0_), channel_id=1, source_target_pairs={{0,1},{1,0},{2,3},{3,2},{4,5},{5,4},{6,7},{7,6},{8,9},{9,8},{10,11... | collective-permute-start | bytes 393224 | tf_op jit(solution)/shard_map/ppermute | solution.py:328
  33.8 9.4 %collective-permute-start.2 = (f32[128,256]{1,0:T(8,128)S(1)}, f32[128,256]{1,0:T(8,128)S(1)}, u32[]{:S(2)}, u32[]{:S(2)}) collective-permute-start(f32[128,256]{1,0:T(8,128)S(1)} %add_far.1.refs_0_), channel_id=1, source_target_pairs={{0,2},{1,7},{2,4},{3,1},{4,6},{5,3},{6,0},{7,5},{8,10},{9,15},{10,... | collective-permute-start | bytes 393224 | tf_op jit(solution)/shard_map/ppermute | solution.py:325
  40.2 1.6 %collective-permute-start.1 = (f32[2,128,256]{2,1,0:T(8,128)S(1)}, f32[2,128,256]{2,1,0:T(8,128)S(1)}, u32[]{:S(2)}, u32[]{:S(2)}) collective-permute-start(f32[2,128,256]{2,1,0:T(8,128)S(1)} %stack_behind.1.refs_0_), channel_id=1, source_target_pairs={{0,1},{1,0},{2,3},{3,2},{4,5},{5,4},{6,7},{7,6},{8,9},{9,8},{10,11... | collective-permute-start | bytes 786440 | tf_op jit(solution)/shard_map/ppermute | solution.py:328
  41.9 7.9 %collective-permute-start.4 = (f32[128,256]{1,0:T(8,128)S(1)}, f32[128,256]{1,0:T(8,128)S(1)}, u32[]{:S(2)}, u32[]{:S(2)}) collective-permute-start(f32[128,256]{1,0:T(8,128)S(1)} %get-tuple-element.16), channel_id=1, source_target_pairs={{0,2},{1,7},{2,4},{3,1},{4,6},{5,3},{6,0},{7,5},{8,10},{9,15},{10,... | collective-permute-start | bytes 393224 | tf_op jit(solution)/shard_map/ppermute | solution.py:325
  43.1 8.2 %collective-permute-start.3 = (f32[128,256]{1,0:T(8,128)S(1)}, f32[128,256]{1,0:T(8,128)S(1)}, u32[]{:S(2)}, u32[]{:S(2)}) collective-permute-start(f32[128,256]{1,0:T(8,128)S(1)} %add_passing.1.refs_0_), channel_id=1, source_target_pairs={{0,2},{1,7},{2,4},{3,1},{4,6},{5,3},{6,0},{7,5},{8,10},{9,15},{10,... | collective-permute-start | bytes 393224 | tf_op jit(solution)/shard_map/ppermute | solution.py:325
  50.5 1.4 %collective-permute-start.5 = (f32[128,256]{1,0:T(8,128)S(1)}, f32[128,256]{1,0:T(8,128)S(1)}, u32[]{:S(2)}, u32[]{:S(2)}) collective-permute-start(f32[128,256]{1,0:T(8,128)S(1)} %add.10), channel_id=1, source_target_pairs={{0,1},{1,0},{2,3},{3,2},{4,5},{5,4},{6,7},{7,6},{8,9},{9,8},{10,11... | collective-permute-start | bytes 393224 | tf_op jit(solution)/shard_map/ppermute | solution.py:328

commit v7 on v6

--- a/solution.py
+++ b/solution.py
@@ -324,6 +324,10 @@
         pairs = [(i, (i + (2 if i % 2 == 0 else -2)) % 8) for i in range(8)]
         return lax.ppermute(value, "win", pairs)
 
+    def onward_other(value):
+        pairs = [(i, (i + (3 if i % 2 == 0 else -3)) % 8) for i in range(8)]
+        return lax.ppermute(value, "win", pairs)
+
     def across(value):
         return lax.ppermute(value, "win", [(i, i ^ 1) for i in range(8)])
 
@@ -334,13 +338,12 @@
     (behind,) = stack("behind", after=far)
     own, other = stack("ahead", after=behind)
     own, other = small(join_kernel, 2, "join", own, other, across(behind))
-    early = onward(other)
+    early = onward_other(other)
     (own,) = small(add_kernel, 1, "add_passing", own, passing)
     late = onward(own)
-    (here_own,) = stack("here_own", after=own)
-    (here_other,) = stack("here_other", after=early)
-    turned = across(here_other + early)
-    result = (here_own + late) + turned
+    (here_other,) = stack("here_other", after=other)
+    (here_own,) = stack("here_own", after=here_other)
+    result = (here_own + across(here_other)) + (early + late)
     return jnp.transpose(result.reshape(4, 32, lag_count), (0, 2, 1))
 
 

time: 52.8 us -> 52.9 us (level)
  waiting for transfers between devices: 4.48 us -> 5.14 us
    ppermute x3 -> x2, starting transfers between devices: 9.72 us -> 7.31 us  [onward(): return lax.ppermute(value, 'win', pairs)]
    ppermute x0 -> x1, starting transfers between devices: none -> 1.38 us  [onward_other(): return lax.ppermute(value, 'win', pairs)]
    ppermute x3 -> x2, waiting for transfers between devices: 3.36 us -> 4.57 us  [onward(): return lax.ppermute(value, 'win', pairs)]
    ppermute x3, waiting for transfers between devices: 1.12 us -> 0.57 us  [across(): return lax.ppermute(value, 'win', [(i, i ^ 1) for i in range(8)])]
  transfers between devices with their start and end apart: 6 -> 6, of which waited for: 4 -> 3; matrix products, arithmetic and copies ran while one was open for 0% -> 0% of each run, Pallas kernels for 9% -> 9%
where the time goes in v7:
time: 52.9 us; the launch traced here: 52.7 us
  blocking collectives  25.8 us (49%)
  starting transfers between devices  11.7 us (22%)
  Pallas kernels  7.99 us (15%)
  waiting for transfers between devices  5.14 us (10%)
  local copies, waits for them, and re-layouts  1.23 us (2%)
  other arithmetic  0.69 us (1%)
    all_to_all x1, blocking collectives, local(): blocks = lax.all_to_all(packed, 'chan', 0, 0, tiled=True)  25.8 us
    ppermute x2, starting transfers between devices, onward(): return lax.ppermute(value, 'win', pairs)  7.31 us
    pallas_call x6, Pallas kernels, stack(): pl.pallas_call(functools.partial(stack_kernel, kind), out_shape=outs, in_...  5.25 us
    ppermute x2, waiting for transfers between devices, onward(): return lax.ppermute(value, 'win', pairs)  4.57 us
    ppermute x3, starting transfers between devices, across(): return lax.ppermute(value, 'win', [(i, i ^ 1) for i in range(8)])  2.98 us
    ppermute x1, starting transfers between devices, onward_other(): return lax.ppermute(value, 'win', pairs)  1.38 us
    unnamed x8, local copies, waits for them, and re-layouts  1.23 us
    pallas_call x1, Pallas kernels, local(): pl.pallas_call(spectra_kernel, out_shape=(shape((rows, half), F32), shape...  1.22 us
  transfers between devices with their start and end apart: 6, of which 3 were waited for; matrix products, arithmetic and copies ran while one was open for 0% of the time, Pallas kernels for 9%

profile of v7, /device:TPU:1, one launch (start us, length us, event | category | flops | bytes accessed | tf_op | source)
XLA Modules:
  0.0 52.7 jit_solution(2227132203174444683)
XLA Ops:
  0.0 1.0 %copy-done = f32[4,32,1024]{2,1,0:T(8,128)S(1)} copy-done((f32[4,32,1024]{2,1,0:T(8,128)S(1)}, f32[4,32,1024]{2,1,0:T(8,128)}, u32[]{:S(2)}) %copy-start) | copy-done | bytes 524312
  1.0 0.5 pack.1.packed_in
  1.5 0.2 copy-done.1
  1.7 0.3 pick.1
  2.0 0.0 copy-start.2
  2.0 25.8 %all_to_all.5.blocks = f32[32,64,128]{2,1,0:T(8,128)S(1)} all-to-all(f32[32,64,128]{2,1,0:T(8,128)S(1)} %pick.1), channel_id=1, replica_groups=mesh['chan'=32,'win'=8] {'chan'}, dimensions={0} | all-to-all | bytes 2097152 | tf_op jit(solution)/shard_map/all_to_all | solution.py:259
  27.9 0.7 %level.1.turned = f32[256,1024]{1,0:T(8,128)S(1)} custom-call(f32[32,64,128]{2,1,0:T(8,128)S(1)} %all_to_all.5.blocks), custom_call_target="tpu_custom_call" | custom-call | flops 268435456 | bytes 1048576 | tf_op jit(solution)/shard_map/level/pallas_call | solution.py:265
  28.6 1.2 %spectra.1 = (f32[256,512]{1,0:T(8,128)S(1)}, f32[256,512]{1,0:T(8,128)S(1)}) custom-call(f32[256,1024]{1,0:T(8,128)S(1)} %level.1.turned, bf16[2048,512]{1,0:T(8,128)(2,1)S(1)} %copy-done.2), custom_call_target="tpu_custom_call" | custom-call | flops 4294967296 | bytes 16777216 | tf_op jit(solution)/shard_map/spectra/pallas_call | solution.py:274
  29.8 0.7 %stack_far_other.1.refs_0_ = f32[128,256]{1,0:T(8,128)S(1)} custom-call(f32[256,512]{1,0:T(8,128)S(1)} %get-tuple-element.11.white_re, f32[256,512]{1,0:T(8,128)S(1)} %get-tuple-element.12.white_im, bf16[2,512,512]{2,1,0:T(8,128)(2,1)S(1)} %copy-done.3), custom_call_target="tpu_custom_call" | custom-call | flops 4294967296 | bytes 16777216 | tf_op jit(solution)/shard_map/stack_far_other/pallas_call | solution.py:301
  30.5 2.2 %collective-permute-start = (f32[128,256]{1,0:T(8,128)S(1)}, f32[128,256]{1,0:T(8,128)S(1)}, u32[]{:S(2)}, u32[]{:S(2)}) collective-permute-start(f32[128,256]{1,0:T(8,128)S(1)} %stack_far_other.1.refs_0_), channel_id=1, source_target_pairs={{0,1},{1,0},{2,3},{3,2},{4,5},{5,4},{6,7},{7,6},{8,9},{9,8},{10,11... | collective-permute-start | bytes 393224 | tf_op jit(solution)/shard_map/ppermute | solution.py:332
  32.8 0.7 %stack_far_own.1.refs_0_ = f32[128,256]{1,0:T(8,128)S(1)} custom-call(f32[256,512]{1,0:T(8,128)S(1)} %get-tuple-element.11.white_re, f32[256,512]{1,0:T(8,128)S(1)} %get-tuple-element.12.white_im, bf16[2,512,512]{2,1,0:T(8,128)(2,1)S(1)} %copy-done.3, f32[128,256]{1,0:T(8,128)S(1)} %stack_far_other.1.refs_0_), custom_call_target="tpu_custom_call" | custom-call | flops 4294967296 | bytes 16777216 | tf_op jit(solution)/shard_map/stack_far_own/pallas_call | solution.py:301
  33.4 0.3 collective-permute-done.refs_1_
  33.8 5.2 %collective-permute-start.4 = (f32[128,256]{1,0:T(8,128)S(1)}, f32[128,256]{1,0:T(8,128)S(1)}, u32[]{:S(2)}, u32[]{:S(2)}) collective-permute-start(f32[128,256]{1,0:T(8,128)S(1)} %add_far.1.refs_0_), channel_id=1, source_target_pairs={{0,2},{1,7},{2,4},{3,1},{4,6},{5,3},{6,0},{7,5},{8,10},{9,15},{10,... | collective-permute-start | bytes 393224 | tf_op jit(solution)/shard_map/ppermute | solution.py:325
  39.0 1.2 %stack_behind.1.refs_0_ = f32[2,128,256]{2,1,0:T(8,128)S(1)} custom-call(f32[256,512]{1,0:T(8,128)S(1)} %get-tuple-element.11.white_re, f32[256,512]{1,0:T(8,128)S(1)} %get-tuple-element.12.white_im, bf16[2,512,512]{2,1,0:T(8,128)(2,1)S(1)} %copy-done.3, f32[128,256]{1,0:T(8,128)S(1)} %add_far.1.refs_0_), custom_call_target="tpu_custom_call" | custom-call | flops 4294967296 | bytes 16777216 | tf_op jit(solution)/shard_map/stack_behind/pallas_call | solution.py:301
  40.2 0.1 collective-permute-start.1
  40.3 1.2 %stack_ahead.1 = (f32[128,256]{1,0:T(8,128)S(1)}, f32[128,256]{1,0:T(8,128)S(1)}) custom-call(f32[256,512]{1,0:T(8,128)S(1)} %get-tuple-element.11.white_re, f32[256,512]{1,0:T(8,128)S(1)} %get-tuple-element.12.white_im, bf16[2,512,512]{2,1,0:T(8,128)(2,1)S(1)} %copy-done.3, f32[2,128,256]{2,1,0:T(8,128)S(1)} %stack_behind.1.refs_0_), custom_call_target="tpu_custom_call" | custom-call | flops 4294967296 | bytes 16777216 | tf_op jit(solution)/shard_map/stack_ahead/pallas_call | solution.py:301
  41.5 0.3 collective-permute-done.1.received
  41.9 0.7 %stack_here_other.1.refs_0_ = f32[128,256]{1,0:T(8,128)S(1)} custom-call(f32[256,512]{1,0:T(8,128)S(1)} %get-tuple-element.11.white_re, f32[256,512]{1,0:T(8,128)S(1)} %get-tuple-element.12.white_im, bf16[2,512,512]{2,1,0:T(8,128)(2,1)S(1)} %copy-done.3, f32[128,256]{1,0:T(8,128)S(1)} %get-tuple-element.15.refs_0_), custom_call_target="tpu_custom_call" | custom-call | flops 4294967296 | bytes 16777216 | tf_op jit(solution)/shard_map/stack_here_other/pallas_call | solution.py:301
  42.5 1.4 %collective-permute-start.3 = (f32[128,256]{1,0:T(8,128)S(1)}, f32[128,256]{1,0:T(8,128)S(1)}, u32[]{:S(2)}, u32[]{:S(2)}) collective-permute-start(f32[128,256]{1,0:T(8,128)S(1)} %get-tuple-element.15.refs_0_), channel_id=1, source_target_pairs={{0,3},{1,6},{2,5},{3,0},{4,7},{5,2},{6,1},{7,4},{8,11},{9,14},{10,... | collective-permute-start | bytes 393224 | tf_op jit(solution)/shard_map/ppermute | solution.py:329
  43.9 0.6 %collective-permute-start.2 = (f32[128,256]{1,0:T(8,128)S(1)}, f32[128,256]{1,0:T(8,128)S(1)}, u32[]{:S(2)}, u32[]{:S(2)}) collective-permute-start(f32[128,256]{1,0:T(8,128)S(1)} %stack_here_other.1.refs_0_), channel_id=1, source_target_pairs={{0,1},{1,0},{2,3},{3,2},{4,5},{5,4},{6,7},{7,6},{8,9},{9,8},{10,11... | collective-permute-start | bytes 393224 | tf_op jit(solution)/shard_map/ppermute | solution.py:332
  44.6 2.1 %collective-permute-start.5 = (f32[128,256]{1,0:T(8,128)S(1)}, f32[128,256]{1,0:T(8,128)S(1)}, u32[]{:S(2)}, u32[]{:S(2)}) collective-permute-start(f32[128,256]{1,0:T(8,128)S(1)} %add_passing.1), channel_id=1, source_target_pairs={{0,2},{1,7},{2,4},{3,1},{4,6},{5,3},{6,0},{7,5},{8,10},{9,15},{10,... | collective-permute-start | bytes 393224 | tf_op jit(solution)/shard_map/ppermute | solution.py:325
  46.7 0.7 %stack_here_own.1 = f32[128,256]{1,0:T(8,128)S(1)} custom-call(f32[256,512]{1,0:T(8,128)S(1)} %get-tuple-element.11.white_re, f32[256,512]{1,0:T(8,128)S(1)} %get-tuple-element.12.white_im, bf16[2,512,512]{2,1,0:T(8,128)(2,1)S(1)} %copy-done.3, f32[128,256]{1,0:T(8,128)S(1)} %stack_here_other.1.refs_0_), custom_call_target="tpu_custom_call" | custom-call | flops 4294967296 | bytes 16777216 | tf_op jit(solution)/shard_map/stack_here_own/pallas_call | solution.py:301
  47.4 4.6 %collective-permute-done.5 = f32[128,256]{1,0:T(8,128)S(1)} collective-permute-done((f32[128,256]{1,0:T(8,128)S(1)}, f32[128,256]{1,0:T(8,128)S(1)}, u32[]{:S(2)}, u32[]{:S(2)}) %collective-permute-start.5) | collective-permute-done | bytes 131104 | tf_op jit(solution)/shard_map/ppermute | solution.py:325
  52.0 0.7 %add_add_fusion = f32[128,256]{1,0:T(8,128)} fusion(f32[128,256]{1,0:T(8,128)S(1)} %collective-permute-done.3, f32[128,256]{1,0:T(8,128)S(1)} %collective-permute-done.5, f32[128,256]{1,0:T(8,128)S(1)} %stack_here_own.1, f32[128,256]{1,0:T(8,128)S(1)} %collective-permute-done.2), kind=kLoop, calls=%fused_computation | loop fusion | flops 98304 | bytes 655360 | tf_op jit(solution)/shard_map/add | solution.py:346
  (11 shorter events, 0.1 us)
Async XLA Ops:
  0.0 1.0 %copy-start = (f32[4,32,1024]{2,1,0:T(8,128)S(1)}, f32[4,32,1024]{2,1,0:T(8,128)}, u32[]{:S(2)}) copy-start(f32[4,32,1024]{2,1,0:T(8,128)} %records.3) | copy-start | bytes 1572868
  1.0 0.7 %copy-start.1 = (s32[32]{0:T(128)S(1)}, s32[32]{0:T(128)}, u32[]{:S(2)}) copy-start(s32[32]{0:T(128)} %param.5) | copy-start | bytes 388
  2.0 26.5 %copy-start.2 = (bf16[2048,512]{1,0:T(8,128)(2,1)S(1)}, bf16[2048,512]{1,0:T(8,128)(2,1)}, u32[]{:S(2)}) copy-start(bf16[2048,512]{1,0:T(8,128)(2,1)} %constant.4.clone.tables) | copy-start | bytes 6291460
  28.6 1.2 %copy-start.3 = (bf16[2,512,512]{2,1,0:T(8,128)(2,1)S(1)}, bf16[2,512,512]{2,1,0:T(8,128)(2,1)}, u32[]{:S(2)}) copy-start(bf16[2,512,512]{2,1,0:T(8,128)(2,1)} %constant.5.clone.tables) | copy-start | bytes 3145732
  30.5 3.2 %collective-permute-start = (f32[128,256]{1,0:T(8,128)S(1)}, f32[128,256]{1,0:T(8,128)S(1)}, u32[]{:S(2)}, u32[]{:S(2)}) collective-permute-start(f32[128,256]{1,0:T(8,128)S(1)} %stack_far_other.1.refs_0_), channel_id=1, source_target_pairs={{0,1},{1,0},{2,3},{3,2},{4,5},{5,4},{6,7},{7,6},{8,9},{9,8},{10,11... | collective-permute-start | bytes 393224 | tf_op jit(solution)/shard_map/ppermute | solution.py:332
  33.8 10.8 %collective-permute-start.4 = (f32[128,256]{1,0:T(8,128)S(1)}, f32[128,256]{1,0:T(8,128)S(1)}, u32[]{:S(2)}, u32[]{:S(2)}) collective-permute-start(f32[128,256]{1,0:T(8,128)S(1)} %add_far.1.refs_0_), channel_id=1, source_target_pairs={{0,2},{1,7},{2,4},{3,1},{4,6},{5,3},{6,0},{7,5},{8,10},{9,15},{10,... | collective-permute-start | bytes 393224 | tf_op jit(solution)/shard_map/ppermute | solution.py:325
  40.2 1.6 %collective-permute-start.1 = (f32[2,128,256]{2,1,0:T(8,128)S(1)}, f32[2,128,256]{2,1,0:T(8,128)S(1)}, u32[]{:S(2)}, u32[]{:S(2)}) collective-permute-start(f32[2,128,256]{2,1,0:T(8,128)S(1)} %stack_behind.1.refs_0_), channel_id=1, source_target_pairs={{0,1},{1,0},{2,3},{3,2},{4,5},{5,4},{6,7},{7,6},{8,9},{9,8},{10,11... | collective-permute-start | bytes 786440 | tf_op jit(solution)/shard_map/ppermute | solution.py:332
  42.5 9.4 %collective-permute-start.3 = (f32[128,256]{1,0:T(8,128)S(1)}, f32[128,256]{1,0:T(8,128)S(1)}, u32[]{:S(2)}, u32[]{:S(2)}) collective-permute-start(f32[128,256]{1,0:T(8,128)S(1)} %get-tuple-element.15.refs_0_), channel_id=1, source_target_pairs={{0,3},{1,6},{2,5},{3,0},{4,7},{5,2},{6,1},{7,4},{8,11},{9,14},{10,... | collective-permute-start | bytes 393224 | tf_op jit(solution)/shard_map/ppermute | solution.py:329
  43.9 3.5 %collective-permute-start.2 = (f32[128,256]{1,0:T(8,128)S(1)}, f32[128,256]{1,0:T(8,128)S(1)}, u32[]{:S(2)}, u32[]{:S(2)}) collective-permute-start(f32[128,256]{1,0:T(8,128)S(1)} %stack_here_other.1.refs_0_), channel_id=1, source_target_pairs={{0,1},{1,0},{2,3},{3,2},{4,5},{5,4},{6,7},{7,6},{8,9},{9,8},{10,11... | collective-permute-start | bytes 393224 | tf_op jit(solution)/shard_map/ppermute | solution.py:332
  44.6 7.4 %collective-permute-start.5 = (f32[128,256]{1,0:T(8,128)S(1)}, f32[128,256]{1,0:T(8,128)S(1)}, u32[]{:S(2)}, u32[]{:S(2)}) collective-permute-start(f32[128,256]{1,0:T(8,128)S(1)} %add_passing.1), channel_id=1, source_target_pairs={{0,2},{1,7},{2,4},{3,1},{4,6},{5,3},{6,0},{7,5},{8,10},{9,15},{10,... | collective-permute-start | bytes 393224 | tf_op jit(solution)/shard_map/ppermute | solution.py:325

commit v8 on v7

--- a/solution.py
+++ b/solution.py
@@ -194,37 +194,23 @@
     white_im[...] = im * gain
 
 
-def stack_kernel(kind, white_re, white_im, tables, *refs):
+def stack_kernel(parts, white_re, white_im, tables, *refs):
+    result, cross_high, cross_low = refs[-3:]
     win = lax.axis_index("win")
     z_hi, core = lax.div(win, 2), lax.rem(win, 2)
-    if kind.startswith(("far", "here")):
-        result, cross_high, cross_low = refs[-3:]
-        which = core if kind.endswith("own") else 1 - core
-        target = lax.rem(z_hi + (2 if kind.startswith("far") else 0), 4)
-        correlate(white_re, white_im, cross_high, cross_low, target, 32, which)
-        result[...] = invert(cross_high, cross_low, tables)
-        return
-    cross_high, cross_low, both = refs[-3:]
-    step = {"ahead": 1 + 2 * core, "behind": 3 - 2 * core}[kind]
-    correlate(white_re, white_im, cross_high, cross_low, lax.rem(z_hi + step, 4), 32)
-    both[...] = invert(cross_high, cross_low, tables).reshape(both.shape)
-    if kind == "behind":
-        refs[-4][0] = both[1 - core]
-        refs[-4][1] = both[core]
-    else:
-        refs[-5][...] = both[core]
-        refs[-4][...] = both[1 - core]
+    for n, (step, own) in enumerate(parts):
+        step = {"here": 0, "ahead": 1 + 2 * core, "far": 2, "behind": 3 - 2 * core}[step]
+        target = lax.rem(z_hi + step, 4)
+        high, low = cross_high.at[n], cross_low.at[n]
+        correlate(white_re, white_im, high, low, target, 32, core if own else 1 - core)
+        result[n] = invert(high, low, tables)
 
 
 def add_kernel(*refs):
-    half = len(refs) // 3
-    for left, right, out in zip(refs[:half], refs[half : 2 * half], refs[2 * half :]):
-        out[...] = left[...] + right[...]
-
-
-def join_kernel(own, other, received, own_sum, other_sum):
-    own_sum[...] = own[...] + received[0]
-    other_sum[...] = other[...] + received[1]
+    total = refs[0][0]
+    for ref in refs[1:-1]:
+        total = total + (ref[0] if len(ref.shape) == 3 else ref[...])
+    refs[-1][...] = total
 
 
 def local(records, sources):
@@ -283,39 +269,26 @@
 
     piece = shape((LANES, lag_count), F32)
 
-    def stack(kind, after=None, handed=None):
+    def stack(*parts, after=None):
         extra = [] if after is None else [after]
-        outs = {
-            "behind": [shape((2, LANES, lag_count), F32)],
-            "ahead": [piece, piece],
-        }.get(kind, [piece])
-        rows = 2 * LANES if kind in ("behind", "ahead") else LANES
-        scratch = [pltpu.VMEM((rows, length), BF16), pltpu.VMEM((rows, length), BF16)]
-        if rows > LANES:
-            scratch.append(pltpu.VMEM((2, LANES, lag_count), F32))
-        aliases = {}
-        if handed is not None:
-            aliases = {3 + len(extra): 0}
-            extra.append(handed)
-            outs.insert(0, shape(handed.shape, F32))
+        count = len(parts)
         return pl.pallas_call(
-            functools.partial(stack_kernel, kind),
-            out_shape=outs,
+            functools.partial(stack_kernel, parts),
+            out_shape=shape((count, LANES, lag_count), F32),
             in_specs=[vmem] * (3 + len(extra)),
-            out_specs=[vmem] * len(outs),
-            scratch_shapes=scratch,
-            input_output_aliases=aliases,
+            out_specs=vmem,
+            scratch_shapes=[pltpu.VMEM((count, LANES, length), BF16)] * 2,
             compiler_params=pltpu.CompilerParams(vmem_limit_bytes=16 << 20),
-            cost_estimate=pl.CostEstimate(flops=1 << 32, bytes_accessed=1 << 24, transcendentals=0),
-            name="stack_" + kind,
+            cost_estimate=pl.CostEstimate(flops=count << 32, bytes_accessed=1, transcendentals=0),
+            name="stack_" + "_".join(step for step, _ in parts),
         )(white_re, white_im, inverse, *extra)
 
-    def small(kernel, outs, name, *operands):
+    def add(name, *operands):
         return pl.pallas_call(
-            kernel,
-            out_shape=[piece] * outs,
+            add_kernel,
+            out_shape=piece,
             in_specs=[vmem] * len(operands),
-            out_specs=[vmem] * outs,
+            out_specs=vmem,
             compiler_params=pltpu.CompilerParams(vmem_limit_bytes=4 << 20),
             name=name,
         )(*operands)
@@ -331,19 +304,21 @@
     def across(value):
         return lax.ppermute(value, "win", [(i, i ^ 1) for i in range(8)])
 
-    (send_far,) = stack("far_other")
-    (keep_far,) = stack("far_own", after=send_far)
-    (far,) = small(add_kernel, 1, "add_far", keep_far, across(send_far))
+    far_other = stack(("far", False))
+    far_own = stack(("far", True), after=far_other)
+    far = add("add_far", far_own, across(far_other))
     passing = onward(far)
-    (behind,) = stack("behind", after=far)
-    own, other = stack("ahead", after=behind)
-    own, other = small(join_kernel, 2, "join", own, other, across(behind))
+    behind_own = stack(("behind", True), after=far)
+    ahead_other = stack(("ahead", False), after=behind_own)
+    other = add("add_other", ahead_other, across(behind_own))
     early = onward_other(other)
-    (own,) = small(add_kernel, 1, "add_passing", own, passing)
+    rest = stack(("behind", False), ("here", False), after=other)
+    ahead_own = stack(("ahead", True), after=rest)
+    rest = across(rest)
+    own = add("add_own", ahead_own, rest, passing)
     late = onward(own)
-    (here_other,) = stack("here_other", after=other)
-    (here_own,) = stack("here_own", after=here_other)
-    result = (here_own + across(here_other)) + (early + late)
+    here_own = stack(("here", True), after=own)
+    result = (here_own[0] + rest[1]) + (early + late)
     return jnp.transpose(result.reshape(4, 32, lag_count), (0, 2, 1))
 
 

time: 52.9 us -> 52.2 us (0.987)
  waiting for transfers between devices: 5.14 us -> 3.43 us
  starting transfers between devices: 11.7 us -> 12.6 us
    ppermute x2, starting transfers between devices: 7.31 us -> 9.29 us  [onward(): return lax.ppermute(value, 'win', pairs)]
    ppermute x2, waiting for transfers between devices: 4.57 us -> 3.13 us  [onward(): return lax.ppermute(value, 'win', pairs)]
    ppermute x1, starting transfers between devices: 1.38 us -> 0.54 us  [onward_other(): return lax.ppermute(value, 'win', pairs)]
    pallas_call x9 -> x10, Pallas kernels: 5.3 us -> 5.35 us  [the longest x7 5.3 us: stack(): pl.pallas_call(functools.partial(stack_kernel, parts), out_shape=shape((c...]
  transfers between devices with their start and end apart: 6 -> 6, of which waited for: 3 -> 3; matrix products, arithmetic and copies ran while one was open for 0% -> 0% of each run, Pallas kernels for 9% -> 8%
where the time goes in v8:
time: 52.2 us; the launch traced here: 52 us
  blocking collectives  25.8 us (49%)
  starting transfers between devices  12.6 us (24%)
  Pallas kernels  8.04 us (15%)
  waiting for transfers between devices  3.43 us (7%)
  local copies, waits for them, and re-layouts  1.23 us (2%)
  other arithmetic  0.69 us (1%)
    all_to_all x1, blocking collectives, local(): blocks = lax.all_to_all(packed, 'chan', 0, 0, tiled=True)  25.8 us
    ppermute x2, starting transfers between devices, onward(): return lax.ppermute(value, 'win', pairs)  9.29 us
    pallas_call x7, Pallas kernels, stack(): pl.pallas_call(functools.partial(stack_kernel, parts), out_shape=shape((c...  5.3 us
    ppermute x2, waiting for transfers between devices, onward(): return lax.ppermute(value, 'win', pairs)  3.13 us
    ppermute x3, starting transfers between devices, across(): return lax.ppermute(value, 'win', [(i, i ^ 1) for i in range(8)])  2.79 us
    unnamed x8, local copies, waits for them, and re-layouts  1.23 us
    pallas_call x1, Pallas kernels, local(): pl.pallas_call(spectra_kernel, out_shape=(shape((rows, half), F32), shape...  1.22 us
  transfers between devices with their start and end apart: 6, of which 3 were waited for; matrix products, arithmetic and copies ran while one was open for 0% of the time, Pallas kernels for 8%

profile of v8, /device:TPU:1, one launch (start us, length us, event | category | flops | bytes accessed | tf_op | source)
XLA Modules:
  0.0 52.0 jit_solution(18337122272139578030)
XLA Ops:
  0.0 1.0 %copy-done = f32[4,32,1024]{2,1,0:T(8,128)S(1)} copy-done((f32[4,32,1024]{2,1,0:T(8,128)S(1)}, f32[4,32,1024]{2,1,0:T(8,128)}, u32[]{:S(2)}) %copy-start) | copy-done | bytes 524312
  1.0 0.5 pack.1.packed_in
  1.5 0.2 copy-done.1
  1.7 0.3 pick.1
  2.0 25.8 %all_to_all.5.blocks = f32[32,64,128]{2,1,0:T(8,128)S(1)} all-to-all(f32[32,64,128]{2,1,0:T(8,128)S(1)} %pick.1), channel_id=1, replica_groups=mesh['chan'=32,'win'=8] {'chan'}, dimensions={0} | all-to-all | bytes 2097152 | tf_op jit(solution)/shard_map/all_to_all | solution.py:245
  27.9 0.7 %level.1.turned = f32[256,1024]{1,0:T(8,128)S(1)} custom-call(f32[32,64,128]{2,1,0:T(8,128)S(1)} %all_to_all.5.blocks), custom_call_target="tpu_custom_call" | custom-call | flops 268435456 | bytes 1048576 | tf_op jit(solution)/shard_map/level/pallas_call | solution.py:251
  28.6 1.2 %spectra.1 = (f32[256,512]{1,0:T(8,128)S(1)}, f32[256,512]{1,0:T(8,128)S(1)}) custom-call(f32[256,1024]{1,0:T(8,128)S(1)} %level.1.turned, bf16[2048,512]{1,0:T(8,128)(2,1)S(1)} %copy-done.2), custom_call_target="tpu_custom_call" | custom-call | flops 4294967296 | bytes 16777216 | tf_op jit(solution)/shard_map/spectra/pallas_call | solution.py:260
  29.8 0.7 %stack_far.2.refs_0_ = f32[1,128,256]{2,1,0:T(8,128)S(1)} custom-call(f32[256,512]{1,0:T(8,128)S(1)} %get-tuple-element.7.white_re, f32[256,512]{1,0:T(8,128)S(1)} %get-tuple-element.8.white_im, bf16[2,512,512]{2,1,0:T(8,128)(2,1)S(1)} %copy-done.3), custom_call_target="tpu_custom_call" | custom-call | flops 4294967296 | bytes 1 | tf_op jit(solution)/shard_map/stack_far/pallas_call | solution.py:275
  30.5 2.2 %collective-permute-start = (f32[1,128,256]{2,1,0:T(8,128)S(1)}, f32[1,128,256]{2,1,0:T(8,128)S(1)}, u32[]{:S(2)}, u32[]{:S(2)}) collective-permute-start(f32[1,128,256]{2,1,0:T(8,128)S(1)} %stack_far.2.refs_0_), channel_id=1, source_target_pairs={{0,1},{1,0},{2,3},{3,2},{4,5},{5,4},{6,7},{7,6},{8,9},{9,8},{10,11... | collective-permute-start | bytes 393224 | tf_op jit(solution)/shard_map/ppermute | solution.py:305
  32.8 0.7 %stack_far.3.refs_0_ = f32[1,128,256]{2,1,0:T(8,128)S(1)} custom-call(f32[256,512]{1,0:T(8,128)S(1)} %get-tuple-element.7.white_re, f32[256,512]{1,0:T(8,128)S(1)} %get-tuple-element.8.white_im, bf16[2,512,512]{2,1,0:T(8,128)(2,1)S(1)} %copy-done.3, f32[1,128,256]{2,1,0:T(8,128)S(1)} %stack_far.2.refs_0_), custom_call_target="tpu_custom_call" | custom-call | flops 4294967296 | bytes 1 | tf_op jit(solution)/shard_map/stack_far/pallas_call | solution.py:275
  33.4 0.3 collective-permute-done.refs_1_
  33.8 0.7 %stack_behind.1.refs_0_ = f32[1,128,256]{2,1,0:T(8,128)S(1)} custom-call(f32[256,512]{1,0:T(8,128)S(1)} %get-tuple-element.7.white_re, f32[256,512]{1,0:T(8,128)S(1)} %get-tuple-element.8.white_im, bf16[2,512,512]{2,1,0:T(8,128)(2,1)S(1)} %copy-done.3, f32[128,256]{1,0:T(8,128)S(1)} %add_far.1.refs_0_), custom_call_target="tpu_custom_call" | custom-call | flops 4294967296 | bytes 1 | tf_op jit(solution)/shard_map/stack_behind/pallas_call | solution.py:275
  34.5 0.4 collective-permute-start.1
  34.9 0.7 %stack_ahead.2.refs_0_ = f32[1,128,256]{2,1,0:T(8,128)S(1)} custom-call(f32[256,512]{1,0:T(8,128)S(1)} %get-tuple-element.7.white_re, f32[256,512]{1,0:T(8,128)S(1)} %get-tuple-element.8.white_im, bf16[2,512,512]{2,1,0:T(8,128)(2,1)S(1)} %copy-done.3, f32[1,128,256]{2,1,0:T(8,128)S(1)} %stack_behind.1.refs_0_), custom_call_target="tpu_custom_call" | custom-call | flops 4294967296 | bytes 1 | tf_op jit(solution)/shard_map/stack_ahead/pallas_call | solution.py:275
  35.6 5.2 %collective-permute-start.3 = (f32[128,256]{1,0:T(8,128)S(1)}, f32[128,256]{1,0:T(8,128)S(1)}, u32[]{:S(2)}, u32[]{:S(2)}) collective-permute-start(f32[128,256]{1,0:T(8,128)S(1)} %add_far.1.refs_0_), channel_id=1, source_target_pairs={{0,2},{1,7},{2,4},{3,1},{4,6},{5,3},{6,0},{7,5},{8,10},{9,15},{10,... | collective-permute-start | bytes 393224 | tf_op jit(solution)/shard_map/ppermute | solution.py:298
  40.8 0.5 %collective-permute-start.4 = (f32[128,256]{1,0:T(8,128)S(1)}, f32[128,256]{1,0:T(8,128)S(1)}, u32[]{:S(2)}, u32[]{:S(2)}) collective-permute-start(f32[128,256]{1,0:T(8,128)S(1)} %add_other.1.refs_0_), channel_id=1, source_target_pairs={{0,3},{1,6},{2,5},{3,0},{4,7},{5,2},{6,1},{7,4},{8,11},{9,14},{10,... | collective-permute-start | bytes 393224 | tf_op jit(solution)/shard_map/ppermute | solution.py:302
  41.4 1.2 %stack_behind_here.1.refs_0_ = f32[2,128,256]{2,1,0:T(8,128)S(1)} custom-call(f32[256,512]{1,0:T(8,128)S(1)} %get-tuple-element.7.white_re, f32[256,512]{1,0:T(8,128)S(1)} %get-tuple-element.8.white_im, bf16[2,512,512]{2,1,0:T(8,128)(2,1)S(1)} %copy-done.3, f32[128,256]{1,0:T(8,128)S(1)} %add_other.1.refs_0_), custom_call_target="tpu_custom_call" | custom-call | flops 8589934592 | bytes 1 | tf_op jit(solution)/shard_map/stack_behind_here/pallas_call | solution.py:275
  42.5 0.1 collective-permute-start.2
  42.6 0.7 %stack_ahead.3.refs_0_ = f32[1,128,256]{2,1,0:T(8,128)S(1)} custom-call(f32[256,512]{1,0:T(8,128)S(1)} %get-tuple-element.7.white_re, f32[256,512]{1,0:T(8,128)S(1)} %get-tuple-element.8.white_im, bf16[2,512,512]{2,1,0:T(8,128)(2,1)S(1)} %copy-done.3, f32[2,128,256]{2,1,0:T(8,128)S(1)} %stack_behind_here.1.refs_0_), custom_call_target="tpu_custom_call" | custom-call | flops 4294967296 | bytes 1 | tf_op jit(solution)/shard_map/stack_ahead/pallas_call | solution.py:275
  43.3 0.9 %collective-permute-done.3.refs_2_ = f32[128,256]{1,0:T(8,128)S(1)} collective-permute-done((f32[128,256]{1,0:T(8,128)S(1)}, f32[128,256]{1,0:T(8,128)S(1)}, u32[]{:S(2)}, u32[]{:S(2)}) %collective-permute-start.3) | collective-permute-done | bytes 131104 | tf_op jit(solution)/shard_map/ppermute | solution.py:298
  44.2 4.1 %collective-permute-start.5 = (f32[128,256]{1,0:T(8,128)S(1)}, f32[128,256]{1,0:T(8,128)S(1)}, u32[]{:S(2)}, u32[]{:S(2)}) collective-permute-start(f32[128,256]{1,0:T(8,128)S(1)} %add_own.1.refs_0_), channel_id=1, source_target_pairs={{0,2},{1,7},{2,4},{3,1},{4,6},{5,3},{6,0},{7,5},{8,10},{9,15},{10,... | collective-permute-start | bytes 393224 | tf_op jit(solution)/shard_map/ppermute | solution.py:298
  48.3 0.7 %stack_here.1 = f32[1,128,256]{2,1,0:T(8,128)S(1)} custom-call(f32[256,512]{1,0:T(8,128)S(1)} %get-tuple-element.7.white_re, f32[256,512]{1,0:T(8,128)S(1)} %get-tuple-element.8.white_im, bf16[2,512,512]{2,1,0:T(8,128)(2,1)S(1)} %copy-done.3, f32[128,256]{1,0:T(8,128)S(1)} %add_own.1.refs_0_), custom_call_target="tpu_custom_call" | custom-call | flops 4294967296 | bytes 1 | tf_op jit(solution)/shard_map/stack_here/pallas_call | solution.py:275
  49.0 2.2 %collective-permute-done.5 = f32[128,256]{1,0:T(8,128)S(1)} collective-permute-done((f32[128,256]{1,0:T(8,128)S(1)}, f32[128,256]{1,0:T(8,128)S(1)}, u32[]{:S(2)}, u32[]{:S(2)}) %collective-permute-start.5) | collective-permute-done | bytes 131104 | tf_op jit(solution)/shard_map/ppermute | solution.py:298
  51.3 0.7 %fusion.1 = f32[128,256]{1,0:T(8,128)} fusion(f32[1,128,256]{2,1,0:T(8,128)S(1)} %stack_here.1, f32[2,128,256]{2,1,0:T(8,128)S(1)} %collective-permute-done.2.refs_1_, f32[128,256]{1,0:T(8,128)S(1)} %collective-permute-done.4, f32[128,256]{1,0:T(8,128)S(1)} %collective-permute-done.5), kind=kLoop, calls=%fused_computation.2 | loop fusion | flops 98304 | bytes 655360 | tf_op jit(solution)/shard_map/add | solution.py:321
  (12 shorter events, 0.1 us)
Async XLA Ops:
  0.0 1.0 %copy-start = (f32[4,32,1024]{2,1,0:T(8,128)S(1)}, f32[4,32,1024]{2,1,0:T(8,128)}, u32[]{:S(2)}) copy-start(f32[4,32,1024]{2,1,0:T(8,128)} %records.3) | copy-start | bytes 1572868
  1.0 0.7 %copy-start.1 = (s32[32]{0:T(128)S(1)}, s32[32]{0:T(128)}, u32[]{:S(2)}) copy-start(s32[32]{0:T(128)} %param.5) | copy-start | bytes 388
  2.0 26.5 %copy-start.2 = (bf16[2048,512]{1,0:T(8,128)(2,1)S(1)}, bf16[2048,512]{1,0:T(8,128)(2,1)}, u32[]{:S(2)}) copy-start(bf16[2048,512]{1,0:T(8,128)(2,1)} %constant.4.clone.tables) | copy-start | bytes 6291460
  28.6 1.2 %copy-start.3 = (bf16[2,512,512]{2,1,0:T(8,128)(2,1)S(1)}, bf16[2,512,512]{2,1,0:T(8,128)(2,1)}, u32[]{:S(2)}) copy-start(bf16[2,512,512]{2,1,0:T(8,128)(2,1)} %constant.5.clone.tables) | copy-start | bytes 3145732
  30.5 3.2 %collective-permute-start = (f32[1,128,256]{2,1,0:T(8,128)S(1)}, f32[1,128,256]{2,1,0:T(8,128)S(1)}, u32[]{:S(2)}, u32[]{:S(2)}) collective-permute-start(f32[1,128,256]{2,1,0:T(8,128)S(1)} %stack_far.2.refs_0_), channel_id=1, source_target_pairs={{0,1},{1,0},{2,3},{3,2},{4,5},{5,4},{6,7},{7,6},{8,9},{9,8},{10,11... | collective-permute-start | bytes 393224 | tf_op jit(solution)/shard_map/ppermute | solution.py:305
  34.5 6.3 %collective-permute-start.1 = (f32[1,128,256]{2,1,0:T(8,128)S(1)}, f32[1,128,256]{2,1,0:T(8,128)S(1)}, u32[]{:S(2)}, u32[]{:S(2)}) collective-permute-start(f32[1,128,256]{2,1,0:T(8,128)S(1)} %stack_behind.1.refs_0_), channel_id=1, source_target_pairs={{0,1},{1,0},{2,3},{3,2},{4,5},{5,4},{6,7},{7,6},{8,9},{9,8},{10,11... | collective-permute-start | bytes 393224 | tf_op jit(solution)/shard_map/ppermute | solution.py:305
  35.6 8.6 %collective-permute-start.3 = (f32[128,256]{1,0:T(8,128)S(1)}, f32[128,256]{1,0:T(8,128)S(1)}, u32[]{:S(2)}, u32[]{:S(2)}) collective-permute-start(f32[128,256]{1,0:T(8,128)S(1)} %add_far.1.refs_0_), channel_id=1, source_target_pairs={{0,2},{1,7},{2,4},{3,1},{4,6},{5,3},{6,0},{7,5},{8,10},{9,15},{10,... | collective-permute-start | bytes 393224 | tf_op jit(solution)/shard_map/ppermute | solution.py:298
  40.8 8.2 %collective-permute-start.4 = (f32[128,256]{1,0:T(8,128)S(1)}, f32[128,256]{1,0:T(8,128)S(1)}, u32[]{:S(2)}, u32[]{:S(2)}) collective-permute-start(f32[128,256]{1,0:T(8,128)S(1)} %add_other.1.refs_0_), channel_id=1, source_target_pairs={{0,3},{1,6},{2,5},{3,0},{4,7},{5,2},{6,1},{7,4},{8,11},{9,14},{10,... | collective-permute-start | bytes 393224 | tf_op jit(solution)/shard_map/ppermute | solution.py:302
  42.5 1.7 %collective-permute-start.2 = (f32[2,128,256]{2,1,0:T(8,128)S(1)}, f32[2,128,256]{2,1,0:T(8,128)S(1)}, u32[]{:S(2)}, u32[]{:S(2)}) collective-permute-start(f32[2,128,256]{2,1,0:T(8,128)S(1)} %stack_behind_here.1.refs_0_), channel_id=1, source_target_pairs={{0,1},{1,0},{2,3},{3,2},{4,5},{5,4},{6,7},{7,6},{8,9},{9,8},{10,11... | collective-permute-start | bytes 786440 | tf_op jit(solution)/shard_map/ppermute | solution.py:305
  44.2 7.0 %collective-permute-start.5 = (f32[128,256]{1,0:T(8,128)S(1)}, f32[128,256]{1,0:T(8,128)S(1)}, u32[]{:S(2)}, u32[]{:S(2)}) collective-permute-start(f32[128,256]{1,0:T(8,128)S(1)} %add_own.1.refs_0_), channel_id=1, source_target_pairs={{0,2},{1,7},{2,4},{3,1},{4,6},{5,3},{6,0},{7,5},{8,10},{9,15},{10,... | collective-permute-start | bytes 393224 | tf_op jit(solution)/shard_map/ppermute | solution.py:298

commit v9 on v8

--- a/solution.py
+++ b/solution.py
@@ -213,6 +213,11 @@
     refs[-1][...] = total
 
 
+def add_far_kernel(own, other, total, token):
+    total[...] = own[0] + other[0]
+    token[...] = total[: token.shape[0], : token.shape[1]]
+
+
 def local(records, sources):
     chan_count = lax.axis_size("chan")
     windows, times, channels = records.shape
@@ -306,9 +311,16 @@
 
     far_other = stack(("far", False))
     far_own = stack(("far", True), after=far_other)
-    far = add("add_far", far_own, across(far_other))
+    far, token = pl.pallas_call(
+        add_far_kernel,
+        out_shape=[piece, shape((8, LANES), F32)],
+        in_specs=[vmem] * 2,
+        out_specs=[vmem] * 2,
+        compiler_params=pltpu.CompilerParams(vmem_limit_bytes=4 << 20),
+        name="add_far",
+    )(far_own, across(far_other))
     passing = onward(far)
-    behind_own = stack(("behind", True), after=far)
+    behind_own = stack(("behind", True), after=across(token))
     ahead_other = stack(("ahead", False), after=behind_own)
     other = add("add_other", ahead_other, across(behind_own))
     early = onward_other(other)

time: 52.2 us -> 53.1 us (1.017)
  waiting for transfers between devices: 3.43 us -> 4.79 us
    ppermute x2, starting transfers between devices: 9.29 us -> 7.53 us  [onward(): return lax.ppermute(value, 'win', pairs)]
    ppermute x3 -> x4, waiting for transfers between devices: 0.3 us -> 1.38 us  [across(): return lax.ppermute(value, 'win', [(i, i ^ 1) for i in range(8)])]
    ppermute x1, starting transfers between devices: 0.54 us -> 1.3 us  [onward_other(): return lax.ppermute(value, 'win', pairs)]
    ppermute x3 -> x4, starting transfers between devices: 2.79 us -> 3.3 us  [across(): return lax.ppermute(value, 'win', [(i, i ^ 1) for i in range(8)])]
  transfers between devices with their start and end apart: 6 -> 7, of which waited for: 3 -> 4; matrix products, arithmetic and copies ran while one was open for 0% -> 0% of each run, Pallas kernels for 8% -> 9%
where the time goes in v9:
time: 53.1 us; the launch traced here: 52.9 us
  blocking collectives  25.8 us (49%)
  starting transfers between devices  12.1 us (23%)
  Pallas kernels  8.04 us (15%)
  waiting for transfers between devices  4.79 us (9%)
  local copies, waits for them, and re-layouts  1.23 us (2%)
  other arithmetic  0.69 us (1%)
    all_to_all x1, blocking collectives, local(): blocks = lax.all_to_all(packed, 'chan', 0, 0, tiled=True)  25.8 us
    ppermute x2, starting transfers between devices, onward(): return lax.ppermute(value, 'win', pairs)  7.53 us
    pallas_call x7, Pallas kernels, stack(): pl.pallas_call(functools.partial(stack_kernel, parts), out_shape=shape((c...  5.3 us
    ppermute x2, waiting for transfers between devices, onward(): return lax.ppermute(value, 'win', pairs)  3.4 us
    ppermute x4, starting transfers between devices, across(): return lax.ppermute(value, 'win', [(i, i ^ 1) for i in range(8)])  3.3 us
    ppermute x4, waiting for transfers between devices, across(): return lax.ppermute(value, 'win', [(i, i ^ 1) for i in range(8)])  1.38 us
    ppermute x1, starting transfers between devices, onward_other(): return lax.ppermute(value, 'win', pairs)  1.3 us
    unnamed x8, local copies, waits for them, and re-layouts  1.23 us
  transfers between devices with their start and end apart: 7, of which 4 were waited for; matrix products, arithmetic and copies ran while one was open for 0% of the time, Pallas kernels for 9%

profile of v9, /device:TPU:1, one launch (start us, length us, event | category | flops | bytes accessed | tf_op | source)
XLA Modules:
  0.0 52.9 jit_solution(5587694581326233568)
XLA Ops:
  0.0 1.0 %copy-done = f32[4,32,1024]{2,1,0:T(8,128)S(1)} copy-done((f32[4,32,1024]{2,1,0:T(8,128)S(1)}, f32[4,32,1024]{2,1,0:T(8,128)}, u32[]{:S(2)}) %copy-start) | copy-done | bytes 524312
  1.0 0.5 pack.1.packed_in
  1.7 0.3 pick.1
  2.0 25.8 %all_to_all.5.blocks = f32[32,64,128]{2,1,0:T(8,128)S(1)} all-to-all(f32[32,64,128]{2,1,0:T(8,128)S(1)} %pick.1), channel_id=1, replica_groups=mesh['chan'=32,'win'=8] {'chan'}, dimensions={0} | all-to-all | bytes 2097152 | tf_op jit(solution)/shard_map/all_to_all | solution.py:250
  27.9 0.7 %level.1.turned = f32[256,1024]{1,0:T(8,128)S(1)} custom-call(f32[32,64,128]{2,1,0:T(8,128)S(1)} %all_to_all.5.blocks), custom_call_target="tpu_custom_call" | custom-call | flops 268435456 | bytes 1048576 | tf_op jit(solution)/shard_map/level/pallas_call | solution.py:256
  28.6 1.2 %spectra.1 = (f32[256,512]{1,0:T(8,128)S(1)}, f32[256,512]{1,0:T(8,128)S(1)}) custom-call(f32[256,1024]{1,0:T(8,128)S(1)} %level.1.turned, bf16[2048,512]{1,0:T(8,128)(2,1)S(1)} %copy-done.2), custom_call_target="tpu_custom_call" | custom-call | flops 4294967296 | bytes 16777216 | tf_op jit(solution)/shard_map/spectra/pallas_call | solution.py:265
  29.8 0.7 %stack_far.2.refs_0_ = f32[1,128,256]{2,1,0:T(8,128)S(1)} custom-call(f32[256,512]{1,0:T(8,128)S(1)} %get-tuple-element.9.white_re, f32[256,512]{1,0:T(8,128)S(1)} %get-tuple-element.10.white_im, bf16[2,512,512]{2,1,0:T(8,128)(2,1)S(1)} %copy-done.3), custom_call_target="tpu_custom_call" | custom-call | flops 4294967296 | bytes 1 | tf_op jit(solution)/shard_map/stack_far/pallas_call | solution.py:280
  30.5 2.2 %collective-permute-start = (f32[1,128,256]{2,1,0:T(8,128)S(1)}, f32[1,128,256]{2,1,0:T(8,128)S(1)}, u32[]{:S(2)}, u32[]{:S(2)}) collective-permute-start(f32[1,128,256]{2,1,0:T(8,128)S(1)} %stack_far.2.refs_0_), channel_id=1, source_target_pairs={{0,1},{1,0},{2,3},{3,2},{4,5},{5,4},{6,7},{7,6},{8,9},{9,8},{10,11... | collective-permute-start | bytes 393224 | tf_op jit(solution)/shard_map/ppermute | solution.py:310
  32.8 0.7 %stack_far.3.own = f32[1,128,256]{2,1,0:T(8,128)S(1)} custom-call(f32[256,512]{1,0:T(8,128)S(1)} %get-tuple-element.9.white_re, f32[256,512]{1,0:T(8,128)S(1)} %get-tuple-element.10.white_im, bf16[2,512,512]{2,1,0:T(8,128)(2,1)S(1)} %copy-done.3, f32[1,128,256]{2,1,0:T(8,128)S(1)} %stack_far.2.refs_0_), custom_call_target="tpu_custom_call" | custom-call | flops 4294967296 | bytes 1 | tf_op jit(solution)/shard_map/stack_far/pallas_call | solution.py:280
  33.4 0.3 collective-permute-done.other
  33.8 0.4 collective-permute-start.1
  34.2 5.1 %collective-permute-start.4 = (f32[128,256]{1,0:T(8,128)S(1)}, f32[128,256]{1,0:T(8,128)S(1)}, u32[]{:S(2)}, u32[]{:S(2)}) collective-permute-start(f32[128,256]{1,0:T(8,128)S(1)} %get-tuple-element.12), channel_id=1, source_target_pairs={{0,2},{1,7},{2,4},{3,1},{4,6},{5,3},{6,0},{7,5},{8,10},{9,15},{10,... | collective-permute-start | bytes 393224 | tf_op jit(solution)/shard_map/ppermute | solution.py:303
  39.3 0.7 %stack_behind.1.refs_0_ = f32[1,128,256]{2,1,0:T(8,128)S(1)} custom-call(f32[256,512]{1,0:T(8,128)S(1)} %get-tuple-element.9.white_re, f32[256,512]{1,0:T(8,128)S(1)} %get-tuple-element.10.white_im, bf16[2,512,512]{2,1,0:T(8,128)(2,1)S(1)} %copy-done.3, f32[8,128]{1,0:T(8,128)S(1)} %collective-permute-done.1.refs_0_), custom_call_target="tpu_custom_call" | custom-call | flops 4294967296 | bytes 1 | tf_op jit(solution)/shard_map/stack_behind/pallas_call | solution.py:280
  40.1 0.7 %stack_ahead.2.refs_0_ = f32[1,128,256]{2,1,0:T(8,128)S(1)} custom-call(f32[256,512]{1,0:T(8,128)S(1)} %get-tuple-element.9.white_re, f32[256,512]{1,0:T(8,128)S(1)} %get-tuple-element.10.white_im, bf16[2,512,512]{2,1,0:T(8,128)(2,1)S(1)} %copy-done.3, f32[1,128,256]{2,1,0:T(8,128)S(1)} %stack_behind.1.refs_0_), custom_call_target="tpu_custom_call" | custom-call | flops 4294967296 | bytes 1 | tf_op jit(solution)/shard_map/stack_ahead/pallas_call | solution.py:280
  40.8 0.6 %collective-permute-done.2.refs_1_ = f32[1,128,256]{2,1,0:T(8,128)S(1)} collective-permute-done((f32[1,128,256]{2,1,0:T(8,128)S(1)}, f32[1,128,256]{2,1,0:T(8,128)S(1)}, u32[]{:S(2)}, u32[]{:S(2)}) %collective-permute-start.2) | collective-permute-done | bytes 131104 | tf_op jit(solution)/shard_map/ppermute | solution.py:310
  41.5 1.3 %collective-permute-start.5 = (f32[128,256]{1,0:T(8,128)S(1)}, f32[128,256]{1,0:T(8,128)S(1)}, u32[]{:S(2)}, u32[]{:S(2)}) collective-permute-start(f32[128,256]{1,0:T(8,128)S(1)} %add_other.1.refs_0_), channel_id=1, source_target_pairs={{0,3},{1,6},{2,5},{3,0},{4,7},{5,2},{6,1},{7,4},{8,11},{9,14},{10,... | collective-permute-start | bytes 393224 | tf_op jit(solution)/shard_map/ppermute | solution.py:307
  42.8 1.2 %stack_behind_here.1.refs_0_ = f32[2,128,256]{2,1,0:T(8,128)S(1)} custom-call(f32[256,512]{1,0:T(8,128)S(1)} %get-tuple-element.9.white_re, f32[256,512]{1,0:T(8,128)S(1)} %get-tuple-element.10.white_im, bf16[2,512,512]{2,1,0:T(8,128)(2,1)S(1)} %copy-done.3, f32[128,256]{1,0:T(8,128)S(1)} %add_other.1.refs_0_), custom_call_target="tpu_custom_call" | custom-call | flops 8589934592 | bytes 1 | tf_op jit(solution)/shard_map/stack_behind_here/pallas_call | solution.py:280
  43.9 0.5 collective-permute-start.3
  44.5 0.7 %stack_ahead.3.refs_0_ = f32[1,128,256]{2,1,0:T(8,128)S(1)} custom-call(f32[256,512]{1,0:T(8,128)S(1)} %get-tuple-element.9.white_re, f32[256,512]{1,0:T(8,128)S(1)} %get-tuple-element.10.white_im, bf16[2,512,512]{2,1,0:T(8,128)(2,1)S(1)} %copy-done.3, f32[2,128,256]{2,1,0:T(8,128)S(1)} %stack_behind_here.1.refs_0_), custom_call_target="tpu_custom_call" | custom-call | flops 4294967296 | bytes 1 | tf_op jit(solution)/shard_map/stack_ahead/pallas_call | solution.py:280
  45.2 0.5 collective-permute-done.3.refs_1_
  45.6 2.4 %collective-permute-start.6 = (f32[128,256]{1,0:T(8,128)S(1)}, f32[128,256]{1,0:T(8,128)S(1)}, u32[]{:S(2)}, u32[]{:S(2)}) collective-permute-start(f32[128,256]{1,0:T(8,128)S(1)} %add_own.1.refs_0_), channel_id=1, source_target_pairs={{0,2},{1,7},{2,4},{3,1},{4,6},{5,3},{6,0},{7,5},{8,10},{9,15},{10,... | collective-permute-start | bytes 393224 | tf_op jit(solution)/shard_map/ppermute | solution.py:303
  48.1 0.7 %stack_here.1 = f32[1,128,256]{2,1,0:T(8,128)S(1)} custom-call(f32[256,512]{1,0:T(8,128)S(1)} %get-tuple-element.9.white_re, f32[256,512]{1,0:T(8,128)S(1)} %get-tuple-element.10.white_im, bf16[2,512,512]{2,1,0:T(8,128)(2,1)S(1)} %copy-done.3, f32[128,256]{1,0:T(8,128)S(1)} %add_own.1.refs_0_), custom_call_target="tpu_custom_call" | custom-call | flops 4294967296 | bytes 1 | tf_op jit(solution)/shard_map/stack_here/pallas_call | solution.py:280
  48.8 3.4 %collective-permute-done.6 = f32[128,256]{1,0:T(8,128)S(1)} collective-permute-done((f32[128,256]{1,0:T(8,128)S(1)}, f32[128,256]{1,0:T(8,128)S(1)}, u32[]{:S(2)}, u32[]{:S(2)}) %collective-permute-start.6) | collective-permute-done | bytes 131104 | tf_op jit(solution)/shard_map/ppermute | solution.py:303
  52.2 0.7 %fusion.1 = f32[128,256]{1,0:T(8,128)} fusion(f32[1,128,256]{2,1,0:T(8,128)S(1)} %stack_here.1, f32[2,128,256]{2,1,0:T(8,128)S(1)} %collective-permute-done.3.refs_1_, f32[128,256]{1,0:T(8,128)S(1)} %collective-permute-done.5, f32[128,256]{1,0:T(8,128)S(1)} %collective-permute-done.6), kind=kLoop, calls=%fused_computation.2 | loop fusion | flops 98304 | bytes 655360 | tf_op jit(solution)/shard_map/add | solution.py:333
  (14 shorter events, 0.3 us)
Async XLA Ops:
  0.0 1.0 %copy-start = (f32[4,32,1024]{2,1,0:T(8,128)S(1)}, f32[4,32,1024]{2,1,0:T(8,128)}, u32[]{:S(2)}) copy-start(f32[4,32,1024]{2,1,0:T(8,128)} %records.3) | copy-start | bytes 1572868
  1.0 0.7 %copy-start.1 = (s32[32]{0:T(128)S(1)}, s32[32]{0:T(128)}, u32[]{:S(2)}) copy-start(s32[32]{0:T(128)} %param.5) | copy-start | bytes 388
  2.0 26.5 %copy-start.2 = (bf16[2048,512]{1,0:T(8,128)(2,1)S(1)}, bf16[2048,512]{1,0:T(8,128)(2,1)}, u32[]{:S(2)}) copy-start(bf16[2048,512]{1,0:T(8,128)(2,1)} %constant.4.clone.tables) | copy-start | bytes 6291460
  28.6 1.2 %copy-start.3 = (bf16[2,512,512]{2,1,0:T(8,128)(2,1)S(1)}, bf16[2,512,512]{2,1,0:T(8,128)(2,1)}, u32[]{:S(2)}) copy-start(bf16[2,512,512]{2,1,0:T(8,128)(2,1)} %constant.5.clone.tables) | copy-start | bytes 3145732
  30.5 3.2 %collective-permute-start = (f32[1,128,256]{2,1,0:T(8,128)S(1)}, f32[1,128,256]{2,1,0:T(8,128)S(1)}, u32[]{:S(2)}, u32[]{:S(2)}) collective-permute-start(f32[1,128,256]{2,1,0:T(8,128)S(1)} %stack_far.2.refs_0_), channel_id=1, source_target_pairs={{0,1},{1,0},{2,3},{3,2},{4,5},{5,4},{6,7},{7,6},{8,9},{9,8},{10,11... | collective-permute-start | bytes 393224 | tf_op jit(solution)/shard_map/ppermute | solution.py:310
  33.8 5.6 %collective-permute-start.1 = (f32[8,128]{1,0:T(8,128)S(1)}, f32[8,128]{1,0:T(8,128)S(1)}, u32[]{:S(2)}, u32[]{:S(2)}) collective-permute-start(f32[8,128]{1,0:T(8,128)S(1)} %get-tuple-element.11), channel_id=1, source_target_pairs={{0,1},{1,0},{2,3},{3,2},{4,5},{5,4},{6,7},{7,6},{8,9},{9,8},{10,11... | collective-permute-start | bytes 12296 | tf_op jit(solution)/shard_map/ppermute | solution.py:310
  34.2 11.0 %collective-permute-start.4 = (f32[128,256]{1,0:T(8,128)S(1)}, f32[128,256]{1,0:T(8,128)S(1)}, u32[]{:S(2)}, u32[]{:S(2)}) collective-permute-start(f32[128,256]{1,0:T(8,128)S(1)} %get-tuple-element.12), channel_id=1, source_target_pairs={{0,2},{1,7},{2,4},{3,1},{4,6},{5,3},{6,0},{7,5},{8,10},{9,15},{10,... | collective-permute-start | bytes 393224 | tf_op jit(solution)/shard_map/ppermute | solution.py:303
  40.0 1.4 %collective-permute-start.2 = (f32[1,128,256]{2,1,0:T(8,128)S(1)}, f32[1,128,256]{2,1,0:T(8,128)S(1)}, u32[]{:S(2)}, u32[]{:S(2)}) collective-permute-start(f32[1,128,256]{2,1,0:T(8,128)S(1)} %stack_behind.1.refs_0_), channel_id=1, source_target_pairs={{0,1},{1,0},{2,3},{3,2},{4,5},{5,4},{6,7},{7,6},{8,9},{9,8},{10,11... | collective-permute-start | bytes 393224 | tf_op jit(solution)/shard_map/ppermute | solution.py:310
  41.5 7.3 %collective-permute-start.5 = (f32[128,256]{1,0:T(8,128)S(1)}, f32[128,256]{1,0:T(8,128)S(1)}, u32[]{:S(2)}, u32[]{:S(2)}) collective-permute-start(f32[128,256]{1,0:T(8,128)S(1)} %add_other.1.refs_0_), channel_id=1, source_target_pairs={{0,3},{1,6},{2,5},{3,0},{4,7},{5,2},{6,1},{7,4},{8,11},{9,14},{10,... | collective-permute-start | bytes 393224 | tf_op jit(solution)/shard_map/ppermute | solution.py:307
  43.9 1.7 %collective-permute-start.3 = (f32[2,128,256]{2,1,0:T(8,128)S(1)}, f32[2,128,256]{2,1,0:T(8,128)S(1)}, u32[]{:S(2)}, u32[]{:S(2)}) collective-permute-start(f32[2,128,256]{2,1,0:T(8,128)S(1)} %stack_behind_here.1.refs_0_), channel_id=1, source_target_pairs={{0,1},{1,0},{2,3},{3,2},{4,5},{5,4},{6,7},{7,6},{8,9},{9,8},{10,11... | collective-permute-start | bytes 786440 | tf_op jit(solution)/shard_map/ppermute | solution.py:310
  45.6 6.5 %collective-permute-start.6 = (f32[128,256]{1,0:T(8,128)S(1)}, f32[128,256]{1,0:T(8,128)S(1)}, u32[]{:S(2)}, u32[]{:S(2)}) collective-permute-start(f32[128,256]{1,0:T(8,128)S(1)} %add_own.1.refs_0_), channel_id=1, source_target_pairs={{0,2},{1,7},{2,4},{3,1},{4,6},{5,3},{6,0},{7,5},{8,10},{9,15},{10,... | collective-permute-start | bytes 393224 | tf_op jit(solution)/shard_map/ppermute | solution.py:303

commit v10 on v7

--- a/solution.py
+++ b/solution.py
@@ -222,6 +222,11 @@
         out[...] = left[...] + right[...]
 
 
+def add_late_kernel(own, passing, total, token):
+    total[...] = own[...] + passing[...]
+    token[...] = total[: token.shape[0], : token.shape[1]]
+
+
 def join_kernel(own, other, received, own_sum, other_sum):
     own_sum[...] = own[...] + received[0]
     other_sum[...] = other[...] + received[1]
@@ -339,9 +344,16 @@
     own, other = stack("ahead", after=behind)
     own, other = small(join_kernel, 2, "join", own, other, across(behind))
     early = onward_other(other)
-    (own,) = small(add_kernel, 1, "add_passing", own, passing)
+    own, token = pl.pallas_call(
+        add_late_kernel,
+        out_shape=[piece, shape((8, LANES), F32)],
+        in_specs=[vmem] * 2,
+        out_specs=[vmem] * 2,
+        compiler_params=pltpu.CompilerParams(vmem_limit_bytes=4 << 20),
+        name="add_passing",
+    )(own, passing)
     late = onward(own)
-    (here_other,) = stack("here_other", after=other)
+    (here_other,) = stack("here_other", after=across(token))
     (here_own,) = stack("here_own", after=here_other)
     result = (here_own + across(here_other)) + (early + late)
     return jnp.transpose(result.reshape(4, 32, lag_count), (0, 2, 1))

time: 52.9 us -> 54 us (1.021)
  waiting for transfers between devices: 5.14 us -> 5.78 us
    ppermute x1, waiting for transfers between devices: 0.01 us -> 3.72 us  [onward_other(): return lax.ppermute(value, 'win', pairs)]
    ppermute x2, waiting for transfers between devices: 4.57 us -> 1.49 us  [onward(): return lax.ppermute(value, 'win', pairs)]
    ppermute x2, starting transfers between devices: 7.31 us -> 8.93 us  [onward(): return lax.ppermute(value, 'win', pairs)]
    ppermute x1, starting transfers between devices: 1.38 us -> 0.31 us  [onward_other(): return lax.ppermute(value, 'win', pairs)]
    ppermute x3 -> x4, starting transfers between devices: 2.98 us -> 2.89 us  [across(): return lax.ppermute(value, 'win', [(i, i ^ 1) for i in range(8)])]
  transfers between devices with their start and end apart: 6 -> 7, of which waited for: 3 -> 5; matrix products, arithmetic and copies ran while one was open for 0% -> 0% of each run, Pallas kernels for 9% -> 9%
where the time goes in v10:
time: 54 us; the launch traced here: 53.8 us
  blocking collectives  25.8 us (48%)
  starting transfers between devices  12.1 us (22%)
  Pallas kernels  7.99 us (15%)
  waiting for transfers between devices  5.78 us (11%)
  local copies, waits for them, and re-layouts  1.23 us (2%)
  other arithmetic  0.69 us (1%)
    all_to_all x1, blocking collectives, local(): blocks = lax.all_to_all(packed, 'chan', 0, 0, tiled=True)  25.8 us
    ppermute x2, starting transfers between devices, onward(): return lax.ppermute(value, 'win', pairs)  8.93 us
    pallas_call x6, Pallas kernels, stack(): pl.pallas_call(functools.partial(stack_kernel, kind), out_shape=outs, in_...  5.25 us
    ppermute x1, waiting for transfers between devices, onward_other(): return lax.ppermute(value, 'win', pairs)  3.72 us
    ppermute x4, starting transfers between devices, across(): return lax.ppermute(value, 'win', [(i, i ^ 1) for i in range(8)])  2.89 us
    ppermute x2, waiting for transfers between devices, onward(): return lax.ppermute(value, 'win', pairs)  1.49 us
    unnamed x8, local copies, waits for them, and re-layouts  1.23 us
    pallas_call x1, Pallas kernels, local(): pl.pallas_call(spectra_kernel, out_shape=(shape((rows, half), F32), shape...  1.22 us
  transfers between devices with their start and end apart: 7, of which 5 were waited for; matrix products, arithmetic and copies ran while one was open for 0% of the time, Pallas kernels for 9%

profile of v10, /device:TPU:1, one launch (start us, length us, event | category | flops | bytes accessed | tf_op | source)
XLA Modules:
  0.0 53.8 jit_solution(14915826089393943652)
XLA Ops:
  0.0 1.0 %copy-done = f32[4,32,1024]{2,1,0:T(8,128)S(1)} copy-done((f32[4,32,1024]{2,1,0:T(8,128)S(1)}, f32[4,32,1024]{2,1,0:T(8,128)}, u32[]{:S(2)}) %copy-start) | copy-done | bytes 524312
  1.0 0.5 pack.1.packed_in
  1.5 0.2 copy-done.1
  1.7 0.3 pick.1
  2.0 25.8 %all_to_all.5.blocks = f32[32,64,128]{2,1,0:T(8,128)S(1)} all-to-all(f32[32,64,128]{2,1,0:T(8,128)S(1)} %pick.1), channel_id=1, replica_groups=mesh['chan'=32,'win'=8] {'chan'}, dimensions={0} | all-to-all | bytes 2097152 | tf_op jit(solution)/shard_map/all_to_all | solution.py:264
  27.9 0.7 %level.1.turned = f32[256,1024]{1,0:T(8,128)S(1)} custom-call(f32[32,64,128]{2,1,0:T(8,128)S(1)} %all_to_all.5.blocks), custom_call_target="tpu_custom_call" | custom-call | flops 268435456 | bytes 1048576 | tf_op jit(solution)/shard_map/level/pallas_call | solution.py:270
  28.6 1.2 %spectra.1 = (f32[256,512]{1,0:T(8,128)S(1)}, f32[256,512]{1,0:T(8,128)S(1)}) custom-call(f32[256,1024]{1,0:T(8,128)S(1)} %level.1.turned, bf16[2048,512]{1,0:T(8,128)(2,1)S(1)} %copy-done.2), custom_call_target="tpu_custom_call" | custom-call | flops 4294967296 | bytes 16777216 | tf_op jit(solution)/shard_map/spectra/pallas_call | solution.py:279
  29.8 0.7 %stack_far_other.1.refs_0_ = f32[128,256]{1,0:T(8,128)S(1)} custom-call(f32[256,512]{1,0:T(8,128)S(1)} %get-tuple-element.13.white_re, f32[256,512]{1,0:T(8,128)S(1)} %get-tuple-element.14.white_im, bf16[2,512,512]{2,1,0:T(8,128)(2,1)S(1)} %copy-done.3), custom_call_target="tpu_custom_call" | custom-call | flops 4294967296 | bytes 16777216 | tf_op jit(solution)/shard_map/stack_far_other/pallas_call | solution.py:306
  30.5 2.2 %collective-permute-start = (f32[128,256]{1,0:T(8,128)S(1)}, f32[128,256]{1,0:T(8,128)S(1)}, u32[]{:S(2)}, u32[]{:S(2)}) collective-permute-start(f32[128,256]{1,0:T(8,128)S(1)} %stack_far_other.1.refs_0_), channel_id=1, source_target_pairs={{0,1},{1,0},{2,3},{3,2},{4,5},{5,4},{6,7},{7,6},{8,9},{9,8},{10,11... | collective-permute-start | bytes 393224 | tf_op jit(solution)/shard_map/ppermute | solution.py:337
  32.8 0.7 %stack_far_own.1.refs_0_ = f32[128,256]{1,0:T(8,128)S(1)} custom-call(f32[256,512]{1,0:T(8,128)S(1)} %get-tuple-element.13.white_re, f32[256,512]{1,0:T(8,128)S(1)} %get-tuple-element.14.white_im, bf16[2,512,512]{2,1,0:T(8,128)(2,1)S(1)} %copy-done.3, f32[128,256]{1,0:T(8,128)S(1)} %stack_far_other.1.refs_0_), custom_call_target="tpu_custom_call" | custom-call | flops 4294967296 | bytes 16777216 | tf_op jit(solution)/shard_map/stack_far_own/pallas_call | solution.py:306
  33.4 0.3 collective-permute-done.refs_1_
  33.8 5.2 %collective-permute-start.2 = (f32[128,256]{1,0:T(8,128)S(1)}, f32[128,256]{1,0:T(8,128)S(1)}, u32[]{:S(2)}, u32[]{:S(2)}) collective-permute-start(f32[128,256]{1,0:T(8,128)S(1)} %add_far.1.refs_0_), channel_id=1, source_target_pairs={{0,2},{1,7},{2,4},{3,1},{4,6},{5,3},{6,0},{7,5},{8,10},{9,15},{10,... | collective-permute-start | bytes 393224 | tf_op jit(solution)/shard_map/ppermute | solution.py:330
  39.0 1.2 %stack_behind.1.refs_0_ = f32[2,128,256]{2,1,0:T(8,128)S(1)} custom-call(f32[256,512]{1,0:T(8,128)S(1)} %get-tuple-element.13.white_re, f32[256,512]{1,0:T(8,128)S(1)} %get-tuple-element.14.white_im, bf16[2,512,512]{2,1,0:T(8,128)(2,1)S(1)} %copy-done.3, f32[128,256]{1,0:T(8,128)S(1)} %add_far.1.refs_0_), custom_call_target="tpu_custom_call" | custom-call | flops 4294967296 | bytes 16777216 | tf_op jit(solution)/shard_map/stack_behind/pallas_call | solution.py:306
  40.3 1.2 %stack_ahead.1 = (f32[128,256]{1,0:T(8,128)S(1)}, f32[128,256]{1,0:T(8,128)S(1)}) custom-call(f32[256,512]{1,0:T(8,128)S(1)} %get-tuple-element.13.white_re, f32[256,512]{1,0:T(8,128)S(1)} %get-tuple-element.14.white_im, bf16[2,512,512]{2,1,0:T(8,128)(2,1)S(1)} %copy-done.3, f32[2,128,256]{2,1,0:T(8,128)S(1)} %stack_behind.1.refs_0_), custom_call_target="tpu_custom_call" | custom-call | flops 4294967296 | bytes 16777216 | tf_op jit(solution)/shard_map/stack_ahead/pallas_call | solution.py:306
  41.5 0.3 collective-permute-done.1.received
  41.9 0.4 collective-permute-done.2.passing
  42.3 0.5 collective-permute-start.3
  42.8 3.7 %collective-permute-start.6 = (f32[128,256]{1,0:T(8,128)S(1)}, f32[128,256]{1,0:T(8,128)S(1)}, u32[]{:S(2)}, u32[]{:S(2)}) collective-permute-start(f32[128,256]{1,0:T(8,128)S(1)} %get-tuple-element.20), channel_id=1, source_target_pairs={{0,2},{1,7},{2,4},{3,1},{4,6},{5,3},{6,0},{7,5},{8,10},{9,15},{10,... | collective-permute-start | bytes 393224 | tf_op jit(solution)/shard_map/ppermute | solution.py:330
  46.5 0.3 collective-permute-start.5
  46.8 0.7 %stack_here_other.1.refs_0_ = f32[128,256]{1,0:T(8,128)S(1)} custom-call(f32[256,512]{1,0:T(8,128)S(1)} %get-tuple-element.13.white_re, f32[256,512]{1,0:T(8,128)S(1)} %get-tuple-element.14.white_im, bf16[2,512,512]{2,1,0:T(8,128)(2,1)S(1)} %copy-done.3, f32[8,128]{1,0:T(8,128)S(1)} %collective-permute-done.3.refs_0_), custom_call_target="tpu_custom_call" | custom-call | flops 4294967296 | bytes 16777216 | tf_op jit(solution)/shard_map/stack_here_other/pallas_call | solution.py:306
  47.6 0.7 %stack_here_own.1 = f32[128,256]{1,0:T(8,128)S(1)} custom-call(f32[256,512]{1,0:T(8,128)S(1)} %get-tuple-element.13.white_re, f32[256,512]{1,0:T(8,128)S(1)} %get-tuple-element.14.white_im, bf16[2,512,512]{2,1,0:T(8,128)(2,1)S(1)} %copy-done.3, f32[128,256]{1,0:T(8,128)S(1)} %stack_here_other.1.refs_0_), custom_call_target="tpu_custom_call" | custom-call | flops 4294967296 | bytes 16777216 | tf_op jit(solution)/shard_map/stack_here_own/pallas_call | solution.py:306
  48.3 1.1 %collective-permute-done.6 = f32[128,256]{1,0:T(8,128)S(1)} collective-permute-done((f32[128,256]{1,0:T(8,128)S(1)}, f32[128,256]{1,0:T(8,128)S(1)}, u32[]{:S(2)}, u32[]{:S(2)}) %collective-permute-start.6) | collective-permute-done | bytes 131104 | tf_op jit(solution)/shard_map/ppermute | solution.py:330
  49.4 3.7 %collective-permute-done.5 = f32[128,256]{1,0:T(8,128)S(1)} collective-permute-done((f32[128,256]{1,0:T(8,128)S(1)}, f32[128,256]{1,0:T(8,128)S(1)}, u32[]{:S(2)}, u32[]{:S(2)}) %collective-permute-start.5) | collective-permute-done | bytes 131104 | tf_op jit(solution)/shard_map/ppermute | solution.py:334
  53.1 0.7 %add_add_fusion = f32[128,256]{1,0:T(8,128)} fusion(f32[128,256]{1,0:T(8,128)S(1)} %collective-permute-done.5, f32[128,256]{1,0:T(8,128)S(1)} %collective-permute-done.6, f32[128,256]{1,0:T(8,128)S(1)} %stack_here_own.1, f32[128,256]{1,0:T(8,128)S(1)} %collective-permute-done.4), kind=kLoop, calls=%fused_computation | loop fusion | flops 98304 | bytes 655360 | tf_op jit(solution)/shard_map/add | solution.py:358
  (13 shorter events, 0.3 us)
Async XLA Ops:
  0.0 1.0 %copy-start = (f32[4,32,1024]{2,1,0:T(8,128)S(1)}, f32[4,32,1024]{2,1,0:T(8,128)}, u32[]{:S(2)}) copy-start(f32[4,32,1024]{2,1,0:T(8,128)} %records.3) | copy-start | bytes 1572868
  1.0 0.7 %copy-start.1 = (s32[32]{0:T(128)S(1)}, s32[32]{0:T(128)}, u32[]{:S(2)}) copy-start(s32[32]{0:T(128)} %param.5) | copy-start | bytes 388
  2.0 26.5 %copy-start.2 = (bf16[2048,512]{1,0:T(8,128)(2,1)S(1)}, bf16[2048,512]{1,0:T(8,128)(2,1)}, u32[]{:S(2)}) copy-start(bf16[2048,512]{1,0:T(8,128)(2,1)} %constant.4.clone.tables) | copy-start | bytes 6291460
  28.6 1.2 %copy-start.3 = (bf16[2,512,512]{2,1,0:T(8,128)(2,1)S(1)}, bf16[2,512,512]{2,1,0:T(8,128)(2,1)}, u32[]{:S(2)}) copy-start(bf16[2,512,512]{2,1,0:T(8,128)(2,1)} %constant.5.clone.tables) | copy-start | bytes 3145732
  30.5 3.2 %collective-permute-start = (f32[128,256]{1,0:T(8,128)S(1)}, f32[128,256]{1,0:T(8,128)S(1)}, u32[]{:S(2)}, u32[]{:S(2)}) collective-permute-start(f32[128,256]{1,0:T(8,128)S(1)} %stack_far_other.1.refs_0_), channel_id=1, source_target_pairs={{0,1},{1,0},{2,3},{3,2},{4,5},{5,4},{6,7},{7,6},{8,9},{9,8},{10,11... | collective-permute-start | bytes 393224 | tf_op jit(solution)/shard_map/ppermute | solution.py:337
  33.8 8.5 %collective-permute-start.2 = (f32[128,256]{1,0:T(8,128)S(1)}, f32[128,256]{1,0:T(8,128)S(1)}, u32[]{:S(2)}, u32[]{:S(2)}) collective-permute-start(f32[128,256]{1,0:T(8,128)S(1)} %add_far.1.refs_0_), channel_id=1, source_target_pairs={{0,2},{1,7},{2,4},{3,1},{4,6},{5,3},{6,0},{7,5},{8,10},{9,15},{10,... | collective-permute-start | bytes 393224 | tf_op jit(solution)/shard_map/ppermute | solution.py:330
  40.2 1.6 %collective-permute-start.1 = (f32[2,128,256]{2,1,0:T(8,128)S(1)}, f32[2,128,256]{2,1,0:T(8,128)S(1)}, u32[]{:S(2)}, u32[]{:S(2)}) collective-permute-start(f32[2,128,256]{2,1,0:T(8,128)S(1)} %stack_behind.1.refs_0_), channel_id=1, source_target_pairs={{0,1},{1,0},{2,3},{3,2},{4,5},{5,4},{6,7},{7,6},{8,9},{9,8},{10,11... | collective-permute-start | bytes 786440 | tf_op jit(solution)/shard_map/ppermute | solution.py:337
  42.3 4.5 %collective-permute-start.3 = (f32[8,128]{1,0:T(8,128)S(1)}, f32[8,128]{1,0:T(8,128)S(1)}, u32[]{:S(2)}, u32[]{:S(2)}) collective-permute-start(f32[8,128]{1,0:T(8,128)S(1)} %get-tuple-element.18), channel_id=1, source_target_pairs={{0,1},{1,0},{2,3},{3,2},{4,5},{5,4},{6,7},{7,6},{8,9},{9,8},{10,11... | collective-permute-start | bytes 12296 | tf_op jit(solution)/shard_map/ppermute | solution.py:337
  42.8 6.6 %collective-permute-start.6 = (f32[128,256]{1,0:T(8,128)S(1)}, f32[128,256]{1,0:T(8,128)S(1)}, u32[]{:S(2)}, u32[]{:S(2)}) collective-permute-start(f32[128,256]{1,0:T(8,128)S(1)} %get-tuple-element.20), channel_id=1, source_target_pairs={{0,2},{1,7},{2,4},{3,1},{4,6},{5,3},{6,0},{7,5},{8,10},{9,15},{10,... | collective-permute-start | bytes 393224 | tf_op jit(solution)/shard_map/ppermute | solution.py:330
  46.5 6.6 %collective-permute-start.5 = (f32[128,256]{1,0:T(8,128)S(1)}, f32[128,256]{1,0:T(8,128)S(1)}, u32[]{:S(2)}, u32[]{:S(2)}) collective-permute-start(f32[128,256]{1,0:T(8,128)S(1)} %get-tuple-element.19), channel_id=1, source_target_pairs={{0,3},{1,6},{2,5},{3,0},{4,7},{5,2},{6,1},{7,4},{8,11},{9,14},{10,... | collective-permute-start | bytes 393224 | tf_op jit(solution)/shard_map/ppermute | solution.py:334
  47.5 5.6 %collective-permute-start.4 = (f32[128,256]{1,0:T(8,128)S(1)}, f32[128,256]{1,0:T(8,128)S(1)}, u32[]{:S(2)}, u32[]{:S(2)}) collective-permute-start(f32[128,256]{1,0:T(8,128)S(1)} %stack_here_other.1.refs_0_), channel_id=1, source_target_pairs={{0,1},{1,0},{2,3},{3,2},{4,5},{5,4},{6,7},{7,6},{8,9},{9,8},{10,11... | collective-permute-start | bytes 393224 | tf_op jit(solution)/shard_map/ppermute | solution.py:337

commit v11 on v8

--- a/solution.py
+++ b/solution.py
@@ -306,10 +306,10 @@
 
     far_other = stack(("far", False))
     far_own = stack(("far", True), after=far_other)
+    behind_own = stack(("behind", True), after=far_own)
     far = add("add_far", far_own, across(far_other))
     passing = onward(far)
-    behind_own = stack(("behind", True), after=far)
-    ahead_other = stack(("ahead", False), after=behind_own)
+    ahead_other = stack(("ahead", False), after=far)
     other = add("add_other", ahead_other, across(behind_own))
     early = onward_other(other)
     rest = stack(("behind", False), ("here", False), after=other)

time: 52.2 us -> 51.9 us (level)
  no operation moved by 1% of the time
where the time goes in v11:
time: 51.9 us; the launch traced here: 51.7 us
  blocking collectives  25.8 us (50%)
  starting transfers between devices  12.2 us (24%)
  Pallas kernels  8.04 us (15%)
  waiting for transfers between devices  3.62 us (7%)
  local copies, waits for them, and re-layouts  1.23 us (2%)
  other arithmetic  0.69 us (1%)
    all_to_all x1, blocking collectives, local(): blocks = lax.all_to_all(packed, 'chan', 0, 0, tiled=True)  25.8 us
    ppermute x2, starting transfers between devices, onward(): return lax.ppermute(value, 'win', pairs)  9.29 us
    pallas_call x7, Pallas kernels, stack(): pl.pallas_call(functools.partial(stack_kernel, parts), out_shape=shape((c...  5.31 us
    ppermute x2, waiting for transfers between devices, onward(): return lax.ppermute(value, 'win', pairs)  3.42 us
    ppermute x3, starting transfers between devices, across(): return lax.ppermute(value, 'win', [(i, i ^ 1) for i in range(8)])  2.43 us
    unnamed x8, local copies, waits for them, and re-layouts  1.23 us
    pallas_call x1, Pallas kernels, local(): pl.pallas_call(spectra_kernel, out_shape=(shape((rows, half), F32), shape...  1.22 us
  transfers between devices with their start and end apart: 6, of which 3 were waited for; matrix products, arithmetic and copies ran while one was open for 0% of the time, Pallas kernels for 8%

profile of v11, /device:TPU:1, one launch (start us, length us, event | category | flops | bytes accessed | tf_op | source)
XLA Modules:
  0.0 51.7 jit_solution(3101640245219923356)
XLA Ops:
  0.0 1.0 %copy-done = f32[4,32,1024]{2,1,0:T(8,128)S(1)} copy-done((f32[4,32,1024]{2,1,0:T(8,128)S(1)}, f32[4,32,1024]{2,1,0:T(8,128)}, u32[]{:S(2)}) %copy-start) | copy-done | bytes 524312
  1.0 0.5 pack.1.packed_in
  1.5 0.2 copy-done.1
  1.7 0.3 pick.1
  2.0 25.8 %all_to_all.5.blocks = f32[32,64,128]{2,1,0:T(8,128)S(1)} all-to-all(f32[32,64,128]{2,1,0:T(8,128)S(1)} %pick.1), channel_id=1, replica_groups=mesh['chan'=32,'win'=8] {'chan'}, dimensions={0} | all-to-all | bytes 2097152 | tf_op jit(solution)/shard_map/all_to_all | solution.py:245
  27.9 0.7 %level.1.turned = f32[256,1024]{1,0:T(8,128)S(1)} custom-call(f32[32,64,128]{2,1,0:T(8,128)S(1)} %all_to_all.5.blocks), custom_call_target="tpu_custom_call" | custom-call | flops 268435456 | bytes 1048576 | tf_op jit(solution)/shard_map/level/pallas_call | solution.py:251
  28.6 1.2 %spectra.1 = (f32[256,512]{1,0:T(8,128)S(1)}, f32[256,512]{1,0:T(8,128)S(1)}) custom-call(f32[256,1024]{1,0:T(8,128)S(1)} %level.1.turned, bf16[2048,512]{1,0:T(8,128)(2,1)S(1)} %copy-done.2), custom_call_target="tpu_custom_call" | custom-call | flops 4294967296 | bytes 16777216 | tf_op jit(solution)/shard_map/spectra/pallas_call | solution.py:260
  29.8 0.7 %stack_far.2.refs_0_ = f32[1,128,256]{2,1,0:T(8,128)S(1)} custom-call(f32[256,512]{1,0:T(8,128)S(1)} %get-tuple-element.7.white_re, f32[256,512]{1,0:T(8,128)S(1)} %get-tuple-element.8.white_im, bf16[2,512,512]{2,1,0:T(8,128)(2,1)S(1)} %copy-done.3), custom_call_target="tpu_custom_call" | custom-call | flops 4294967296 | bytes 1 | tf_op jit(solution)/shard_map/stack_far/pallas_call | solution.py:275
  30.5 0.7 %stack_far.3.refs_0_ = f32[1,128,256]{2,1,0:T(8,128)S(1)} custom-call(f32[256,512]{1,0:T(8,128)S(1)} %get-tuple-element.7.white_re, f32[256,512]{1,0:T(8,128)S(1)} %get-tuple-element.8.white_im, bf16[2,512,512]{2,1,0:T(8,128)(2,1)S(1)} %copy-done.3, f32[1,128,256]{2,1,0:T(8,128)S(1)} %stack_far.2.refs_0_), custom_call_target="tpu_custom_call" | custom-call | flops 4294967296 | bytes 1 | tf_op jit(solution)/shard_map/stack_far/pallas_call | solution.py:275
  31.2 2.2 %collective-permute-start = (f32[1,128,256]{2,1,0:T(8,128)S(1)}, f32[1,128,256]{2,1,0:T(8,128)S(1)}, u32[]{:S(2)}, u32[]{:S(2)}) collective-permute-start(f32[1,128,256]{2,1,0:T(8,128)S(1)} %stack_far.2.refs_0_), channel_id=1, source_target_pairs={{0,1},{1,0},{2,3},{3,2},{4,5},{5,4},{6,7},{7,6},{8,9},{9,8},{10,11... | collective-permute-start | bytes 393224 | tf_op jit(solution)/shard_map/ppermute | solution.py:305
  33.4 0.7 %stack_behind.1 = f32[1,128,256]{2,1,0:T(8,128)S(1)} custom-call(f32[256,512]{1,0:T(8,128)S(1)} %get-tuple-element.7.white_re, f32[256,512]{1,0:T(8,128)S(1)} %get-tuple-element.8.white_im, bf16[2,512,512]{2,1,0:T(8,128)(2,1)S(1)} %copy-done.3, f32[1,128,256]{2,1,0:T(8,128)S(1)} %stack_far.3.refs_0_), custom_call_target="tpu_custom_call" | custom-call | flops 4294967296 | bytes 1 | tf_op jit(solution)/shard_map/stack_behind/pallas_call | solution.py:275
  34.1 0.1 collective-permute-start.1
  34.2 0.2 collective-permute-done.refs_1_
  34.5 0.7 %stack_ahead.2.refs_0_ = f32[1,128,256]{2,1,0:T(8,128)S(1)} custom-call(f32[256,512]{1,0:T(8,128)S(1)} %get-tuple-element.7.white_re, f32[256,512]{1,0:T(8,128)S(1)} %get-tuple-element.8.white_im, bf16[2,512,512]{2,1,0:T(8,128)(2,1)S(1)} %copy-done.3, f32[128,256]{1,0:T(8,128)S(1)} %add_far.1.refs_0_), custom_call_target="tpu_custom_call" | custom-call | flops 4294967296 | bytes 1 | tf_op jit(solution)/shard_map/stack_ahead/pallas_call | solution.py:275
  35.2 5.2 %collective-permute-start.3 = (f32[128,256]{1,0:T(8,128)S(1)}, f32[128,256]{1,0:T(8,128)S(1)}, u32[]{:S(2)}, u32[]{:S(2)}) collective-permute-start(f32[128,256]{1,0:T(8,128)S(1)} %add_far.1.refs_0_), channel_id=1, source_target_pairs={{0,2},{1,7},{2,4},{3,1},{4,6},{5,3},{6,0},{7,5},{8,10},{9,15},{10,... | collective-permute-start | bytes 393224 | tf_op jit(solution)/shard_map/ppermute | solution.py:298
  40.4 0.5 collective-permute-start.4
  40.8 1.2 %stack_behind_here.1.refs_0_ = f32[2,128,256]{2,1,0:T(8,128)S(1)} custom-call(f32[256,512]{1,0:T(8,128)S(1)} %get-tuple-element.7.white_re, f32[256,512]{1,0:T(8,128)S(1)} %get-tuple-element.8.white_im, bf16[2,512,512]{2,1,0:T(8,128)(2,1)S(1)} %copy-done.3, f32[128,256]{1,0:T(8,128)S(1)} %add_other.1.refs_0_), custom_call_target="tpu_custom_call" | custom-call | flops 8589934592 | bytes 1 | tf_op jit(solution)/shard_map/stack_behind_here/pallas_call | solution.py:275
  42.0 0.1 collective-permute-start.2
  42.1 0.7 %stack_ahead.3.refs_0_ = f32[1,128,256]{2,1,0:T(8,128)S(1)} custom-call(f32[256,512]{1,0:T(8,128)S(1)} %get-tuple-element.7.white_re, f32[256,512]{1,0:T(8,128)S(1)} %get-tuple-element.8.white_im, bf16[2,512,512]{2,1,0:T(8,128)(2,1)S(1)} %copy-done.3, f32[2,128,256]{2,1,0:T(8,128)S(1)} %stack_behind_here.1.refs_0_), custom_call_target="tpu_custom_call" | custom-call | flops 4294967296 | bytes 1 | tf_op jit(solution)/shard_map/stack_ahead/pallas_call | solution.py:275
  42.8 1.2 %collective-permute-done.3.refs_2_ = f32[128,256]{1,0:T(8,128)S(1)} collective-permute-done((f32[128,256]{1,0:T(8,128)S(1)}, f32[128,256]{1,0:T(8,128)S(1)}, u32[]{:S(2)}, u32[]{:S(2)}) %collective-permute-start.3) | collective-permute-done | bytes 131104 | tf_op jit(solution)/shard_map/ppermute | solution.py:298
  44.0 4.1 %collective-permute-start.5 = (f32[128,256]{1,0:T(8,128)S(1)}, f32[128,256]{1,0:T(8,128)S(1)}, u32[]{:S(2)}, u32[]{:S(2)}) collective-permute-start(f32[128,256]{1,0:T(8,128)S(1)} %add_own.1.refs_0_), channel_id=1, source_target_pairs={{0,2},{1,7},{2,4},{3,1},{4,6},{5,3},{6,0},{7,5},{8,10},{9,15},{10,... | collective-permute-start | bytes 393224 | tf_op jit(solution)/shard_map/ppermute | solution.py:298
  48.1 0.7 %stack_here.1 = f32[1,128,256]{2,1,0:T(8,128)S(1)} custom-call(f32[256,512]{1,0:T(8,128)S(1)} %get-tuple-element.7.white_re, f32[256,512]{1,0:T(8,128)S(1)} %get-tuple-element.8.white_im, bf16[2,512,512]{2,1,0:T(8,128)(2,1)S(1)} %copy-done.3, f32[128,256]{1,0:T(8,128)S(1)} %add_own.1.refs_0_), custom_call_target="tpu_custom_call" | custom-call | flops 4294967296 | bytes 1 | tf_op jit(solution)/shard_map/stack_here/pallas_call | solution.py:275
  48.8 2.3 %collective-permute-done.5 = f32[128,256]{1,0:T(8,128)S(1)} collective-permute-done((f32[128,256]{1,0:T(8,128)S(1)}, f32[128,256]{1,0:T(8,128)S(1)}, u32[]{:S(2)}, u32[]{:S(2)}) %collective-permute-start.5) | collective-permute-done | bytes 131104 | tf_op jit(solution)/shard_map/ppermute | solution.py:298
  51.1 0.7 %fusion.1 = f32[128,256]{1,0:T(8,128)} fusion(f32[1,128,256]{2,1,0:T(8,128)S(1)} %stack_here.1, f32[2,128,256]{2,1,0:T(8,128)S(1)} %collective-permute-done.2.refs_1_, f32[128,256]{1,0:T(8,128)S(1)} %collective-permute-done.4, f32[128,256]{1,0:T(8,128)S(1)} %collective-permute-done.5), kind=kLoop, calls=%fused_computation.2 | loop fusion | flops 98304 | bytes 655360 | tf_op jit(solution)/shard_map/add | solution.py:321
  (12 shorter events, 0.1 us)
Async XLA Ops:
  0.0 1.0 %copy-start = (f32[4,32,1024]{2,1,0:T(8,128)S(1)}, f32[4,32,1024]{2,1,0:T(8,128)}, u32[]{:S(2)}) copy-start(f32[4,32,1024]{2,1,0:T(8,128)} %records.3) | copy-start | bytes 1572868
  1.0 0.7 %copy-start.1 = (s32[32]{0:T(128)S(1)}, s32[32]{0:T(128)}, u32[]{:S(2)}) copy-start(s32[32]{0:T(128)} %param.5) | copy-start | bytes 388
  2.0 26.5 %copy-start.2 = (bf16[2048,512]{1,0:T(8,128)(2,1)S(1)}, bf16[2048,512]{1,0:T(8,128)(2,1)}, u32[]{:S(2)}) copy-start(bf16[2048,512]{1,0:T(8,128)(2,1)} %constant.4.clone.tables) | copy-start | bytes 6291460
  28.6 1.2 %copy-start.3 = (bf16[2,512,512]{2,1,0:T(8,128)(2,1)S(1)}, bf16[2,512,512]{2,1,0:T(8,128)(2,1)}, u32[]{:S(2)}) copy-start(bf16[2,512,512]{2,1,0:T(8,128)(2,1)} %constant.5.clone.tables) | copy-start | bytes 3145732
  31.2 3.2 %collective-permute-start = (f32[1,128,256]{2,1,0:T(8,128)S(1)}, f32[1,128,256]{2,1,0:T(8,128)S(1)}, u32[]{:S(2)}, u32[]{:S(2)}) collective-permute-start(f32[1,128,256]{2,1,0:T(8,128)S(1)} %stack_far.2.refs_0_), channel_id=1, source_target_pairs={{0,1},{1,0},{2,3},{3,2},{4,5},{5,4},{6,7},{7,6},{8,9},{9,8},{10,11... | collective-permute-start | bytes 393224 | tf_op jit(solution)/shard_map/ppermute | solution.py:305
  34.1 6.2 %collective-permute-start.1 = (f32[1,128,256]{2,1,0:T(8,128)S(1)}, f32[1,128,256]{2,1,0:T(8,128)S(1)}, u32[]{:S(2)}, u32[]{:S(2)}) collective-permute-start(f32[1,128,256]{2,1,0:T(8,128)S(1)} %stack_behind.1), channel_id=1, source_target_pairs={{0,1},{1,0},{2,3},{3,2},{4,5},{5,4},{6,7},{7,6},{8,9},{9,8},{10,11... | collective-permute-start | bytes 393224 | tf_op jit(solution)/shard_map/ppermute | solution.py:305
  35.2 8.8 %collective-permute-start.3 = (f32[128,256]{1,0:T(8,128)S(1)}, f32[128,256]{1,0:T(8,128)S(1)}, u32[]{:S(2)}, u32[]{:S(2)}) collective-permute-start(f32[128,256]{1,0:T(8,128)S(1)} %add_far.1.refs_0_), channel_id=1, source_target_pairs={{0,2},{1,7},{2,4},{3,1},{4,6},{5,3},{6,0},{7,5},{8,10},{9,15},{10,... | collective-permute-start | bytes 393224 | tf_op jit(solution)/shard_map/ppermute | solution.py:298
  40.4 8.4 %collective-permute-start.4 = (f32[128,256]{1,0:T(8,128)S(1)}, f32[128,256]{1,0:T(8,128)S(1)}, u32[]{:S(2)}, u32[]{:S(2)}) collective-permute-start(f32[128,256]{1,0:T(8,128)S(1)} %add_other.1.refs_0_), channel_id=1, source_target_pairs={{0,3},{1,6},{2,5},{3,0},{4,7},{5,2},{6,1},{7,4},{8,11},{9,14},{10,... | collective-permute-start | bytes 393224 | tf_op jit(solution)/shard_map/ppermute | solution.py:302
  42.0 2.0 %collective-permute-start.2 = (f32[2,128,256]{2,1,0:T(8,128)S(1)}, f32[2,128,256]{2,1,0:T(8,128)S(1)}, u32[]{:S(2)}, u32[]{:S(2)}) collective-permute-start(f32[2,128,256]{2,1,0:T(8,128)S(1)} %stack_behind_here.1.refs_0_), channel_id=1, source_target_pairs={{0,1},{1,0},{2,3},{3,2},{4,5},{5,4},{6,7},{7,6},{8,9},{9,8},{10,11... | collective-permute-start | bytes 786440 | tf_op jit(solution)/shard_map/ppermute | solution.py:305
  44.0 7.1 %collective-permute-start.5 = (f32[128,256]{1,0:T(8,128)S(1)}, f32[128,256]{1,0:T(8,128)S(1)}, u32[]{:S(2)}, u32[]{:S(2)}) collective-permute-start(f32[128,256]{1,0:T(8,128)S(1)} %add_own.1.refs_0_), channel_id=1, source_target_pairs={{0,2},{1,7},{2,4},{3,1},{4,6},{5,3},{6,0},{7,5},{8,10},{9,15},{10,... | collective-permute-start | bytes 393224 | tf_op jit(solution)/shard_map/ppermute | solution.py:298
